TPU v7x, 32 devices: a whole 2x2x4 slice. The times are simulated.
32 devices in a mesh: rep: 2 (over y), seq: 4 (over z), head: 4 (over x, core).
Axes of the slice: x: 2, y: 2, z: 4, core: 2. Of those that a mesh axis runs over, the one named last changes fastest.
Arguments:
- queries: bfloat16 [5120, 4096], P(('rep', 'seq'), 'head'), parts along dimension 0, may hold values from -5 to 5
- keys: bfloat16 [5120, 4096], P(('rep', 'seq'), 'head'), parts along dimension 0, may hold values from -5 to 5
- values: bfloat16 [5120, 4096], P(('rep', 'seq'), 'head'), parts along dimension 0, may hold values from -6 to 6
- d_out: bfloat16 [5120, 4096], P(('rep', 'seq'), 'head'), parts along dimension 0, may hold values from -6 to 6
- shift: int32 [2], P('rep'), parts along dimension 0, may hold values from 160 to 480
- head_order: int32 [32], replicated, may hold values from 0 to 31, each once
Outputs:
- d_queries: bfloat16 [5120, 4096], P(('rep', 'seq'), 'head'), parts along dimension 0
- d_keys: bfloat16 [5120, 4096], P(('rep', 'seq'), 'head'), parts along dimension 0
- d_values: bfloat16 [5120, 4096], P(('rep', 'seq'), 'head'), parts along dimension 0
There are 2 independent parts, one for each index of `rep`. A program takes and returns all parts, laid end to end along the dimension named above; an argument that names none is the same for every part. Nothing has to cross between parts.
Inputs may be any that keep to these rules, and one draw needn't show every extreme that they name: head_order is a permutation of the 32 heads.
All inputs are finite; a program needn't handle non-finite values.
Results may differ from a plain program's by a relative error of at most 0.01.
Values may be sent and summed in bfloat16 or wider, within the bound.
No kernel may reach another device: no remote copies, remote signals or barrier semaphores. Data moves between devices by JAX's collectives and lax.ppermute only.
A program may use at most 64 MiB of HBM per device.

v0:
```python
import functools
import math

import jax
import jax.numpy as jnp
from jax import lax
from jax.experimental import pallas as pl
from jax.experimental.pallas import tpu as pltpu
from jax.sharding import PartitionSpec as P


HEADS = 32
HDIM = 128
SCALE = HDIM ** (-0.5)
LOG2_SCALE = SCALE * math.log2(math.e)
NEG = -1e30
GRAIN = 32
BLOCK = 256
F32 = jnp.float32
BF16 = jnp.bfloat16


def up(x, m):
    return (x + m - 1) // m * m


def dot_nt(a, b):
    return lax.dot_general(a, b, (((1,), (1,)), ((), ())), preferred_element_type=F32)


def dot_nn(a, b):
    return lax.dot_general(a, b, (((1,), (0,)), ((), ())), preferred_element_type=F32)


def dot_tn(a, b):
    return lax.dot_general(a, b, (((0,), (0,)), ((), ())), preferred_element_type=F32)


def query_blocks(rows):
    return [(q0, min(BLOCK, rows - q0)) for q0 in range(0, rows, BLOCK)]


def iotas(k0, kn, q0, w):
    key = k0 + lax.broadcasted_iota(jnp.int32, (kn, w), 0)
    query = q0 + lax.broadcasted_iota(jnp.int32, (1, w), 1)
    return key, query


def meta_kernel(heads, grain, caps, shift_ref, order_ref, out_ref, flag_ref):
    base = lax.axis_index("head") * heads
    for h in range(heads):
        flag_ref[h] = 0
    for i in range(HEADS // 2):
        loc = order_ref[i] - base

        @pl.when((loc >= 0) & (loc < heads))
        def _():
            flag_ref[loc] = 1

    count = flag_ref[0]
    for h in range(1, heads):
        count = count + flag_ref[h]
    yes, no = jnp.int32(0), count
    for h in range(heads):
        flag = flag_ref[h]
        out_ref[jnp.where(flag > 0, yes, no)] = h
        yes, no = yes + flag, no + 1 - flag
    off = shift_ref[0]
    slot = (off + grain - 1) // grain * grain
    pick = jnp.where(count > 0, 1, 0)
    for cap in caps[:-1]:
        pick = pick + jnp.where(count * slot > cap, 1, 0)
    out_ref[heads] = count
    out_ref[heads + 1] = off
    out_ref[heads + 2] = slot
    out_ref[heads + 3] = pick


def shifted_at(heads):
    return lambda s, m: m[jnp.minimum(s, m[heads] - 1)]


def pack_kernel(heads, base, sizes, meta, q_ref, d_ref, out_ref, sem):
    count, slot = meta[heads], meta[heads + 2]

    def each(act):
        def step(s, c):
            column = pl.multiple_of(meta[s] * HDIM, HDIM)

            def copy(at, size, i):
                src = pl.multiple_of(at, GRAIN)
                dst = pl.multiple_of(s * slot + at, GRAIN)
                for j, ref in enumerate((q_ref, d_ref)):
                    act(
                        pltpu.make_async_copy(
                            ref.at[pl.ds(src, size), pl.ds(column, HDIM)],
                            out_ref.at[pl.ds(dst, size), pl.ds(j * HDIM, HDIM)],
                            sem.at[s, j, i],
                        )
                    )

            copy(0, base, 0)
            at = jnp.int32(base)
            for i, size in enumerate(sizes):
                bit = ((slot - base) // size) % 2

                @pl.when(bit == 1)
                def _(at=at, size=size, i=i):
                    copy(at, size, i + 1)

                at = at + bit * size
            return c

        lax.fori_loop(0, count, step, 0)

    each(lambda copy: copy.start())
    each(lambda copy: copy.wait())


def stats_kernel(heads, rows, reach, meta, q_ref, k_ref, v_ref, d_ref, send_ref, own_ref):
    s = pl.program_id(0)

    @pl.when(s < meta[heads])
    def _():
        off = meta[heads + 1]
        for q0, w in query_blocks(rows):
            kn = q0 + w
            key, query = iotas(0, kn, q0, w)
            low = jnp.where(query >= off, off, 0)
            sc = dot_nt(k_ref[:kn, :], q_ref[q0:kn, :]) * LOG2_SCALE
            sc = jnp.where((key <= query) & (key >= low), sc, NEG)
            top = jnp.max(sc, axis=0, keepdims=True)
            e = jnp.exp2(sc - top)
            total = jnp.sum(e, axis=0, keepdims=True)
            dp = dot_nt(v_ref[:kn, :], d_ref[q0:kn, :])
            rd = jnp.sum(e * dp, axis=0, keepdims=True) / total
            lse = top + jnp.log2(total)
            own_ref[s, 0:1, q0:kn] = lse
            own_ref[s, 1:2, q0:kn] = rd
            if q0 < reach:
                send_ref[s, 0:1, q0:kn] = lse
                send_ref[s, 1:2, q0:kn] = rd


def plain_kernel(heads, rows, meta, q_ref, k_ref, v_ref, d_ref, dq_ref, dk_ref, dv_ref, ak_ref, av_ref):
    s = pl.program_id(0)

    @pl.when(s >= meta[heads])
    def _():
        for q0, w in query_blocks(rows):
            kn = q0 + w
            qb, db = q_ref[q0:kn, :], d_ref[q0:kn, :]
            parts = ([(0, q0, False)] if q0 else []) + [(q0, w, True)]
            scores = []
            for k0, n, diagonal in parts:
                sc = dot_nt(k_ref[k0 : k0 + n, :], qb) * LOG2_SCALE
                if diagonal:
                    key, query = iotas(k0, n, q0, w)
                    sc = jnp.where(key <= query, sc, NEG)
                scores.append(sc)
            tops = [jnp.max(sc, axis=0, keepdims=True) for sc in scores]
            top = functools.reduce(jnp.maximum, tops)
            es = [jnp.exp2(sc - top) for sc in scores]
            total = sum(jnp.sum(e, axis=0, keepdims=True) for e in es)
            dps = [dot_nt(v_ref[k0 : k0 + n, :], db) for k0, n, _ in parts]
            inv = 1.0 / total
            rd = sum(jnp.sum(e * dp, axis=0, keepdims=True) for e, dp in zip(es, dps)) * inv
            dq = None
            for (k0, n, diagonal), e, dp in zip(parts, es, dps):
                p = e * inv
                ds = (p * (dp - rd)).astype(BF16)
                gv = dot_nn(p.astype(BF16), db)
                gk = dot_nn(ds, qb)
                gq = dot_tn(ds, k_ref[k0 : k0 + n, :])
                dq = gq if dq is None else dq + gq
                if diagonal:
                    av_ref[k0 : k0 + n, :] = gv
                    ak_ref[k0 : k0 + n, :] = gk
                else:
                    av_ref[k0 : k0 + n, :] += gv
                    ak_ref[k0 : k0 + n, :] += gk
            dq_ref[q0:kn, :] = (dq * SCALE).astype(BF16)
        dk_ref[...] = (ak_ref[...] * SCALE).astype(BF16)
        dv_ref[...] = av_ref[...].astype(BF16)


def cross_kernel(
    heads, rows, first, meta, k_ref, v_ref, got_ref, st_ref, _after,
    back_ref, tot_ref, gk_ref, gv_ref, buf_ref, acc_ref,
):
    s = pl.program_id(0)
    count, off, slot = meta[heads], meta[heads + 1], meta[heads + 2]
    filled = count * slot

    @pl.when(s == 0)
    def _():
        def step(i, c):
            at = pl.multiple_of(i * GRAIN, GRAIN)
            buf_ref[pl.ds(at, GRAIN), :] = got_ref[pl.ds(at, GRAIN), :]
            return c

        lax.fori_loop(0, filled // GRAIN, step, 0)
        tail = pl.multiple_of(filled, GRAIN)
        buf_ref[pl.ds(tail, BLOCK), :] = jnp.zeros((BLOCK, 2 * HDIM), BF16)

    def block(j, k0):
        q0 = pl.multiple_of(j * BLOCK, BLOCK)
        start = pl.multiple_of(s * slot + q0, GRAIN)
        qb = buf_ref[pl.ds(start, BLOCK), :HDIM]
        db = buf_ref[pl.ds(start, BLOCK), HDIM:]
        kb, vb = k_ref[k0:, :], v_ref[k0:, :]
        key = k0 + lax.broadcasted_iota(jnp.int32, (rows - k0, BLOCK), 0)
        query = q0 + lax.broadcasted_iota(jnp.int32, (1, BLOCK), 1)
        inside = query < off
        sc = dot_nt(kb, qb) * LOG2_SCALE
        sc = jnp.where(key >= off, sc, NEG)
        top = jnp.max(sc, axis=0, keepdims=True)
        e = jnp.exp2(sc - top)
        total = jnp.sum(e, axis=0, keepdims=True)
        dp = dot_nt(vb, db)
        rd = jnp.sum(e * dp, axis=0, keepdims=True) / total
        lse = top + jnp.log2(total)
        lse1 = jnp.where(inside, st_ref[s, 0:1, pl.ds(q0, BLOCK)], 0.0)
        rd1 = jnp.where(inside, st_ref[s, 1:2, pl.ds(q0, BLOCK)], 0.0)
        high = jnp.maximum(lse, lse1)
        both = high + jnp.log2(jnp.exp2(lse - high) + jnp.exp2(lse1 - high))
        rd = jnp.exp2(lse - both) * rd + jnp.exp2(lse1 - both) * rd1
        tot_ref[s, 0:1, pl.ds(q0, BLOCK)] = both
        tot_ref[s, 1:2, pl.ds(q0, BLOCK)] = rd
        p = e * jnp.where(inside, jnp.exp2(top - both), 0.0)
        ds = (p * (dp - rd)).astype(BF16)
        gv_ref[s, k0 - first :, :] += dot_nn(p.astype(BF16), db)
        gk_ref[s, k0 - first :, :] += dot_nn(ds, qb)
        acc_ref[pl.ds(start, BLOCK), :] = (dot_tn(ds, kb) * SCALE).astype(BF16)

    @pl.when(s < count)
    def _():
        gv_ref[s] = jnp.zeros(gv_ref.shape[1:], F32)
        gk_ref[s] = jnp.zeros(gk_ref.shape[1:], F32)
        starts = (first, up(2 * first, GRAIN))
        blocks = (off + BLOCK - 1) // BLOCK
        for k0, mine in ((starts[0], off < starts[1]), (starts[1], off >= starts[1])):

            @pl.when(mine)
            def _(k0=k0):
                def step(j, c):
                    block(j, k0)
                    return c

                lax.fori_loop(0, blocks, step, 0)

    @pl.when(s == pl.num_programs(0) - 1)
    def _():
        def step(i, c):
            at = pl.multiple_of(i * GRAIN, GRAIN)
            back_ref[pl.ds(at, GRAIN), :] = acc_ref[pl.ds(at, GRAIN), :]
            return c

        lax.fori_loop(0, filled // GRAIN, step, 0)


def local_kernel(
    heads, rows, first, reach, meta, q_ref, k_ref, v_ref, d_ref, own_ref, tot_ref, gk_ref, gv_ref,
    _dq, _dk, _dv, dq_ref, dk_ref, dv_ref, part_ref, ak_ref, av_ref,
):
    s = pl.program_id(0)

    @pl.when(s < meta[heads])
    def _():
        off = meta[heads + 1]
        for q0, w in query_blocks(rows):
            kn = q0 + w
            key, query = iotas(0, kn, q0, w)
            low = jnp.where(query >= off, off, 0)
            lse = own_ref[s, 0:1, q0:kn]
            rd = own_ref[s, 1:2, q0:kn]
            if q0 < reach:
                lse = jnp.where(query < off, tot_ref[s, 0:1, q0:kn], lse)
                rd = jnp.where(query < off, tot_ref[s, 1:2, q0:kn], rd)
            qb, db = q_ref[q0:kn, :], d_ref[q0:kn, :]
            sc = dot_nt(k_ref[:kn, :], qb) * LOG2_SCALE
            p = jnp.where((key <= query) & (key >= low), jnp.exp2(sc - lse), 0.0)
            dp = dot_nt(v_ref[:kn, :], db)
            ds = (p * (dp - rd)).astype(BF16)
            gv = dot_nn(p.astype(BF16), db)
            gk = dot_nn(ds, qb)
            dq = dot_tn(ds, k_ref[:kn, :]) * SCALE
            dq_ref[q0:kn, :] = dq.astype(BF16)
            if q0 < reach:
                part_ref[s, q0:kn, :] = dq
            if q0:
                av_ref[:q0, :] += gv[:q0]
                ak_ref[:q0, :] += gk[:q0]
            av_ref[q0:kn, :] = gv[q0:]
            ak_ref[q0:kn, :] = gk[q0:]
        dk_ref[:first, :] = (ak_ref[:first, :] * SCALE).astype(BF16)
        dv_ref[:first, :] = av_ref[:first, :].astype(BF16)
        dk_ref[first:, :] = ((ak_ref[first:, :] + gk_ref[s]) * SCALE).astype(BF16)
        dv_ref[first:, :] = (av_ref[first:, :] + gv_ref[s]).astype(BF16)


def add_kernel(heads, tallest, meta, part_ref, got_ref, _dq, dq_ref, stage_ref, sem):
    slot = meta[heads + 2]

    def copy(s):
        column = pl.multiple_of(meta[s] * HDIM, HDIM)
        return pltpu.make_async_copy(
            stage_ref.at[s], dq_ref.at[pl.ds(0, tallest), pl.ds(column, HDIM)], sem.at[s]
        )

    def send(s, c):
        def both(i, c):
            at = pl.multiple_of(i * GRAIN, GRAIN)
            src = pl.multiple_of(s * slot + i * GRAIN, GRAIN)
            there = got_ref[pl.ds(src, GRAIN), :].astype(F32)
            stage_ref[s, pl.ds(at, GRAIN), :] = (part_ref[s, pl.ds(at, GRAIN), :] + there).astype(BF16)
            return c

        def here(i, c):
            at = pl.multiple_of(i * GRAIN, GRAIN)
            stage_ref[s, pl.ds(at, GRAIN), :] = part_ref[s, pl.ds(at, GRAIN), :].astype(BF16)
            return c

        lax.fori_loop(0, slot // GRAIN, both, 0)
        lax.fori_loop(slot // GRAIN, tallest // GRAIN, here, 0)
        copy(s).start()
        return c

    def wait(s, c):
        copy(s).wait()
        return c

    lax.fori_loop(0, meta[heads], send, 0)
    lax.fori_loop(0, meta[heads], wait, 0)


def cost(flops, moved):
    return pl.CostEstimate(flops=int(flops), bytes_accessed=int(moved), transcendentals=0)


def shards(queries, keys, values, d_out, shift, head_order):
    rows, width = queries.shape
    heads = width // HDIM
    first, last = rows // 4, rows - rows // 4
    base = first // GRAIN * GRAIN
    tallest = up(last, GRAIN)
    reach = up(last, BLOCK)
    most = heads * tallest
    fractions = (0.25, 0.38, 0.5, 0.67, 1.0)
    caps = [up(int(most * f), GRAIN) for f in fractions]
    seq = lax.axis_size("seq")
    back = [(i, (i - 1) % seq) for i in range(seq)]
    ahead = [(i, (i + 1) % seq) for i in range(seq)]

    meta = pl.pallas_call(
        functools.partial(meta_kernel, heads, GRAIN, caps),
        out_shape=jax.ShapeDtypeStruct((heads + 4,), jnp.int32),
        in_specs=[pl.BlockSpec(memory_space=pltpu.SMEM)] * 2,
        out_specs=pl.BlockSpec(memory_space=pltpu.SMEM),
        scratch_shapes=[pltpu.SMEM((heads,), jnp.int32)],
        name="meta",
    )(shift, head_order)

    at = shifted_at(heads)
    whole = jax.ShapeDtypeStruct((rows, width), BF16)
    head_spec = pl.BlockSpec((rows, HDIM), lambda s, m: (0, at(s, m)))
    plain_at = lambda s, m: m[jnp.minimum(jnp.maximum(s, m[heads]), heads - 1)]
    plain_spec = pl.BlockSpec((rows, HDIM), lambda s, m: (0, plain_at(s, m)))
    any_spec = pl.BlockSpec(memory_space=pl.ANY)
    vmem = pl.BlockSpec(memory_space=pltpu.VMEM)
    smem = pl.BlockSpec(memory_space=pltpu.SMEM)
    tile = rows * HDIM * 2
    work = 2 * rows * rows * HDIM

    def call(kernel, in_specs, out_specs, out_shape, estimate, scratch=(), aliases={}):
        return pl.pallas_call(
            kernel,
            out_shape=out_shape,
            grid_spec=pltpu.PrefetchScalarGridSpec(
                num_scalar_prefetch=1,
                grid=(heads,),
                in_specs=in_specs,
                out_specs=out_specs,
                scratch_shapes=list(scratch),
            ),
            input_output_aliases=aliases,
            cost_estimate=estimate,
        )

    def plain(meta, queries, keys, values, d_out):
        return call(
            functools.partial(plain_kernel, heads, rows),
            [plain_spec] * 4,
            [plain_spec] * 3,
            [whole] * 3,
            cost(heads / 2 * 4 * work, heads / 2 * 7 * tile),
            [pltpu.VMEM((rows, HDIM), F32)] * 2,
        )(meta, queries, keys, values, d_out)

    def branch(cap):
        def steps(meta, queries, keys, values, d_out):
            sizes, left = [], tallest - base
            while sum(sizes) < left:
                sizes.append(GRAIN * 2 ** len(sizes))
            sent = pl.pallas_call(
                functools.partial(pack_kernel, heads, base, sizes),
                out_shape=jax.ShapeDtypeStruct((cap, 2 * HDIM), BF16),
                in_specs=[smem, any_spec, any_spec],
                out_specs=vmem,
                scratch_shapes=[pltpu.SemaphoreType.DMA((heads, 2, 1 + len(sizes)))],
                cost_estimate=cost(0, 2 * cap * HDIM * 4),
                name="pack",
            )(meta, queries, d_out)
            got = lax.ppermute(sent, "seq", back)
            st_send, st_own = call(
                functools.partial(stats_kernel, heads, rows, reach),
                [head_spec] * 4,
                [vmem, vmem],
                [
                    jax.ShapeDtypeStruct((heads, 2, reach), F32),
                    jax.ShapeDtypeStruct((heads, 2, rows), F32),
                ],
                cost(heads / 2 * 2 * work, heads / 2 * 4 * tile),
            )(meta, queries, keys, values, d_out)
            st_got = lax.ppermute(st_send, "seq", back)
            dq, dk, dv = plain(meta, queries, keys, values, d_out)
            side = jax.ShapeDtypeStruct((heads, rows - first, HDIM), F32)
            back_q, tot, gk, gv = call(
                functools.partial(cross_kernel, heads, rows, first),
                [head_spec] * 2 + [vmem, vmem, any_spec],
                [vmem] * 4,
                [
                    jax.ShapeDtypeStruct((cap, HDIM), BF16),
                    jax.ShapeDtypeStruct((heads, 2, reach), F32),
                    side,
                    side,
                ],
                cost(heads / 2 * 5 * work, heads / 2 * 6 * tile),
                [pltpu.VMEM((cap + BLOCK, 2 * HDIM), BF16), pltpu.VMEM((cap + BLOCK, HDIM), BF16)],
            )(meta, keys, values, got, st_got, dq)
            tot_got = lax.ppermute(tot, "seq", ahead)
            dq_got = lax.ppermute(back_q, "seq", ahead)
            dq, dk, dv, part = call(
                functools.partial(local_kernel, heads, rows, first, reach),
                [head_spec] * 4
                + [vmem] * 4
                + [any_spec] * 3,
                [head_spec] * 3 + [vmem],
                [whole] * 3 + [jax.ShapeDtypeStruct((heads, reach, HDIM), F32)],
                cost(heads / 2 * 4 * work, heads / 2 * 9 * tile),
                [pltpu.VMEM((rows, HDIM), F32)] * 2,
                {9: 0, 10: 1, 11: 2},
            )(meta, queries, keys, values, d_out, st_own, tot_got, gk, gv, dq, dk, dv)
            dq = pl.pallas_call(
                functools.partial(add_kernel, heads, tallest),
                out_shape=whole,
                in_specs=[smem, vmem, vmem, any_spec],
                out_specs=any_spec,
                scratch_shapes=[
                    pltpu.VMEM((heads, tallest, HDIM), BF16),
                    pltpu.SemaphoreType.DMA((heads,)),
                ],
                input_output_aliases={3: 0},
                cost_estimate=cost(0, heads / 2 * 3 * tile),
                name="add",
            )(meta, part, dq_got, dq)
            return dq, dk, dv

        return steps

    return tuple(
        lax.switch(
            meta[heads + 3],
            [plain] + [branch(cap) for cap in caps],
            meta,
            queries,
            keys,
            values,
            d_out,
        )
    )


def solution(mesh):
    spec = P(("rep", "seq"), "head")
    return jax.shard_map(
        shards,
        mesh=mesh,
        in_specs=(spec, spec, spec, spec, P("rep"), P()),
        out_specs=(spec, spec, spec),
        check_vma=False,
    )
```

profile of v0, /device:TPU:0, one launch (start us, length us, event | category | flops | bytes accessed | tf_op | source)
XLA Modules:
  0.0 71.2 jit_solution(16252149022780279926)
XLA Ops:
  1.3 1.3 %meta.1 = s32[12]{0:T(128)S(1)} custom-call(s32[1]{0:T(128)S(6)} %copy.109.shift_ref, s32[32]{0:T(128)} %order_ref.1), custom_call_target="tpu_custom_call" | custom-call | tf_op jit(solution)/shard_map/meta/pallas_call | solution.py:355
  2.6 0.6 slice.3
  3.8 67.1 %conditional.1 = ((bf16[640,1024]{1,0:T(8,128)(2,1)}, bf16[640,1024]{1,0:T(8,128)(2,1)}, bf16[640,1024]{1,0:T(8,128)(2,1)})) conditional(s32[]{:T(128)} %bitcast, (s32[12]{0:T(128)S(1)}, bf16[640,1024]{1,0:T(8,128)(2,1)}, bf16[640,1024]{1,0:T(8,128)(2,1)}, bf16[640,1024]{1,0:T(8,128)(2,1)}, ...), branch_computations={%region_0.0_spmd, %region_1.0_spmd, %region_2.0_spmd, %region_3.0_... | conditional | flops 6291456000 | bytes 45744432 | solution.py:472
  3.9 0.0 copy-start.1
  3.9 0.0 copy-start.6
  3.9 3.4 %pack.6 = bf16[1472,256]{1,0:T(8,128)(2,1)} custom-call(s32[12]{0:T(128)S(1)} %get-tuple-element.83.meta, bf16[640,1024]{1,0:T(8,128)(2,1)} %get-tuple-element.190.q_ref, bf16[640,1024]{1,0:T(8,128)(2,1)} %get-tuple-element.208.d_ref), custom_call_target="tpu_custom_call" | custom-call | bytes 1507328 | tf_op jit(solution)/shard_map/cond/branch_2_fun/pack/pallas_call | solution.py:405
  7.4 5.1 %collective-permute-start.4 = (bf16[1472,256]{1,0:T(8,128)(2,1)}, bf16[1472,256]{1,0:T(8,128)(2,1)}, u32[]{:S(2)}, u32[]{:S(2)}) collective-permute-start(bf16[1472,256]{1,0:T(8,128)(2,1)} %pack.6), channel_id=1, source_target_pairs={{0,12},{4,0},{8,4},{12,8},{1,13},{5,1},{9,5},{13,9},{2,14},{6,2},{... | collective-permute-start | bytes 2261000 | tf_op jit(solution)/shard_map/cond/branch_2_fun/ppermute | solution.py:414
  12.5 0.0 copy-done.1
  12.5 0.0 copy-done.6
  12.5 6.6 %branch_2_fun.4 = (f32[8,2,512]{2,1,0:T(2,128)}, f32[8,2,640]{2,1,0:T(2,128)}) custom-call(s32[12]{0:T(128)S(1)} %get-tuple-element.83.meta, bf16[640,1024]{1,0:T(8,128)(2,1)S(1)} %copy-done.1, bf16[640,1024]{1,0:T(8,128)(2,1)} %get-tuple-element.196.k_ref, bf16[640,1024]{1,0:T(8,128)(2,1)} %get-tuple-element.202.v_ref, bf16[640,1024]{1,0:T(8,128)(2,1)S(1)} %copy-done.6), custom_call_target="tpu_custom_call" | custom-call | flops 838860800 | bytes 2621440 | tf_op jit(solution)/shard_map/cond/branch_2_fun/pallas_call | solution.py:415
  19.1 0.5 collective-permute-start.5
  19.5 7.7 %branch_2_fun.5 = (bf16[640,1024]{1,0:T(8,128)(2,1)}, bf16[640,1024]{1,0:T(8,128)(2,1)}, bf16[640,1024]{1,0:T(8,128)(2,1)}) custom-call(s32[12]{0:T(128)S(1)} %get-tuple-element.83.meta, bf16[640,1024]{1,0:T(8,128)(2,1)S(1)} %copy-done.1, bf16[640,1024]{1,0:T(8,128)(2,1)} %get-tuple-element.196.k_ref, bf16[640,1024]{1,0:T(8,128)(2,1)} %get-tuple-element.202.v_ref, ...), custom_call_target="tpu_custom_call" | custom-call | flops 1677721600 | bytes 4587520 | tf_op jit(solution)/shard_map/cond/branch_2_fun/pallas_call | solution.py:391
  27.2 2.4 %collective-permute-done.5.st_ref = f32[8,2,512]{2,1,0:T(2,128)S(1)} collective-permute-done((f32[8,2,512]{2,1,0:T(2,128)}, f32[8,2,512]{2,1,0:T(2,128)S(1)}, u32[]{:S(2)}, u32[]{:S(2)}) %collective-permute-start.5) | collective-permute-done | bytes 32800 | tf_op jit(solution)/shard_map/cond/branch_2_fun/ppermute | solution.py:425
  29.5 0.0 copy-start.21
  29.5 0.0 collective-permute-done.4.got_ref
  29.5 0.6 copy-done.21
  30.1 13.2 %branch_2_fun.6 = (bf16[1472,128]{1,0:T(8,128)(2,1)}, f32[8,2,512]{2,1,0:T(2,128)}, f32[8,480,128]{2,1,0:T(8,128)}, f32[8,480,128]{2,1,0:T(8,128)}) custom-call(s32[12]{0:T(128)S(1)} %get-tuple-element.83.meta, bf16[640,1024]{1,0:T(8,128)(2,1)} %get-tuple-element.196.k_ref, bf16[640,1024]{1,0:T(8,128)(2,1)} %get-tuple-element.202.v_ref, ...), custom_call_target="tpu_custom_call" | custom-call | flops 2097152000 | bytes 3932160 | tf_op jit(solution)/shard_map/cond/branch_2_fun/pallas_call | solution.py:428
  43.4 0.4 collective-permute-start.7
  43.7 1.6 %collective-permute-start.6 = (f32[8,2,512]{2,1,0:T(2,128)}, f32[8,2,512]{2,1,0:T(2,128)S(1)}, u32[]{:S(2)}, u32[]{:S(2)}) collective-permute-start(f32[8,2,512]{2,1,0:T(2,128)} %get-tuple-element.91), channel_id=1, source_target_pairs={{0,4},{4,8},{8,12},{12,0},{1,5},{5,9},{9,13},{13,1},{2,6},{6,10},{... | collective-permute-start | bytes 98312 | tf_op jit(solution)/shard_map/cond/branch_2_fun/ppermute | solution.py:441
  45.3 9.3 %collective-permute-done.6.tot_ref = f32[8,2,512]{2,1,0:T(2,128)S(1)} collective-permute-done((f32[8,2,512]{2,1,0:T(2,128)}, f32[8,2,512]{2,1,0:T(2,128)S(1)}, u32[]{:S(2)}, u32[]{:S(2)}) %collective-permute-start.6) | collective-permute-done | bytes 32800 | tf_op jit(solution)/shard_map/cond/branch_2_fun/ppermute | solution.py:441
  54.6 0.0 copy-start.15
  54.6 0.6 copy-done.15
  55.2 11.5 %branch_2_fun.7 = (bf16[640,1024]{1,0:T(8,128)(2,1)}, bf16[640,1024]{1,0:T(8,128)(2,1)}, bf16[640,1024]{1,0:T(8,128)(2,1)}, f32[8,512,128]{2,1,0:T(8,128)}) custom-call(s32[12]{0:T(128)S(1)} %get-tuple-element.83.meta, bf16[640,1024]{1,0:T(8,128)(2,1)S(1)} %copy-done.1, ...), custom_call_target="tpu_custom_call", output_to_operand_aliasing={{0}: (9, {}), {1}: (10, {}), {2}: (11, {})} | custom-call | flops 1677721600 | bytes 5898240 | tf_op jit(solution)/shard_map/cond/branch_2_fun/pallas_call | solution.py:443
  66.7 0.0 collective-permute-done.7.got_ref
  66.8 0.0 copy-start.12
  66.8 0.7 %copy-done.12 = bf16[1472,128]{1,0:T(8,128)(2,1)} copy-done((bf16[1472,128]{1,0:T(8,128)(2,1)}, bf16[1472,128]{1,0:T(8,128)(2,1)S(1)}, u32[]{:S(2)}) %copy-start.12) | copy-done | bytes 376856 | tf_op jit(solution)/shard_map/cond
  67.5 3.0 %add.6 = bf16[640,1024]{1,0:T(8,128)(2,1)} custom-call(s32[12]{0:T(128)S(1)} %get-tuple-element.83.meta, f32[8,512,128]{2,1,0:T(8,128)} %get-tuple-element.96.part_ref, bf16[1472,128]{1,0:T(8,128)(2,1)} %copy-done.12, bf16[640,1024]{1,0:T(8,128)(2,1)} %get-tuple-element.98._dq), custom_call_target="tpu_custom_call", output_to_operand_aliasing={{}: (3, {})} | custom-call | bytes 1966080 | tf_op jit(solution)/shard_map/cond/branch_2_fun/add/pallas_call | solution.py:454
Async XLA Ops:
  3.9 8.6 %copy-start.1 = (bf16[640,1024]{1,0:T(8,128)(2,1)S(1)}, bf16[640,1024]{1,0:T(8,128)(2,1)}, u32[]{:S(2)}) copy-start(bf16[640,1024]{1,0:T(8,128)(2,1)} %get-tuple-element.190.q_ref) | copy-start | bytes 3932164 | tf_op jit(solution)/shard_map/cond
  3.9 8.6 %copy-start.6 = (bf16[640,1024]{1,0:T(8,128)(2,1)S(1)}, bf16[640,1024]{1,0:T(8,128)(2,1)}, u32[]{:S(2)}) copy-start(bf16[640,1024]{1,0:T(8,128)(2,1)} %get-tuple-element.208.d_ref) | copy-start | bytes 3932164 | tf_op jit(solution)/shard_map/cond
  7.4 22.2 %collective-permute-start.4 = (bf16[1472,256]{1,0:T(8,128)(2,1)}, bf16[1472,256]{1,0:T(8,128)(2,1)}, u32[]{:S(2)}, u32[]{:S(2)}) collective-permute-start(bf16[1472,256]{1,0:T(8,128)(2,1)} %pack.6), channel_id=1, source_target_pairs={{0,12},{4,0},{8,4},{12,8},{1,13},{5,1},{9,5},{13,9},{2,14},{6,2},{... | collective-permute-start | bytes 2261000 | tf_op jit(solution)/shard_map/cond/branch_2_fun/ppermute | solution.py:414
  19.1 10.5 %collective-permute-start.5 = (f32[8,2,512]{2,1,0:T(2,128)}, f32[8,2,512]{2,1,0:T(2,128)S(1)}, u32[]{:S(2)}, u32[]{:S(2)}) collective-permute-start(f32[8,2,512]{2,1,0:T(2,128)} %get-tuple-element.89), channel_id=1, source_target_pairs={{0,12},{4,0},{8,4},{12,8},{1,13},{5,1},{9,5},{13,9},{2,14},{6,2},{... | collective-permute-start | bytes 98312 | tf_op jit(solution)/shard_map/cond/branch_2_fun/ppermute | solution.py:425
  29.5 0.6 copy-start.21
  43.4 23.4 %collective-permute-start.7 = (bf16[1472,128]{1,0:T(8,128)(2,1)}, bf16[1472,128]{1,0:T(8,128)(2,1)S(1)}, u32[]{:S(2)}, u32[]{:S(2)}) collective-permute-start(bf16[1472,128]{1,0:T(8,128)(2,1)} %get-tuple-element.97), channel_id=1, source_target_pairs={{0,4},{4,8},{8,12},{12,0},{1,5},{5,9},{9,13},{13,1},{2,6},{6,10},{... | collective-permute-start | bytes 1130504 | tf_op jit(solution)/shard_map/cond/branch_2_fun/ppermute | solution.py:442
  43.7 10.9 %collective-permute-start.6 = (f32[8,2,512]{2,1,0:T(2,128)}, f32[8,2,512]{2,1,0:T(2,128)S(1)}, u32[]{:S(2)}, u32[]{:S(2)}) collective-permute-start(f32[8,2,512]{2,1,0:T(2,128)} %get-tuple-element.91), channel_id=1, source_target_pairs={{0,4},{4,8},{8,12},{12,0},{1,5},{5,9},{9,13},{13,1},{2,6},{6,10},{... | collective-permute-start | bytes 98312 | tf_op jit(solution)/shard_map/cond/branch_2_fun/ppermute | solution.py:441
  54.6 0.6 copy-start.15
  66.8 0.7 %copy-start.12 = (bf16[1472,128]{1,0:T(8,128)(2,1)}, bf16[1472,128]{1,0:T(8,128)(2,1)S(1)}, u32[]{:S(2)}) copy-start(bf16[1472,128]{1,0:T(8,128)(2,1)S(1)} %collective-permute-done.7.got_ref) | copy-start | bytes 1130500 | tf_op jit(solution)/shard_map/cond
where the time goes:
time: 71.5 us; the launch traced here: 71.2 us
  Pallas kernels  46.7 us (65%)
  waiting for transfers between devices  11.7 us (16%)
  starting transfers between devices  7.51 us (11%)
  local copies, waits for them, and re-layouts  2.53 us (4%)
  between operations  2.14 us (3%)
    pallas_call x1, Pallas kernels, steps(): call(functools.partial(cross_kernel, heads, rows, first), [head_spec] * 2...  13.2 us
    pallas_call x1, Pallas kernels, steps(): call(functools.partial(local_kernel, heads, rows, first, reach), [head_sp...  11.5 us
    ppermute x1, waiting for transfers between devices, steps(): tot_got = lax.ppermute(tot, 'seq', ahead)  9.34 us
    pallas_call x1, Pallas kernels, plain(): call(functools.partial(plain_kernel, heads, rows), [plain_spec] * 4, [pla...  7.66 us
    pallas_call x1, Pallas kernels, steps(): call(functools.partial(stats_kernel, heads, rows, reach), [head_spec] * 4...  6.57 us
    ppermute x1, starting transfers between devices, steps(): got = lax.ppermute(sent, 'seq', back)  5.13 us
    pallas_call x1, Pallas kernels, steps(): pl.pallas_call(functools.partial(pack_kernel, heads, base, sizes), out_sh...  3.45 us
    pallas_call x1, Pallas kernels, steps(): pl.pallas_call(functools.partial(add_kernel, heads, tallest), out_shape=w...  3.02 us
  transfers between devices with their start and end apart: 4, of which 2 were waited for; matrix products, arithmetic and copies ran while one was open for 0% of the time, Pallas kernels for 36%

commit v1 on v0

--- a/solution.py
+++ b/solution.py
@@ -338,6 +338,10 @@
     return pl.CostEstimate(flops=int(flops), bytes_accessed=int(moved), transcendentals=0)
 
 
+def params(mebibytes):
+    return pltpu.CompilerParams(vmem_limit_bytes=mebibytes * 2**20)
+
+
 def shards(queries, keys, values, d_out, shift, head_order):
     rows, width = queries.shape
     heads = width // HDIM
@@ -372,7 +376,7 @@
     tile = rows * HDIM * 2
     work = 2 * rows * rows * HDIM
 
-    def call(kernel, in_specs, out_specs, out_shape, estimate, scratch=(), aliases={}):
+    def call(kernel, in_specs, out_specs, out_shape, estimate, limit, scratch=(), aliases={}):
         return pl.pallas_call(
             kernel,
             out_shape=out_shape,
@@ -385,6 +389,7 @@
             ),
             input_output_aliases=aliases,
             cost_estimate=estimate,
+            compiler_params=params(limit),
         )
 
     def plain(meta, queries, keys, values, d_out):
@@ -394,6 +399,7 @@
             [plain_spec] * 3,
             [whole] * 3,
             cost(heads / 2 * 4 * work, heads / 2 * 7 * tile),
+            16,
             [pltpu.VMEM((rows, HDIM), F32)] * 2,
         )(meta, queries, keys, values, d_out)
 
@@ -409,6 +415,7 @@
                 out_specs=vmem,
                 scratch_shapes=[pltpu.SemaphoreType.DMA((heads, 2, 1 + len(sizes)))],
                 cost_estimate=cost(0, 2 * cap * HDIM * 4),
+                compiler_params=params(8),
                 name="pack",
             )(meta, queries, d_out)
             got = lax.ppermute(sent, "seq", back)
@@ -421,6 +428,7 @@
                     jax.ShapeDtypeStruct((heads, 2, rows), F32),
                 ],
                 cost(heads / 2 * 2 * work, heads / 2 * 4 * tile),
+                16,
             )(meta, queries, keys, values, d_out)
             st_got = lax.ppermute(st_send, "seq", back)
             dq, dk, dv = plain(meta, queries, keys, values, d_out)
@@ -436,6 +444,7 @@
                     side,
                 ],
                 cost(heads / 2 * 5 * work, heads / 2 * 6 * tile),
+                24,
                 [pltpu.VMEM((cap + BLOCK, 2 * HDIM), BF16), pltpu.VMEM((cap + BLOCK, HDIM), BF16)],
             )(meta, keys, values, got, st_got, dq)
             tot_got = lax.ppermute(tot, "seq", ahead)
@@ -448,6 +457,7 @@
                 [head_spec] * 3 + [vmem],
                 [whole] * 3 + [jax.ShapeDtypeStruct((heads, reach, HDIM), F32)],
                 cost(heads / 2 * 4 * work, heads / 2 * 9 * tile),
+                24,
                 [pltpu.VMEM((rows, HDIM), F32)] * 2,
                 {9: 0, 10: 1, 11: 2},
             )(meta, queries, keys, values, d_out, st_own, tot_got, gk, gv, dq, dk, dv)
@@ -462,6 +472,7 @@
                 ],
                 input_output_aliases={3: 0},
                 cost_estimate=cost(0, heads / 2 * 3 * tile),
+                compiler_params=params(16),
                 name="add",
             )(meta, part, dq_got, dq)
             return dq, dk, dv

time: 71.5 us -> 61.4 us (0.86)
  Pallas kernels: 46.7 us -> 38.6 us
  local copies, waits for them, and re-layouts: 2.53 us -> 0.6 us
    pallas_call x1, Pallas kernels: 13.2 us -> 10.3 us  [steps(): call(functools.partial(cross_kernel, heads, rows, first), [head_spec] * 2...]
    pallas_call x1, Pallas kernels: 11.5 us -> 8.8 us  [steps(): call(functools.partial(local_kernel, heads, rows, first, reach), [head_sp...]
    cond x10 -> x8, local copies, waits for them, and re-layouts: 1.95 us -> 0.02 us
    pallas_call x1, Pallas kernels: 3.02 us -> 1.93 us  [steps(): pl.pallas_call(functools.partial(add_kernel, heads, tallest), out_shape=w...]
    pallas_call x1, Pallas kernels: 3.45 us -> 2.58 us  [steps(): pl.pallas_call(functools.partial(pack_kernel, heads, base, sizes), out_sh...]
  transfers between devices with their start and end apart: 4 -> 4, of which waited for: 2 -> 2; matrix products, arithmetic and copies ran while one was open for 0% -> 0% of each run, Pallas kernels for 36% -> 37%
where the time goes in v1:
time: 61.4 us; the launch traced here: 61.1 us
  Pallas kernels  38.6 us (63%)
  waiting for transfers between devices  11.3 us (18%)
  starting transfers between devices  7.87 us (13%)
  between operations  2.16 us (4%)
  loops' own time  0.62 us (1%)
    pallas_call x1, Pallas kernels, steps(): call(functools.partial(cross_kernel, heads, rows, first), [head_spec] * 2...  10.3 us
    ppermute x1, waiting for transfers between devices, steps(): tot_got = lax.ppermute(tot, 'seq', ahead)  8.92 us
    pallas_call x1, Pallas kernels, steps(): call(functools.partial(local_kernel, heads, rows, first, reach), [head_sp...  8.8 us
    pallas_call x1, Pallas kernels, plain(): call(functools.partial(plain_kernel, heads, rows), [plain_spec] * 4, [pla...  7.53 us
    pallas_call x1, Pallas kernels, steps(): call(functools.partial(stats_kernel, heads, rows, reach), [head_spec] * 4...  6.12 us
    ppermute x1, starting transfers between devices, steps(): got = lax.ppermute(sent, 'seq', back)  5.13 us
    pallas_call x1, Pallas kernels, steps(): pl.pallas_call(functools.partial(pack_kernel, heads, base, sizes), out_sh...  2.58 us
    ppermute x1, waiting for transfers between devices, steps(): st_got = lax.ppermute(st_send, 'seq', back)  2.39 us
  transfers between devices with their start and end apart: 4, of which 2 were waited for; matrix products, arithmetic and copies ran while one was open for 0% of the time, Pallas kernels for 37%

profile of v1, /device:TPU:0, one launch (start us, length us, event | category | flops | bytes accessed | tf_op | source)
XLA Modules:
  0.0 61.1 jit_solution(4249313561440800694)
XLA Ops:
  1.3 1.3 %meta.1 = s32[12]{0:T(128)S(1)} custom-call(s32[1]{0:T(128)S(6)} %copy.109.shift_ref, s32[32]{0:T(128)} %order_ref.1), custom_call_target="tpu_custom_call" | custom-call | tf_op jit(solution)/shard_map/meta/pallas_call | solution.py:359
  2.6 0.6 slice.3
  3.8 57.1 %conditional.1 = ((bf16[640,1024]{1,0:T(8,128)(2,1)}, bf16[640,1024]{1,0:T(8,128)(2,1)}, bf16[640,1024]{1,0:T(8,128)(2,1)})) conditional(s32[]{:T(128)} %bitcast, (s32[12]{0:T(128)S(1)}, bf16[640,1024]{1,0:T(8,128)(2,1)}, bf16[640,1024]{1,0:T(8,128)(2,1)}, bf16[640,1024]{1,0:T(8,128)(2,1)}, ...), branch_computations={%region_0.0_spmd, %region_1.0_spmd, %region_2.0_spmd, %region_3.0_... | conditional | flops 6291456000 | bytes 55968048 | solution.py:483
  3.9 0.0 copy-start.1
  3.9 0.0 copy-start.6
  3.9 2.6 %pack.6 = bf16[1472,256]{1,0:T(8,128)(2,1)S(1)} custom-call(s32[12]{0:T(128)S(1)} %get-tuple-element.83.meta, bf16[640,1024]{1,0:T(8,128)(2,1)} %get-tuple-element.190.q_ref, bf16[640,1024]{1,0:T(8,128)(2,1)} %get-tuple-element.208.d_ref), custom_call_target="tpu_custom_call" | custom-call | bytes 1507328 | tf_op jit(solution)/shard_map/cond/branch_2_fun/pack/pallas_call | solution.py:411
  6.5 5.1 %collective-permute-start.4 = (bf16[1472,256]{1,0:T(8,128)(2,1)S(1)}, bf16[1472,256]{1,0:T(8,128)(2,1)S(1)}, u32[]{:S(2)}, u32[]{:S(2)}) collective-permute-start(bf16[1472,256]{1,0:T(8,128)(2,1)S(1)} %pack.6), channel_id=1, source_target_pairs={{0,12},{4,0},{8,4},{12,8},{1,13},{5,1},{9,5},{13,9},{2,14},{6,2},{... | collective-permute-start | bytes 2261000 | tf_op jit(solution)/shard_map/cond/branch_2_fun/ppermute | solution.py:421
  11.6 0.0 copy-done.1
  11.6 0.0 copy-done.6
  11.6 0.0 copy-start.11
  11.6 0.0 copy-start.16
  11.6 6.1 %branch_2_fun.4 = (f32[8,2,512]{2,1,0:T(2,128)S(1)}, f32[8,2,640]{2,1,0:T(2,128)S(1)}) custom-call(s32[12]{0:T(128)S(1)} %get-tuple-element.83.meta, bf16[640,1024]{1,0:T(8,128)(2,1)S(1)} %copy-done.1, bf16[640,1024]{1,0:T(8,128)(2,1)} %get-tuple-element.196.k_ref, bf16[640,1024]{1,0:T(8,128)(2,1)} %get-tuple-element.202.v_ref, bf16[640,1024]{1,0:T(8,128)(2,1)S(1)} %copy-done.6), custom_call_target="tpu_custom_call" | custom-call | flops 838860800 | bytes 2621440 | tf_op jit(solution)/shard_map/cond/branch_2_fun/pallas_call | solution.py:422
  17.8 0.7 %collective-permute-start.5 = (f32[8,2,512]{2,1,0:T(2,128)S(1)}, f32[8,2,512]{2,1,0:T(2,128)S(1)}, u32[]{:S(2)}, u32[]{:S(2)}) collective-permute-start(f32[8,2,512]{2,1,0:T(2,128)S(1)} %get-tuple-element.89), channel_id=1, source_target_pairs={{0,12},{4,0},{8,4},{12,8},{1,13},{5,1},{9,5},{13,9},{2,14},{6,2},{... | collective-permute-start | bytes 98312 | tf_op jit(solution)/shard_map/cond/branch_2_fun/ppermute | solution.py:433
  18.4 0.0 copy-done.11
  18.4 0.0 copy-done.16
  18.4 7.5 %branch_2_fun.5 = (bf16[640,1024]{1,0:T(8,128)(2,1)}, bf16[640,1024]{1,0:T(8,128)(2,1)}, bf16[640,1024]{1,0:T(8,128)(2,1)}) custom-call(s32[12]{0:T(128)S(1)} %get-tuple-element.83.meta, bf16[640,1024]{1,0:T(8,128)(2,1)S(1)} %copy-done.1, bf16[640,1024]{1,0:T(8,128)(2,1)S(1)} %copy-done.11, bf16[640,1024]{1,0:T(8,128)(2,1)S(1)} %copy-done.16, ...), custom_call_target="tpu_custom_call" | custom-call | flops 1677721600 | bytes 4587520 | tf_op jit(solution)/shard_map/cond/branch_2_fun/pallas_call | solution.py:396
  26.0 2.4 %collective-permute-done.5.st_ref = f32[8,2,512]{2,1,0:T(2,128)S(1)} collective-permute-done((f32[8,2,512]{2,1,0:T(2,128)S(1)}, f32[8,2,512]{2,1,0:T(2,128)S(1)}, u32[]{:S(2)}, u32[]{:S(2)}) %collective-permute-start.5) | collective-permute-done | bytes 32800 | tf_op jit(solution)/shard_map/cond/branch_2_fun/ppermute | solution.py:433
  28.4 0.0 collective-permute-done.4.got_ref
  28.4 10.3 %branch_2_fun.6 = (bf16[1472,128]{1,0:T(8,128)(2,1)S(1)}, f32[8,2,512]{2,1,0:T(2,128)S(1)}, f32[8,480,128]{2,1,0:T(8,128)S(1)}, f32[8,480,128]{2,1,0:T(8,128)S(1)}) custom-call(s32[12]{0:T(128)S(1)} %get-tuple-element.83.meta, bf16[640,1024]{1,0:T(8,128)(2,1)S(1)} %copy-done.11, bf16[640,1024]{1,0:T(8,128)(2,1)S(1)} %copy-done.16, ...), custom_call_target="tpu_custom_call" | custom-call | flops 2097152000 | bytes 3932160 | tf_op jit(solution)/shard_map/cond/branch_2_fun/pallas_call | solution.py:436
  38.7 0.5 collective-permute-start.7
  39.2 1.6 %collective-permute-start.6 = (f32[8,2,512]{2,1,0:T(2,128)S(1)}, f32[8,2,512]{2,1,0:T(2,128)S(1)}, u32[]{:S(2)}, u32[]{:S(2)}) collective-permute-start(f32[8,2,512]{2,1,0:T(2,128)S(1)} %get-tuple-element.91), channel_id=1, source_target_pairs={{0,4},{4,8},{8,12},{12,0},{1,5},{5,9},{9,13},{13,1},{2,6},{6,10},{... | collective-permute-start | bytes 98312 | tf_op jit(solution)/shard_map/cond/branch_2_fun/ppermute | solution.py:450
  40.7 8.9 %collective-permute-done.6.tot_ref = f32[8,2,512]{2,1,0:T(2,128)S(1)} collective-permute-done((f32[8,2,512]{2,1,0:T(2,128)S(1)}, f32[8,2,512]{2,1,0:T(2,128)S(1)}, u32[]{:S(2)}, u32[]{:S(2)}) %collective-permute-start.6) | collective-permute-done | bytes 32800 | tf_op jit(solution)/shard_map/cond/branch_2_fun/ppermute | solution.py:450
  49.7 8.8 %branch_2_fun.7 = (bf16[640,1024]{1,0:T(8,128)(2,1)}, bf16[640,1024]{1,0:T(8,128)(2,1)}, bf16[640,1024]{1,0:T(8,128)(2,1)}, f32[8,512,128]{2,1,0:T(8,128)S(1)}) custom-call(s32[12]{0:T(128)S(1)} %get-tuple-element.83.meta, bf16[640,1024]{1,0:T(8,128)(2,1)S(1)} %copy-done.1, ...), custom_call_target="tpu_custom_call", output_to_operand_aliasing={{0}: (9, {}), {1}: (10, {}), {2}: (11, {})} | custom-call | flops 1677721600 | bytes 5898240 | tf_op jit(solution)/shard_map/cond/branch_2_fun/pallas_call | solution.py:452
  58.5 0.0 collective-permute-done.7.got_ref
  58.5 1.9 %add.6 = bf16[640,1024]{1,0:T(8,128)(2,1)} custom-call(s32[12]{0:T(128)S(1)} %get-tuple-element.83.meta, f32[8,512,128]{2,1,0:T(8,128)S(1)} %get-tuple-element.96.part_ref, bf16[1472,128]{1,0:T(8,128)(2,1)S(1)} %collective-permute-done.7.got_ref, bf16[640,1024]{1,0:T(8,128)(2,1)} %get-tuple-element.98._dq), custom_call_target="tpu_custom_call", output_to_operand_aliasing={{}: (3, {})} | custom-call | bytes 1966080 | tf_op jit(solution)/shard_map/cond/branch_2_fun/add/pallas_call | solution.py:464
Async XLA Ops:
  3.9 7.7 %copy-start.1 = (bf16[640,1024]{1,0:T(8,128)(2,1)S(1)}, bf16[640,1024]{1,0:T(8,128)(2,1)}, u32[]{:S(2)}) copy-start(bf16[640,1024]{1,0:T(8,128)(2,1)} %get-tuple-element.190.q_ref) | copy-start | bytes 3932164 | tf_op jit(solution)/shard_map/cond
  3.9 7.7 %copy-start.6 = (bf16[640,1024]{1,0:T(8,128)(2,1)S(1)}, bf16[640,1024]{1,0:T(8,128)(2,1)}, u32[]{:S(2)}) copy-start(bf16[640,1024]{1,0:T(8,128)(2,1)} %get-tuple-element.208.d_ref) | copy-start | bytes 3932164 | tf_op jit(solution)/shard_map/cond
  6.5 21.9 %collective-permute-start.4 = (bf16[1472,256]{1,0:T(8,128)(2,1)S(1)}, bf16[1472,256]{1,0:T(8,128)(2,1)S(1)}, u32[]{:S(2)}, u32[]{:S(2)}) collective-permute-start(bf16[1472,256]{1,0:T(8,128)(2,1)S(1)} %pack.6), channel_id=1, source_target_pairs={{0,12},{4,0},{8,4},{12,8},{1,13},{5,1},{9,5},{13,9},{2,14},{6,2},{... | collective-permute-start | bytes 2261000 | tf_op jit(solution)/shard_map/cond/branch_2_fun/ppermute | solution.py:421
  11.6 6.8 %copy-start.11 = (bf16[640,1024]{1,0:T(8,128)(2,1)S(1)}, bf16[640,1024]{1,0:T(8,128)(2,1)}, u32[]{:S(2)}) copy-start(bf16[640,1024]{1,0:T(8,128)(2,1)} %get-tuple-element.196.k_ref) | copy-start | bytes 3932164 | tf_op jit(solution)/shard_map/cond
  11.6 6.8 %copy-start.16 = (bf16[640,1024]{1,0:T(8,128)(2,1)S(1)}, bf16[640,1024]{1,0:T(8,128)(2,1)}, u32[]{:S(2)}) copy-start(bf16[640,1024]{1,0:T(8,128)(2,1)} %get-tuple-element.202.v_ref) | copy-start | bytes 3932164 | tf_op jit(solution)/shard_map/cond
  17.8 10.6 %collective-permute-start.5 = (f32[8,2,512]{2,1,0:T(2,128)S(1)}, f32[8,2,512]{2,1,0:T(2,128)S(1)}, u32[]{:S(2)}, u32[]{:S(2)}) collective-permute-start(f32[8,2,512]{2,1,0:T(2,128)S(1)} %get-tuple-element.89), channel_id=1, source_target_pairs={{0,12},{4,0},{8,4},{12,8},{1,13},{5,1},{9,5},{13,9},{2,14},{6,2},{... | collective-permute-start | bytes 98312 | tf_op jit(solution)/shard_map/cond/branch_2_fun/ppermute | solution.py:433
  38.7 19.8 %collective-permute-start.7 = (bf16[1472,128]{1,0:T(8,128)(2,1)S(1)}, bf16[1472,128]{1,0:T(8,128)(2,1)S(1)}, u32[]{:S(2)}, u32[]{:S(2)}) collective-permute-start(bf16[1472,128]{1,0:T(8,128)(2,1)S(1)} %get-tuple-element.97), channel_id=1, source_target_pairs={{0,4},{4,8},{8,12},{12,0},{1,5},{5,9},{9,13},{13,1},{2,6},{6,10},{... | collective-permute-start | bytes 1130504 | tf_op jit(solution)/shard_map/cond/branch_2_fun/ppermute | solution.py:451
  39.2 10.5 %collective-permute-start.6 = (f32[8,2,512]{2,1,0:T(2,128)S(1)}, f32[8,2,512]{2,1,0:T(2,128)S(1)}, u32[]{:S(2)}, u32[]{:S(2)}) collective-permute-start(f32[8,2,512]{2,1,0:T(2,128)S(1)} %get-tuple-element.91), channel_id=1, source_target_pairs={{0,4},{4,8},{8,12},{12,0},{1,5},{5,9},{9,13},{13,1},{2,6},{6,10},{... | collective-permute-start | bytes 98312 | tf_op jit(solution)/shard_map/cond/branch_2_fun/ppermute | solution.py:450

commit v2 on v1

--- a/solution.py
+++ b/solution.py
@@ -16,6 +16,7 @@
 NEG = -1e30
 GRAIN = 32
 BLOCK = 256
+PART = 0.6
 F32 = jnp.float32
 BF16 = jnp.bfloat16
 
@@ -80,41 +81,70 @@
     return lambda s, m: m[jnp.minimum(s, m[heads] - 1)]
 
 
-def pack_kernel(heads, base, sizes, meta, q_ref, d_ref, out_ref, sem):
+def pack_kernel(heads, base, sizes, meta, q_ref, d_ref, one_ref, two_ref, sem, mid_ref):
     count, slot = meta[heads], meta[heads + 2]
+    split = one_ref.shape[0]
 
     def each(act):
         def step(s, c):
             column = pl.multiple_of(meta[s] * HDIM, HDIM)
-
-            def copy(at, size, i):
-                src = pl.multiple_of(at, GRAIN)
-                dst = pl.multiple_of(s * slot + at, GRAIN)
-                for j, ref in enumerate((q_ref, d_ref)):
-                    act(
-                        pltpu.make_async_copy(
-                            ref.at[pl.ds(src, size), pl.ds(column, HDIM)],
-                            out_ref.at[pl.ds(dst, size), pl.ds(j * HDIM, HDIM)],
-                            sem.at[s, j, i],
+            low = s * slot
+            for ref, shift, mine in (
+                (one_ref, low, low + slot <= split),
+                (two_ref, low - split, low >= split),
+                (mid_ref, 0, (low < split) & (low + slot > split)),
+            ):
+
+                def copy(at, size, i, ref=ref, shift=shift):
+                    src = pl.multiple_of(at, GRAIN)
+                    dst = pl.multiple_of(shift + at, GRAIN)
+                    for j, from_ref in enumerate((q_ref, d_ref)):
+                        act(
+                            pltpu.make_async_copy(
+                                from_ref.at[pl.ds(src, size), pl.ds(column, HDIM)],
+                                ref.at[pl.ds(dst, size), pl.ds(j * HDIM, HDIM)],
+                                sem.at[s, j, i],
+                            )
                         )
-                    )
-
-            copy(0, base, 0)
-            at = jnp.int32(base)
-            for i, size in enumerate(sizes):
-                bit = ((slot - base) // size) % 2
-
-                @pl.when(bit == 1)
-                def _(at=at, size=size, i=i):
-                    copy(at, size, i + 1)
-
-                at = at + bit * size
+
+                @pl.when(mine)
+                def _(copy=copy):
+                    copy(0, base, 0)
+                    at = jnp.int32(base)
+                    for i, size in enumerate(sizes):
+                        bit = ((slot - base) // size) % 2
+
+                        @pl.when(bit == 1)
+                        def _(at=at, size=size, i=i):
+                            copy(at, size, i + 1)
+
+                        at = at + bit * size
+
             return c
 
         lax.fori_loop(0, count, step, 0)
 
     each(lambda copy: copy.start())
     each(lambda copy: copy.wait())
+    low = split // slot * slot
+    cut = split - low
+
+    @pl.when((low < count * slot) & (cut > 0))
+    def _():
+        def front(i, c):
+            src = pl.multiple_of(i * GRAIN, GRAIN)
+            dst = pl.multiple_of(low + i * GRAIN, GRAIN)
+            one_ref[pl.ds(dst, GRAIN), :] = mid_ref[pl.ds(src, GRAIN), :]
+            return c
+
+        def rest(i, c):
+            src = pl.multiple_of(cut + i * GRAIN, GRAIN)
+            dst = pl.multiple_of(i * GRAIN, GRAIN)
+            two_ref[pl.ds(dst, GRAIN), :] = mid_ref[pl.ds(src, GRAIN), :]
+            return c
+
+        lax.fori_loop(0, cut // GRAIN, front, 0)
+        lax.fori_loop(0, (slot - cut) // GRAIN, rest, 0)
 
 
 def stats_kernel(heads, rows, reach, meta, q_ref, k_ref, v_ref, d_ref, send_ref, own_ref):
@@ -184,22 +214,36 @@
         dv_ref[...] = av_ref[...].astype(BF16)
 
 
-def cross_kernel(
-    heads, rows, first, meta, k_ref, v_ref, got_ref, st_ref, _after,
-    back_ref, tot_ref, gk_ref, gv_ref, buf_ref, acc_ref,
-):
+def cross_kernel(heads, rows, first, split, later, meta, *refs):
+    if later:
+        (k_ref, v_ref, one_ref, two_ref, st_ref, back0_ref, tot0_ref, gk0_ref, gv0_ref,
+         back_ref, tot_ref, gk_ref, gv_ref, buf_ref, acc_ref) = refs
+    else:
+        (k_ref, v_ref, one_ref, st_ref, _,
+         back_ref, tot_ref, gk_ref, gv_ref, buf_ref, acc_ref) = refs
     s = pl.program_id(0)
     count, off, slot = meta[heads], meta[heads + 1], meta[heads + 2]
-    filled = count * slot
-
-    @pl.when(s == 0)
-    def _():
+    done = jnp.minimum(count, split // slot)
+    low, high = (done, count) if later else (0, done)
+
+    def move(dst_ref, src_ref, start, stop, shift):
         def step(i, c):
-            at = pl.multiple_of(i * GRAIN, GRAIN)
-            buf_ref[pl.ds(at, GRAIN), :] = got_ref[pl.ds(at, GRAIN), :]
+            dst = pl.multiple_of(start + i * GRAIN, GRAIN)
+            src = pl.multiple_of(start - shift + i * GRAIN, GRAIN)
+            dst_ref[pl.ds(dst, GRAIN), :] = src_ref[pl.ds(src, GRAIN), :]
             return c
 
-        lax.fori_loop(0, filled // GRAIN, step, 0)
+        lax.fori_loop(0, (stop - start) // GRAIN, step, 0)
+
+    @pl.when((s == 0) & (low < high))
+    def _():
+        filled = high * slot
+        if later:
+            edge = jnp.minimum(filled, split)
+            move(buf_ref, one_ref, low * slot, edge, 0)
+            move(buf_ref, two_ref, edge, filled, split)
+        else:
+            move(buf_ref, one_ref, 0, filled, 0)
         tail = pl.multiple_of(filled, GRAIN)
         buf_ref[pl.ds(tail, BLOCK), :] = jnp.zeros((BLOCK, 2 * HDIM), BF16)
 
@@ -233,7 +277,15 @@
         gk_ref[s, k0 - first :, :] += dot_nn(ds, qb)
         acc_ref[pl.ds(start, BLOCK), :] = (dot_tn(ds, kb) * SCALE).astype(BF16)
 
-    @pl.when(s < count)
+    if later:
+
+        @pl.when(s < low)
+        def _():
+            tot_ref[s] = tot0_ref[s]
+            gk_ref[s] = gk0_ref[s]
+            gv_ref[s] = gv0_ref[s]
+
+    @pl.when((s >= low) & (s < high))
     def _():
         gv_ref[s] = jnp.zeros(gv_ref.shape[1:], F32)
         gk_ref[s] = jnp.zeros(gk_ref.shape[1:], F32)
@@ -251,12 +303,9 @@
 
     @pl.when(s == pl.num_programs(0) - 1)
     def _():
-        def step(i, c):
-            at = pl.multiple_of(i * GRAIN, GRAIN)
-            back_ref[pl.ds(at, GRAIN), :] = acc_ref[pl.ds(at, GRAIN), :]
-            return c
-
-        lax.fori_loop(0, filled // GRAIN, step, 0)
+        if later:
+            move(back_ref, back0_ref, 0, low * slot, 0)
+        move(back_ref, acc_ref, low * slot, high * slot, 0)
 
 
 def local_kernel(
@@ -350,7 +399,7 @@
     tallest = up(last, GRAIN)
     reach = up(last, BLOCK)
     most = heads * tallest
-    fractions = (0.25, 0.38, 0.5, 0.67, 1.0)
+    fractions = (0.36, 0.52, 0.7, 1.0)
     caps = [up(int(most * f), GRAIN) for f in fractions]
     seq = lax.axis_size("seq")
     back = [(i, (i - 1) % seq) for i in range(seq)]
@@ -408,17 +457,22 @@
             sizes, left = [], tallest - base
             while sum(sizes) < left:
                 sizes.append(GRAIN * 2 ** len(sizes))
-            sent = pl.pallas_call(
+            split = up(int(cap * PART), GRAIN)
+            shapes = [jax.ShapeDtypeStruct((n, 2 * HDIM), BF16) for n in (split, cap - split)]
+            one, two = pl.pallas_call(
                 functools.partial(pack_kernel, heads, base, sizes),
-                out_shape=jax.ShapeDtypeStruct((cap, 2 * HDIM), BF16),
+                out_shape=shapes,
                 in_specs=[smem, any_spec, any_spec],
-                out_specs=vmem,
-                scratch_shapes=[pltpu.SemaphoreType.DMA((heads, 2, 1 + len(sizes)))],
+                out_specs=[vmem, vmem],
+                scratch_shapes=[
+                    pltpu.SemaphoreType.DMA((heads, 2, 1 + len(sizes))),
+                    pltpu.VMEM((tallest, 2 * HDIM), BF16),
+                ],
                 cost_estimate=cost(0, 2 * cap * HDIM * 4),
                 compiler_params=params(8),
                 name="pack",
             )(meta, queries, d_out)
-            got = lax.ppermute(sent, "seq", back)
+            one_got = lax.ppermute(one, "seq", back)
             st_send, st_own = call(
                 functools.partial(stats_kernel, heads, rows, reach),
                 [head_spec] * 4,
@@ -431,22 +485,38 @@
                 16,
             )(meta, queries, keys, values, d_out)
             st_got = lax.ppermute(st_send, "seq", back)
+            two_got = lax.ppermute(two, "seq", back)
             dq, dk, dv = plain(meta, queries, keys, values, d_out)
             side = jax.ShapeDtypeStruct((heads, rows - first, HDIM), F32)
-            back_q, tot, gk, gv = call(
-                functools.partial(cross_kernel, heads, rows, first),
-                [head_spec] * 2 + [vmem, vmem, any_spec],
-                [vmem] * 4,
-                [
-                    jax.ShapeDtypeStruct((cap, HDIM), BF16),
-                    jax.ShapeDtypeStruct((heads, 2, reach), F32),
-                    side,
-                    side,
-                ],
-                cost(heads / 2 * 5 * work, heads / 2 * 6 * tile),
-                24,
-                [pltpu.VMEM((cap + BLOCK, 2 * HDIM), BF16), pltpu.VMEM((cap + BLOCK, HDIM), BF16)],
-            )(meta, keys, values, got, st_got, dq)
+
+            def cross(later, size, *args):
+                def block_of(s, m):
+                    done = jnp.minimum(m[heads], split // m[heads + 2])
+                    low, high = (done, m[heads]) if later else (0, done)
+                    s = jnp.maximum(jnp.minimum(s, high - 1), low)
+                    return (0, m[jnp.minimum(s, heads - 1)])
+
+                mine = pl.BlockSpec((rows, HDIM), block_of)
+                return call(
+                    functools.partial(cross_kernel, heads, rows, first, split, later),
+                    [mine] * 2 + ([vmem] * 7 if later else [vmem, vmem, any_spec]),
+                    [vmem] * 4,
+                    [
+                        jax.ShapeDtypeStruct((size, HDIM), BF16),
+                        jax.ShapeDtypeStruct((heads, 2, reach), F32),
+                        side,
+                        side,
+                    ],
+                    cost(heads / 4 * 5 * work, heads / 4 * 6 * tile),
+                    20,
+                    [
+                        pltpu.VMEM((size + BLOCK, 2 * HDIM), BF16),
+                        pltpu.VMEM((size + BLOCK, HDIM), BF16),
+                    ],
+                )(meta, keys, values, *args)
+
+            begun = cross(False, split, one_got, st_got, dq)
+            back_q, tot, gk, gv = cross(True, cap, one_got, two_got, st_got, *begun)
             tot_got = lax.ppermute(tot, "seq", ahead)
             dq_got = lax.ppermute(back_q, "seq", ahead)
             dq, dk, dv, part = call(

time: 61.4 us -> 71.5 us (1.16)
  loops' own time: 0.62 us -> 5.32 us
  waiting for transfers between devices: 11.3 us -> 14.2 us
  Pallas kernels: 38.6 us -> 40.6 us
    another operation x1, loops' own time: 0.62 us -> 5.32 us  [shards(): lax.switch(meta[heads + 3], [plain] + [branch(cap) for cap in caps], meta...]
    ppermute x1, waiting for transfers between devices: 2.39 us -> 4.49 us  [steps(): st_got = lax.ppermute(st_send, 'seq', back)]
    pallas_call x1 -> x2, Pallas kernels: 10.3 us -> 12.3 us  [cross(): call(functools.partial(cross_kernel, heads, rows, first, split, later), [...]
    ppermute x1, waiting for transfers between devices: 8.92 us -> 9.69 us  [steps(): tot_got = lax.ppermute(tot, 'seq', ahead)]
    ppermute x1 -> x2, starting transfers between devices: 5.13 us -> 5.58 us  [the longest x1 5.13 us: steps(): one_got = lax.ppermute(one, 'seq', back)]
  transfers between devices with their start and end apart: 4 -> 5, of which waited for: 2 -> 2; matrix products, arithmetic and copies ran while one was open for 0% -> 0% of each run, Pallas kernels for 37% -> 44%
where the time goes in v2:
time: 71.5 us; the launch traced here: 71.3 us
  Pallas kernels  40.6 us (57%)
  waiting for transfers between devices  14.2 us (20%)
  starting transfers between devices  8.4 us (12%)
  loops' own time  5.32 us (7%)
  between operations  2.12 us (3%)
    pallas_call x2, Pallas kernels, cross(): call(functools.partial(cross_kernel, heads, rows, first, split, later), [...  12.3 us
    ppermute x1, waiting for transfers between devices, steps(): tot_got = lax.ppermute(tot, 'seq', ahead)  9.69 us
    pallas_call x1, Pallas kernels, steps(): call(functools.partial(local_kernel, heads, rows, first, reach), [head_sp...  8.83 us
    pallas_call x1, Pallas kernels, plain(): call(functools.partial(plain_kernel, heads, rows), [plain_spec] * 4, [pla...  7.53 us
    pallas_call x1, Pallas kernels, steps(): call(functools.partial(stats_kernel, heads, rows, reach), [head_spec] * 4...  6.1 us
    another operation x1, loops' own time, shards(): lax.switch(meta[heads + 3], [plain] + [branch(cap) for cap in caps], meta...  5.32 us
    ppermute x1, starting transfers between devices, steps(): one_got = lax.ppermute(one, 'seq', back)  5.13 us
    ppermute x1, waiting for transfers between devices, steps(): st_got = lax.ppermute(st_send, 'seq', back)  4.49 us
  transfers between devices with their start and end apart: 5, of which 2 were waited for; matrix products, arithmetic and copies ran while one was open for 0% of the time, Pallas kernels for 44%

profile of v2, /device:TPU:0, one launch (start us, length us, event | category | flops | bytes accessed | tf_op | source)
XLA Modules:
  0.0 71.3 jit_solution(15657467604707758849)
XLA Ops:
  1.3 1.3 %meta.1 = s32[12]{0:T(128)S(1)} custom-call(s32[1]{0:T(128)S(6)} %copy.91.shift_ref, s32[32]{0:T(128)} %order_ref.1), custom_call_target="tpu_custom_call" | custom-call | tf_op jit(solution)/shard_map/meta/pallas_call | solution.py:408
  2.6 0.6 slice.3
  3.8 67.2 %conditional.1 = ((bf16[640,1024]{1,0:T(8,128)(2,1)}, bf16[640,1024]{1,0:T(8,128)(2,1)}, bf16[640,1024]{1,0:T(8,128)(2,1)})) conditional(s32[]{:T(128)} %bitcast, (s32[12]{0:T(128)S(1)}, bf16[640,1024]{1,0:T(8,128)(2,1)}, bf16[640,1024]{1,0:T(8,128)(2,1)}, bf16[640,1024]{1,0:T(8,128)(2,1)}, ...), branch_computations={%region_0.0_spmd, %region_1.0_spmd, %region_2.0_spmd, %region_3.0_... | conditional | flops 6291456000 | bytes 55968088 | solution.py:553
  3.9 0.0 copy-start.1
  3.9 0.0 copy-start.5
  3.9 2.6 %pack.5 = (bf16[1216,256]{1,0:T(8,128)(2,1)S(1)}, bf16[800,256]{1,0:T(8,128)(2,1)S(1)}) custom-call(s32[12]{0:T(128)S(1)} %get-tuple-element.79.meta, bf16[640,1024]{1,0:T(8,128)(2,1)} %get-tuple-element.182.q_ref, bf16[640,1024]{1,0:T(8,128)(2,1)} %get-tuple-element.197.d_ref), custom_call_target="tpu_custom_call" | custom-call | bytes 2064384 | tf_op jit(solution)/shard_map/cond/branch_2_fun/pack/pallas_call | solution.py:462
  6.5 5.1 %collective-permute-start.5 = (bf16[1216,256]{1,0:T(8,128)(2,1)S(1)}, bf16[1216,256]{1,0:T(8,128)(2,1)S(1)}, u32[]{:S(2)}, u32[]{:S(2)}) collective-permute-start(bf16[1216,256]{1,0:T(8,128)(2,1)S(1)} %get-tuple-element.85), channel_id=1, source_target_pairs={{0,12},{4,0},{8,4},{12,8},{1,13},{5,1},{9,5},{13,9},{2,14},{6,2},{... | collective-permute-start | bytes 1867784 | tf_op jit(solution)/shard_map/cond/branch_2_fun/ppermute | solution.py:475
  11.7 0.4 collective-permute-start.6
  12.1 0.0 copy-done.1
  12.1 0.0 copy-done.5
  12.1 0.0 copy-start.9
  12.1 0.0 copy-start.13
  12.1 6.1 %branch_2_fun.5 = (f32[8,2,512]{2,1,0:T(2,128)S(1)}, f32[8,2,640]{2,1,0:T(2,128)S(1)}) custom-call(s32[12]{0:T(128)S(1)} %get-tuple-element.79.meta, bf16[640,1024]{1,0:T(8,128)(2,1)} %get-tuple-element.182.q_ref, bf16[640,1024]{1,0:T(8,128)(2,1)S(1)} %copy-done.1, bf16[640,1024]{1,0:T(8,128)(2,1)S(1)} %copy-done.5, bf16[640,1024]{1,0:T(8,128)(2,1)} %get-tuple-element.197.d_ref), custom_call_target="tpu_custom_call" | custom-call | flops 838860800 | bytes 2621440 | tf_op jit(solution)/shard_map/cond/branch_2_fun/pallas_call | solution.py:476
  18.2 0.7 %collective-permute-start.7 = (f32[8,2,512]{2,1,0:T(2,128)S(1)}, f32[8,2,512]{2,1,0:T(2,128)S(1)}, u32[]{:S(2)}, u32[]{:S(2)}) collective-permute-start(f32[8,2,512]{2,1,0:T(2,128)S(1)} %get-tuple-element.87), channel_id=1, source_target_pairs={{0,12},{4,0},{8,4},{12,8},{1,13},{5,1},{9,5},{13,9},{2,14},{6,2},{... | collective-permute-start | bytes 98312 | tf_op jit(solution)/shard_map/cond/branch_2_fun/ppermute | solution.py:487
  19.0 0.0 copy-done.9
  19.0 0.0 copy-done.13
  19.0 7.5 %branch_2_fun.6 = (bf16[640,1024]{1,0:T(8,128)(2,1)}, bf16[640,1024]{1,0:T(8,128)(2,1)}, bf16[640,1024]{1,0:T(8,128)(2,1)}) custom-call(s32[12]{0:T(128)S(1)} %get-tuple-element.79.meta, bf16[640,1024]{1,0:T(8,128)(2,1)S(1)} %copy-done.9, bf16[640,1024]{1,0:T(8,128)(2,1)S(1)} %copy-done.1, bf16[640,1024]{1,0:T(8,128)(2,1)S(1)} %copy-done.5, ...), custom_call_target="tpu_custom_call" | custom-call | flops 1677721600 | bytes 4587520 | tf_op jit(solution)/shard_map/cond/branch_2_fun/pallas_call | solution.py:445
  26.5 4.5 %collective-permute-done.7.refs_3_.refs_4_ = f32[8,2,512]{2,1,0:T(2,128)S(1)} collective-permute-done((f32[8,2,512]{2,1,0:T(2,128)S(1)}, f32[8,2,512]{2,1,0:T(2,128)S(1)}, u32[]{:S(2)}, u32[]{:S(2)}) %collective-permute-start.7) | collective-permute-done | bytes 32800 | tf_op jit(solution)/shard_map/cond/branch_2_fun/ppermute | solution.py:487
  31.0 0.0 collective-permute-done.5.refs_2_
  31.0 8.8 %branch_2_fun.7 = (bf16[1216,128]{1,0:T(8,128)(2,1)S(1)}, f32[8,2,512]{2,1,0:T(2,128)S(1)}, f32[8,480,128]{2,1,0:T(8,128)S(1)}, f32[8,480,128]{2,1,0:T(8,128)S(1)}) custom-call(s32[12]{0:T(128)S(1)} %get-tuple-element.79.meta, bf16[640,1024]{1,0:T(8,128)(2,1)S(1)} %copy-done.1, bf16[640,1024]{1,0:T(8,128)(2,1)S(1)} %copy-done.5, ...), custom_call_target="tpu_custom_call" | custom-call | flops 1048576000 | bytes 1966080 | tf_op jit(solution)/shard_map/cond/branch_2_fun/pallas_call | solution.py:500
  39.8 0.0 collective-permute-done.6.refs_3_
  39.8 3.5 %branch_2_fun.8 = (bf16[2016,128]{1,0:T(8,128)(2,1)S(1)}, f32[8,2,512]{2,1,0:T(2,128)S(1)}, f32[8,480,128]{2,1,0:T(8,128)S(1)}, f32[8,480,128]{2,1,0:T(8,128)S(1)}) custom-call(s32[12]{0:T(128)S(1)} %get-tuple-element.79.meta, bf16[640,1024]{1,0:T(8,128)(2,1)S(1)} %copy-done.1, bf16[640,1024]{1,0:T(8,128)(2,1)S(1)} %copy-done.5, ...), custom_call_target="tpu_custom_call" | custom-call | flops 1048576000 | bytes 1966080 | tf_op jit(solution)/shard_map/cond/branch_2_fun/pallas_call | solution.py:500
  43.3 0.5 collective-permute-start.9
  43.9 1.5 %collective-permute-start.8 = (f32[8,2,512]{2,1,0:T(2,128)S(1)}, f32[8,2,512]{2,1,0:T(2,128)S(1)}, u32[]{:S(2)}, u32[]{:S(2)}) collective-permute-start(f32[8,2,512]{2,1,0:T(2,128)S(1)} %get-tuple-element.93), channel_id=1, source_target_pairs={{0,4},{4,8},{8,12},{12,0},{1,5},{5,9},{9,13},{13,1},{2,6},{6,10},{... | collective-permute-start | bytes 98312 | tf_op jit(solution)/shard_map/cond/branch_2_fun/ppermute | solution.py:520
  45.4 9.7 %collective-permute-done.8.tot_ref = f32[8,2,512]{2,1,0:T(2,128)S(1)} collective-permute-done((f32[8,2,512]{2,1,0:T(2,128)S(1)}, f32[8,2,512]{2,1,0:T(2,128)S(1)}, u32[]{:S(2)}, u32[]{:S(2)}) %collective-permute-start.8) | collective-permute-done | bytes 32800 | tf_op jit(solution)/shard_map/cond/branch_2_fun/ppermute | solution.py:520
  55.1 8.8 %branch_2_fun.9 = (bf16[640,1024]{1,0:T(8,128)(2,1)}, bf16[640,1024]{1,0:T(8,128)(2,1)}, bf16[640,1024]{1,0:T(8,128)(2,1)}, f32[8,512,128]{2,1,0:T(8,128)S(1)}) custom-call(s32[12]{0:T(128)S(1)} %get-tuple-element.79.meta, bf16[640,1024]{1,0:T(8,128)(2,1)S(1)} %copy-done.9, ...), custom_call_target="tpu_custom_call", output_to_operand_aliasing={{0}: (9, {}), {1}: (10, {}), {2}: (11, {})} | custom-call | flops 1677721600 | bytes 5898240 | tf_op jit(solution)/shard_map/cond/branch_2_fun/pallas_call | solution.py:522
  63.9 0.0 collective-permute-done.9.got_ref
  63.9 1.9 %add.5 = bf16[640,1024]{1,0:T(8,128)(2,1)} custom-call(s32[12]{0:T(128)S(1)} %get-tuple-element.79.meta, f32[8,512,128]{2,1,0:T(8,128)S(1)} %get-tuple-element.98.part_ref, bf16[2016,128]{1,0:T(8,128)(2,1)S(1)} %collective-permute-done.9.got_ref, bf16[640,1024]{1,0:T(8,128)(2,1)} %get-tuple-element.100._dq), custom_call_target="tpu_custom_call", output_to_operand_aliasing={{}: (3, {})} | custom-call | bytes 1966080 | tf_op jit(solution)/shard_map/cond/branch_2_fun/add/pallas_call | solution.py:534
Async XLA Ops:
  3.9 8.2 %copy-start.1 = (bf16[640,1024]{1,0:T(8,128)(2,1)S(1)}, bf16[640,1024]{1,0:T(8,128)(2,1)}, u32[]{:S(2)}) copy-start(bf16[640,1024]{1,0:T(8,128)(2,1)} %get-tuple-element.187.k_ref.refs_0_) | copy-start | bytes 3932164 | tf_op jit(solution)/shard_map/cond
  3.9 8.2 %copy-start.5 = (bf16[640,1024]{1,0:T(8,128)(2,1)S(1)}, bf16[640,1024]{1,0:T(8,128)(2,1)}, u32[]{:S(2)}) copy-start(bf16[640,1024]{1,0:T(8,128)(2,1)} %get-tuple-element.192.v_ref.refs_1_) | copy-start | bytes 3932164 | tf_op jit(solution)/shard_map/cond
  6.5 24.5 %collective-permute-start.5 = (bf16[1216,256]{1,0:T(8,128)(2,1)S(1)}, bf16[1216,256]{1,0:T(8,128)(2,1)S(1)}, u32[]{:S(2)}, u32[]{:S(2)}) collective-permute-start(bf16[1216,256]{1,0:T(8,128)(2,1)S(1)} %get-tuple-element.85), channel_id=1, source_target_pairs={{0,12},{4,0},{8,4},{12,8},{1,13},{5,1},{9,5},{13,9},{2,14},{6,2},{... | collective-permute-start | bytes 1867784 | tf_op jit(solution)/shard_map/cond/branch_2_fun/ppermute | solution.py:475
  11.7 28.1 %collective-permute-start.6 = (bf16[800,256]{1,0:T(8,128)(2,1)S(1)}, bf16[800,256]{1,0:T(8,128)(2,1)S(1)}, u32[]{:S(2)}, u32[]{:S(2)}) collective-permute-start(bf16[800,256]{1,0:T(8,128)(2,1)S(1)} %get-tuple-element.86), channel_id=1, source_target_pairs={{0,12},{4,0},{8,4},{12,8},{1,13},{5,1},{9,5},{13,9},{2,14},{6,2},{... | collective-permute-start | bytes 1228808 | tf_op jit(solution)/shard_map/cond/branch_2_fun/ppermute | solution.py:488
  12.1 6.9 %copy-start.9 = (bf16[640,1024]{1,0:T(8,128)(2,1)S(1)}, bf16[640,1024]{1,0:T(8,128)(2,1)}, u32[]{:S(2)}) copy-start(bf16[640,1024]{1,0:T(8,128)(2,1)} %get-tuple-element.182.q_ref) | copy-start | bytes 3932164 | tf_op jit(solution)/shard_map/cond
  12.1 6.9 %copy-start.13 = (bf16[640,1024]{1,0:T(8,128)(2,1)S(1)}, bf16[640,1024]{1,0:T(8,128)(2,1)}, u32[]{:S(2)}) copy-start(bf16[640,1024]{1,0:T(8,128)(2,1)} %get-tuple-element.197.d_ref) | copy-start | bytes 3932164 | tf_op jit(solution)/shard_map/cond
  18.2 12.8 %collective-permute-start.7 = (f32[8,2,512]{2,1,0:T(2,128)S(1)}, f32[8,2,512]{2,1,0:T(2,128)S(1)}, u32[]{:S(2)}, u32[]{:S(2)}) collective-permute-start(f32[8,2,512]{2,1,0:T(2,128)S(1)} %get-tuple-element.87), channel_id=1, source_target_pairs={{0,12},{4,0},{8,4},{12,8},{1,13},{5,1},{9,5},{13,9},{2,14},{6,2},{... | collective-permute-start | bytes 98312 | tf_op jit(solution)/shard_map/cond/branch_2_fun/ppermute | solution.py:487
  43.3 20.6 %collective-permute-start.9 = (bf16[2016,128]{1,0:T(8,128)(2,1)S(1)}, bf16[2016,128]{1,0:T(8,128)(2,1)S(1)}, u32[]{:S(2)}, u32[]{:S(2)}) collective-permute-start(bf16[2016,128]{1,0:T(8,128)(2,1)S(1)} %get-tuple-element.99), channel_id=1, source_target_pairs={{0,4},{4,8},{8,12},{12,0},{1,5},{5,9},{9,13},{13,1},{2,6},{6,10},{... | collective-permute-start | bytes 1548296 | tf_op jit(solution)/shard_map/cond/branch_2_fun/ppermute | solution.py:521
  43.9 11.2 %collective-permute-start.8 = (f32[8,2,512]{2,1,0:T(2,128)S(1)}, f32[8,2,512]{2,1,0:T(2,128)S(1)}, u32[]{:S(2)}, u32[]{:S(2)}) collective-permute-start(f32[8,2,512]{2,1,0:T(2,128)S(1)} %get-tuple-element.93), channel_id=1, source_target_pairs={{0,4},{4,8},{8,12},{12,0},{1,5},{5,9},{9,13},{13,1},{2,6},{6,10},{... | collective-permute-start | bytes 98312 | tf_op jit(solution)/shard_map/cond/branch_2_fun/ppermute | solution.py:520

commit v3 on v2

--- a/solution.py
+++ b/solution.py
@@ -41,10 +41,58 @@
     return [(q0, min(BLOCK, rows - q0)) for q0 in range(0, rows, BLOCK)]
 
 
-def iotas(k0, kn, q0, w):
+def mask_of(q0, w, diagonal, low=None):
+    k0, kn = (q0, w) if diagonal else (0, q0)
     key = k0 + lax.broadcasted_iota(jnp.int32, (kn, w), 0)
     query = q0 + lax.broadcasted_iota(jnp.int32, (1, w), 1)
-    return key, query
+    if low is None:
+        return key <= query
+    return (key >= low) & (key <= query) if diagonal else key >= low
+
+
+def masked(x, q0, w, other, low=None):
+    below = jnp.where(mask_of(q0, w, True, low), x[q0:], other)
+    if not q0:
+        return below
+    above = x[:q0] if low is None else jnp.where(mask_of(q0, w, False, low), x[:q0], other)
+    return jnp.concatenate([above, below], axis=0)
+
+
+def staggered(blocks, front, back):
+    held = None
+    for block in blocks:
+        fresh = front(*block)
+        if held is not None:
+            back(*held)
+        held = (*block, fresh)
+    back(*held)
+
+
+def column(meta, s):
+    return pl.ds(pl.multiple_of(meta[s] * HDIM, HDIM), HDIM)
+
+
+def written_out(start, stop, copies, compute):
+    def finish(s):
+        for copy in copies(s):
+            copy.wait()
+
+    def step(s, c):
+        @pl.when(s >= start + 2)
+        def _():
+            finish(s - 2)
+
+        compute(s)
+        for copy in copies(s):
+            copy.start()
+        return c
+
+    lax.fori_loop(start, stop, step, 0)
+    for back in (2, 1):
+
+        @pl.when(stop - back >= start)
+        def _(back=back):
+            finish(stop - back)
 
 
 def meta_kernel(heads, grain, caps, shift_ref, order_ref, out_ref, flag_ref):
@@ -77,10 +125,6 @@
     out_ref[heads + 3] = pick
 
 
-def shifted_at(heads):
-    return lambda s, m: m[jnp.minimum(s, m[heads] - 1)]
-
-
 def pack_kernel(heads, base, sizes, meta, q_ref, d_ref, one_ref, two_ref, sem, mid_ref):
     count, slot = meta[heads], meta[heads + 2]
     split = one_ref.shape[0]
@@ -148,21 +192,24 @@
 
 
 def stats_kernel(heads, rows, reach, meta, q_ref, k_ref, v_ref, d_ref, send_ref, own_ref):
-    s = pl.program_id(0)
-
-    @pl.when(s < meta[heads])
-    def _():
-        off = meta[heads + 1]
-        for q0, w in query_blocks(rows):
+    off = meta[heads + 1]
+
+    def step(s, c):
+        col = column(meta, s)
+
+        def front(q0, w):
             kn = q0 + w
-            key, query = iotas(0, kn, q0, w)
-            low = jnp.where(query >= off, off, 0)
-            sc = dot_nt(k_ref[:kn, :], q_ref[q0:kn, :]) * LOG2_SCALE
-            sc = jnp.where((key <= query) & (key >= low), sc, NEG)
+            sc = dot_nt(k_ref[:kn, col], q_ref[q0:kn, col]) * LOG2_SCALE
+            return sc, dot_nt(v_ref[:kn, col], d_ref[q0:kn, col])
+
+        def back(q0, w, held):
+            sc, dp = held
+            kn = q0 + w
+            query = q0 + lax.broadcasted_iota(jnp.int32, (1, w), 1)
+            sc = masked(sc, q0, w, NEG, jnp.where(query >= off, off, 0))
             top = jnp.max(sc, axis=0, keepdims=True)
             e = jnp.exp2(sc - top)
             total = jnp.sum(e, axis=0, keepdims=True)
-            dp = dot_nt(v_ref[:kn, :], d_ref[q0:kn, :])
             rd = jnp.sum(e * dp, axis=0, keepdims=True) / total
             lse = top + jnp.log2(total)
             own_ref[s, 0:1, q0:kn] = lse
@@ -171,57 +218,66 @@
                 send_ref[s, 0:1, q0:kn] = lse
                 send_ref[s, 1:2, q0:kn] = rd
 
-
-def plain_kernel(heads, rows, meta, q_ref, k_ref, v_ref, d_ref, dq_ref, dk_ref, dv_ref, ak_ref, av_ref):
-    s = pl.program_id(0)
-
-    @pl.when(s >= meta[heads])
-    def _():
-        for q0, w in query_blocks(rows):
+        staggered(query_blocks(rows), front, back)
+        return c
+
+    lax.fori_loop(0, meta[heads], step, 0)
+
+
+def plain_kernel(
+    heads, rows, meta, q_ref, k_ref, v_ref, d_ref, dq_ref, dk_ref, dv_ref,
+    oq_ref, ok_ref, ov_ref, ak_ref, av_ref, sem,
+):
+    def copies(s):
+        return [
+            pltpu.make_async_copy(stage.at[s % 2], out.at[:, column(meta, s)], sem.at[s % 2, i])
+            for i, (stage, out) in enumerate(((oq_ref, dq_ref), (ok_ref, dk_ref), (ov_ref, dv_ref)))
+        ]
+
+    def compute(s):
+        col = column(meta, s)
+
+        def front(q0, w):
             kn = q0 + w
-            qb, db = q_ref[q0:kn, :], d_ref[q0:kn, :]
-            parts = ([(0, q0, False)] if q0 else []) + [(q0, w, True)]
-            scores = []
-            for k0, n, diagonal in parts:
-                sc = dot_nt(k_ref[k0 : k0 + n, :], qb) * LOG2_SCALE
-                if diagonal:
-                    key, query = iotas(k0, n, q0, w)
-                    sc = jnp.where(key <= query, sc, NEG)
-                scores.append(sc)
-            tops = [jnp.max(sc, axis=0, keepdims=True) for sc in scores]
-            top = functools.reduce(jnp.maximum, tops)
-            es = [jnp.exp2(sc - top) for sc in scores]
-            total = sum(jnp.sum(e, axis=0, keepdims=True) for e in es)
-            dps = [dot_nt(v_ref[k0 : k0 + n, :], db) for k0, n, _ in parts]
-            inv = 1.0 / total
-            rd = sum(jnp.sum(e * dp, axis=0, keepdims=True) for e, dp in zip(es, dps)) * inv
-            dq = None
-            for (k0, n, diagonal), e, dp in zip(parts, es, dps):
-                p = e * inv
-                ds = (p * (dp - rd)).astype(BF16)
-                gv = dot_nn(p.astype(BF16), db)
-                gk = dot_nn(ds, qb)
-                gq = dot_tn(ds, k_ref[k0 : k0 + n, :])
-                dq = gq if dq is None else dq + gq
-                if diagonal:
-                    av_ref[k0 : k0 + n, :] = gv
-                    ak_ref[k0 : k0 + n, :] = gk
-                else:
-                    av_ref[k0 : k0 + n, :] += gv
-                    ak_ref[k0 : k0 + n, :] += gk
-            dq_ref[q0:kn, :] = (dq * SCALE).astype(BF16)
-        dk_ref[...] = (ak_ref[...] * SCALE).astype(BF16)
-        dv_ref[...] = av_ref[...].astype(BF16)
-
-
-def cross_kernel(heads, rows, first, split, later, meta, *refs):
+            sc = dot_nt(k_ref[:kn, col], q_ref[q0:kn, col]) * LOG2_SCALE
+            sc = masked(sc, q0, w, NEG)
+            dp = dot_nt(v_ref[:kn, col], d_ref[q0:kn, col])
+            top = jnp.max(sc, axis=0, keepdims=True)
+            e = jnp.exp2(sc - top)
+            inv = 1.0 / jnp.sum(e, axis=0, keepdims=True)
+            rd = jnp.sum(e * dp, axis=0, keepdims=True) * inv
+            p = e * inv
+            return p.astype(BF16), (p * (dp - rd)).astype(BF16)
+
+        def back(q0, w, held):
+            accumulate(q0, w, held, col)
+
+        def accumulate(q0, w, held, col):
+            p, ds = held
+            kn = q0 + w
+            gv = dot_nn(p, d_ref[q0:kn, col])
+            gk = dot_nn(ds, q_ref[q0:kn, col])
+            oq_ref[s % 2, q0:kn, :] = (dot_tn(ds, k_ref[:kn, col]) * SCALE).astype(BF16)
+            if q0:
+                av_ref[:q0, :] += gv[:q0]
+                ak_ref[:q0, :] += gk[:q0]
+            av_ref[q0:kn, :] = gv[q0:]
+            ak_ref[q0:kn, :] = gk[q0:]
+
+        staggered(query_blocks(rows), front, back)
+        ok_ref[s % 2] = (ak_ref[...] * SCALE).astype(BF16)
+        ov_ref[s % 2] = av_ref[...].astype(BF16)
+
+    written_out(meta[heads], heads, copies, compute)
+
+
+def cross_kernel(heads, rows, first, reach, split, later, meta, *refs):
     if later:
         (k_ref, v_ref, one_ref, two_ref, st_ref, back0_ref, tot0_ref, gk0_ref, gv0_ref,
          back_ref, tot_ref, gk_ref, gv_ref, buf_ref, acc_ref) = refs
     else:
         (k_ref, v_ref, one_ref, st_ref, _,
          back_ref, tot_ref, gk_ref, gv_ref, buf_ref, acc_ref) = refs
-    s = pl.program_id(0)
     count, off, slot = meta[heads], meta[heads + 1], meta[heads + 2]
     done = jnp.minimum(count, split // slot)
     low, high = (done, count) if later else (0, done)
@@ -235,7 +291,7 @@
 
         lax.fori_loop(0, (stop - start) // GRAIN, step, 0)
 
-    @pl.when((s == 0) & (low < high))
+    @pl.when(low < high)
     def _():
         filled = high * slot
         if later:
@@ -247,105 +303,133 @@
         tail = pl.multiple_of(filled, GRAIN)
         buf_ref[pl.ds(tail, BLOCK), :] = jnp.zeros((BLOCK, 2 * HDIM), BF16)
 
-    def block(j, k0):
-        q0 = pl.multiple_of(j * BLOCK, BLOCK)
-        start = pl.multiple_of(s * slot + q0, GRAIN)
-        qb = buf_ref[pl.ds(start, BLOCK), :HDIM]
-        db = buf_ref[pl.ds(start, BLOCK), HDIM:]
-        kb, vb = k_ref[k0:, :], v_ref[k0:, :]
-        key = k0 + lax.broadcasted_iota(jnp.int32, (rows - k0, BLOCK), 0)
-        query = q0 + lax.broadcasted_iota(jnp.int32, (1, BLOCK), 1)
-        inside = query < off
-        sc = dot_nt(kb, qb) * LOG2_SCALE
-        sc = jnp.where(key >= off, sc, NEG)
-        top = jnp.max(sc, axis=0, keepdims=True)
-        e = jnp.exp2(sc - top)
-        total = jnp.sum(e, axis=0, keepdims=True)
-        dp = dot_nt(vb, db)
-        rd = jnp.sum(e * dp, axis=0, keepdims=True) / total
-        lse = top + jnp.log2(total)
-        lse1 = jnp.where(inside, st_ref[s, 0:1, pl.ds(q0, BLOCK)], 0.0)
-        rd1 = jnp.where(inside, st_ref[s, 1:2, pl.ds(q0, BLOCK)], 0.0)
-        high = jnp.maximum(lse, lse1)
-        both = high + jnp.log2(jnp.exp2(lse - high) + jnp.exp2(lse1 - high))
-        rd = jnp.exp2(lse - both) * rd + jnp.exp2(lse1 - both) * rd1
-        tot_ref[s, 0:1, pl.ds(q0, BLOCK)] = both
-        tot_ref[s, 1:2, pl.ds(q0, BLOCK)] = rd
-        p = e * jnp.where(inside, jnp.exp2(top - both), 0.0)
-        ds = (p * (dp - rd)).astype(BF16)
-        gv_ref[s, k0 - first :, :] += dot_nn(p.astype(BF16), db)
-        gk_ref[s, k0 - first :, :] += dot_nn(ds, qb)
-        acc_ref[pl.ds(start, BLOCK), :] = (dot_tn(ds, kb) * SCALE).astype(BF16)
+    def one_head(s, k0, blocks):
+        col = column(meta, s)
+
+        def rows_of(q0):
+            return pl.ds(pl.multiple_of(s * slot + q0, GRAIN), BLOCK)
+
+        def front(q0):
+            qb, db = buf_ref[rows_of(q0), :HDIM], buf_ref[rows_of(q0), HDIM:]
+            lanes = slice(q0, q0 + BLOCK)
+            key = k0 + lax.broadcasted_iota(jnp.int32, (rows - k0, BLOCK), 0)
+            inside = q0 + lax.broadcasted_iota(jnp.int32, (1, BLOCK), 1) < off
+            sc = dot_nt(k_ref[k0:, col], qb) * LOG2_SCALE
+            sc = jnp.where(key >= off, sc, NEG)
+            dp = dot_nt(v_ref[k0:, col], db)
+            top = jnp.max(sc, axis=0, keepdims=True)
+            e = jnp.exp2(sc - top)
+            total = jnp.sum(e, axis=0, keepdims=True)
+            rd = jnp.sum(e * dp, axis=0, keepdims=True) / total
+            lse = top + jnp.log2(total)
+            lse1 = jnp.where(inside, st_ref[s, 0:1, lanes], 0.0)
+            rd1 = jnp.where(inside, st_ref[s, 1:2, lanes], 0.0)
+            most = jnp.maximum(lse, lse1)
+            both = most + jnp.log2(jnp.exp2(lse - most) + jnp.exp2(lse1 - most))
+            rd = jnp.exp2(lse - both) * rd + jnp.exp2(lse1 - both) * rd1
+            tot_ref[s, 0:1, lanes] = both
+            tot_ref[s, 1:2, lanes] = rd
+            p = e * jnp.where(inside, jnp.exp2(top - both), 0.0)
+            return p.astype(BF16), (p * (dp - rd)).astype(BF16)
+
+        def back(q0, held):
+            p, ds = held
+            qb, db = buf_ref[rows_of(q0), :HDIM], buf_ref[rows_of(q0), HDIM:]
+            gv, gk = dot_nn(p, db), dot_nn(ds, qb)
+            if q0:
+                gv_ref[s, k0 - first :, :] += gv
+                gk_ref[s, k0 - first :, :] += gk
+            else:
+                gv_ref[s, k0 - first :, :] = gv
+                gk_ref[s, k0 - first :, :] = gk
+                if k0 > first:
+                    gv_ref[s, : k0 - first, :] = jnp.zeros((k0 - first, HDIM), F32)
+                    gk_ref[s, : k0 - first, :] = jnp.zeros((k0 - first, HDIM), F32)
+            acc_ref[rows_of(q0), :] = (dot_tn(ds, k_ref[k0:, col]) * SCALE).astype(BF16)
+
+        staggered([(q0,) for q0 in range(0, blocks * BLOCK, BLOCK)], front, back)
 
     if later:
 
-        @pl.when(s < low)
-        def _():
+        def forward(s, c):
             tot_ref[s] = tot0_ref[s]
             gk_ref[s] = gk0_ref[s]
             gv_ref[s] = gv0_ref[s]
-
-    @pl.when((s >= low) & (s < high))
-    def _():
-        gv_ref[s] = jnp.zeros(gv_ref.shape[1:], F32)
-        gk_ref[s] = jnp.zeros(gk_ref.shape[1:], F32)
-        starts = (first, up(2 * first, GRAIN))
-        blocks = (off + BLOCK - 1) // BLOCK
-        for k0, mine in ((starts[0], off < starts[1]), (starts[1], off >= starts[1])):
-
-            @pl.when(mine)
-            def _(k0=k0):
-                def step(j, c):
-                    block(j, k0)
-                    return c
-
-                lax.fori_loop(0, blocks, step, 0)
-
-    @pl.when(s == pl.num_programs(0) - 1)
-    def _():
-        if later:
-            move(back_ref, back0_ref, 0, low * slot, 0)
-        move(back_ref, acc_ref, low * slot, high * slot, 0)
+            return c
+
+        lax.fori_loop(0, low, forward, 0)
+
+    def step(s, c):
+        for blocks in range(1, reach // BLOCK + 1):
+            below = (blocks - 1) * BLOCK
+
+            @pl.when((off > below) & (off <= below + BLOCK))
+            def _(blocks=blocks, below=below):
+                one_head(s, max(first, below), blocks)
+
+        return c
+
+    lax.fori_loop(low, high, step, 0)
+    if later:
+        move(back_ref, back0_ref, 0, low * slot, 0)
+    move(back_ref, acc_ref, low * slot, high * slot, 0)
 
 
 def local_kernel(
-    heads, rows, first, reach, meta, q_ref, k_ref, v_ref, d_ref, own_ref, tot_ref, gk_ref, gv_ref,
-    _dq, _dk, _dv, dq_ref, dk_ref, dv_ref, part_ref, ak_ref, av_ref,
+    heads, rows, first, reach, tallest, meta, q_ref, k_ref, v_ref, d_ref, own_ref, tot_ref, gk_ref, gv_ref,
+    _dq, _dk, _dv, dq_ref, dk_ref, dv_ref, part_ref, oq_ref, ok_ref, ov_ref, ak_ref, av_ref, sem,
 ):
-    s = pl.program_id(0)
-
-    @pl.when(s < meta[heads])
-    def _():
-        off = meta[heads + 1]
-        for q0, w in query_blocks(rows):
+    off = meta[heads + 1]
+
+    def copies(s):
+        col = column(meta, s)
+        return [
+            pltpu.make_async_copy(
+                oq_ref.at[s % 2], dq_ref.at[pl.ds(tallest, rows - tallest), col], sem.at[s % 2, 0]
+            ),
+            pltpu.make_async_copy(ok_ref.at[s % 2], dk_ref.at[:, col], sem.at[s % 2, 1]),
+            pltpu.make_async_copy(ov_ref.at[s % 2], dv_ref.at[:, col], sem.at[s % 2, 2]),
+        ]
+
+    def compute(s):
+        col = column(meta, s)
+
+        def front(q0, w):
             kn = q0 + w
-            key, query = iotas(0, kn, q0, w)
-            low = jnp.where(query >= off, off, 0)
-            lse = own_ref[s, 0:1, q0:kn]
-            rd = own_ref[s, 1:2, q0:kn]
+            query = q0 + lax.broadcasted_iota(jnp.int32, (1, w), 1)
+            lse, rd = own_ref[s, 0:1, q0:kn], own_ref[s, 1:2, q0:kn]
             if q0 < reach:
                 lse = jnp.where(query < off, tot_ref[s, 0:1, q0:kn], lse)
                 rd = jnp.where(query < off, tot_ref[s, 1:2, q0:kn], rd)
-            qb, db = q_ref[q0:kn, :], d_ref[q0:kn, :]
-            sc = dot_nt(k_ref[:kn, :], qb) * LOG2_SCALE
-            p = jnp.where((key <= query) & (key >= low), jnp.exp2(sc - lse), 0.0)
-            dp = dot_nt(v_ref[:kn, :], db)
-            ds = (p * (dp - rd)).astype(BF16)
-            gv = dot_nn(p.astype(BF16), db)
-            gk = dot_nn(ds, qb)
-            dq = dot_tn(ds, k_ref[:kn, :]) * SCALE
-            dq_ref[q0:kn, :] = dq.astype(BF16)
+            sc = dot_nt(k_ref[:kn, col], q_ref[q0:kn, col]) * LOG2_SCALE
+            p = masked(jnp.exp2(sc - lse), q0, w, 0.0, jnp.where(query >= off, off, 0))
+            dp = dot_nt(v_ref[:kn, col], d_ref[q0:kn, col])
+            return p.astype(BF16), (p * (dp - rd)).astype(BF16)
+
+        def back(q0, w, held):
+            p, ds = held
+            kn = q0 + w
+            gv = dot_nn(p, d_ref[q0:kn, col])
+            gk = dot_nn(ds, q_ref[q0:kn, col])
+            dq = dot_tn(ds, k_ref[:kn, col]) * SCALE
             if q0 < reach:
                 part_ref[s, q0:kn, :] = dq
+            at = max(q0, tallest)
+            if at < kn:
+                oq_ref[s % 2, at - tallest : kn - tallest, :] = dq[at - q0 :].astype(BF16)
             if q0:
                 av_ref[:q0, :] += gv[:q0]
                 ak_ref[:q0, :] += gk[:q0]
             av_ref[q0:kn, :] = gv[q0:]
             ak_ref[q0:kn, :] = gk[q0:]
-        dk_ref[:first, :] = (ak_ref[:first, :] * SCALE).astype(BF16)
-        dv_ref[:first, :] = av_ref[:first, :].astype(BF16)
-        dk_ref[first:, :] = ((ak_ref[first:, :] + gk_ref[s]) * SCALE).astype(BF16)
-        dv_ref[first:, :] = (av_ref[first:, :] + gv_ref[s]).astype(BF16)
+
+        staggered(query_blocks(rows), front, back)
+        ok_ref[s % 2, :first, :] = (ak_ref[:first, :] * SCALE).astype(BF16)
+        ov_ref[s % 2, :first, :] = av_ref[:first, :].astype(BF16)
+        ok_ref[s % 2, first:, :] = ((ak_ref[first:, :] + gk_ref[s]) * SCALE).astype(BF16)
+        ov_ref[s % 2, first:, :] = (av_ref[first:, :] + gv_ref[s]).astype(BF16)
+
+    written_out(0, meta[heads], copies, compute)
 
 
 def add_kernel(heads, tallest, meta, part_ref, got_ref, _dq, dq_ref, stage_ref, sem):
@@ -414,28 +498,25 @@
         name="meta",
     )(shift, head_order)
 
-    at = shifted_at(heads)
     whole = jax.ShapeDtypeStruct((rows, width), BF16)
-    head_spec = pl.BlockSpec((rows, HDIM), lambda s, m: (0, at(s, m)))
-    plain_at = lambda s, m: m[jnp.minimum(jnp.maximum(s, m[heads]), heads - 1)]
-    plain_spec = pl.BlockSpec((rows, HDIM), lambda s, m: (0, plain_at(s, m)))
     any_spec = pl.BlockSpec(memory_space=pl.ANY)
     vmem = pl.BlockSpec(memory_space=pltpu.VMEM)
     smem = pl.BlockSpec(memory_space=pltpu.SMEM)
     tile = rows * HDIM * 2
     work = 2 * rows * rows * HDIM
 
+    def stages(top):
+        stage = [pltpu.VMEM((2, n, HDIM), BF16) for n in (rows - top, rows, rows)]
+        sums = [pltpu.VMEM((rows, HDIM), F32)] * 2
+        return stage + sums + [pltpu.SemaphoreType.DMA((2, 3))]
+
     def call(kernel, in_specs, out_specs, out_shape, estimate, limit, scratch=(), aliases={}):
         return pl.pallas_call(
             kernel,
             out_shape=out_shape,
-            grid_spec=pltpu.PrefetchScalarGridSpec(
-                num_scalar_prefetch=1,
-                grid=(heads,),
-                in_specs=in_specs,
-                out_specs=out_specs,
-                scratch_shapes=list(scratch),
-            ),
+            in_specs=[smem] + in_specs,
+            out_specs=out_specs,
+            scratch_shapes=list(scratch),
             input_output_aliases=aliases,
             cost_estimate=estimate,
             compiler_params=params(limit),
@@ -444,12 +525,12 @@
     def plain(meta, queries, keys, values, d_out):
         return call(
             functools.partial(plain_kernel, heads, rows),
-            [plain_spec] * 4,
-            [plain_spec] * 3,
+            [vmem] * 4,
+            [any_spec] * 3,
             [whole] * 3,
             cost(heads / 2 * 4 * work, heads / 2 * 7 * tile),
             16,
-            [pltpu.VMEM((rows, HDIM), F32)] * 2,
+            stages(0),
         )(meta, queries, keys, values, d_out)
 
     def branch(cap):
@@ -475,7 +556,7 @@
             one_got = lax.ppermute(one, "seq", back)
             st_send, st_own = call(
                 functools.partial(stats_kernel, heads, rows, reach),
-                [head_spec] * 4,
+                [vmem] * 4,
                 [vmem, vmem],
                 [
                     jax.ShapeDtypeStruct((heads, 2, reach), F32),
@@ -490,16 +571,9 @@
             side = jax.ShapeDtypeStruct((heads, rows - first, HDIM), F32)
 
             def cross(later, size, *args):
-                def block_of(s, m):
-                    done = jnp.minimum(m[heads], split // m[heads + 2])
-                    low, high = (done, m[heads]) if later else (0, done)
-                    s = jnp.maximum(jnp.minimum(s, high - 1), low)
-                    return (0, m[jnp.minimum(s, heads - 1)])
-
-                mine = pl.BlockSpec((rows, HDIM), block_of)
                 return call(
-                    functools.partial(cross_kernel, heads, rows, first, split, later),
-                    [mine] * 2 + ([vmem] * 7 if later else [vmem, vmem, any_spec]),
+                    functools.partial(cross_kernel, heads, rows, first, reach, split, later),
+                    [vmem] * 9 if later else [vmem] * 4 + [any_spec],
                     [vmem] * 4,
                     [
                         jax.ShapeDtypeStruct((size, HDIM), BF16),
@@ -520,15 +594,13 @@
             tot_got = lax.ppermute(tot, "seq", ahead)
             dq_got = lax.ppermute(back_q, "seq", ahead)
             dq, dk, dv, part = call(
-                functools.partial(local_kernel, heads, rows, first, reach),
-                [head_spec] * 4
-                + [vmem] * 4
-                + [any_spec] * 3,
-                [head_spec] * 3 + [vmem],
+                functools.partial(local_kernel, heads, rows, first, reach, tallest),
+                [vmem] * 8 + [any_spec] * 3,
+                [any_spec] * 3 + [vmem],
                 [whole] * 3 + [jax.ShapeDtypeStruct((heads, reach, HDIM), F32)],
                 cost(heads / 2 * 4 * work, heads / 2 * 9 * tile),
                 24,
-                [pltpu.VMEM((rows, HDIM), F32)] * 2,
+                stages(tallest),
                 {9: 0, 10: 1, 11: 2},
             )(meta, queries, keys, values, d_out, st_own, tot_got, gk, gv, dq, dk, dv)
             dq = pl.pallas_call(

time: 71.5 us -> 62.2 us (0.87)
  Pallas kernels: 40.6 us -> 30.3 us
  waiting for transfers between devices: 14.2 us -> 17.6 us
  loops' own time: 5.32 us -> 3.29 us
    pallas_call x5, Pallas kernels: 34.7 us -> 24.4 us  [the longest x2 7.31 us: cross(): call(functools.partial(cross_kernel, heads, rows, first, reach, split, la...]
    ppermute x1, waiting for transfers between devices: 4.49 us -> 7.91 us  [steps(): st_got = lax.ppermute(st_send, 'seq', back)]
    another operation x1, loops' own time: 5.32 us -> 3.29 us  [shards(): lax.switch(meta[heads + 3], [plain] + [branch(cap) for cap in caps], meta...]
  transfers between devices with their start and end apart: 5 -> 5, of which waited for: 2 -> 2; matrix products, arithmetic and copies ran while one was open for 0% -> 0% of each run, Pallas kernels for 44% -> 36%
where the time goes in v3:
time: 62.2 us; the launch traced here: 62.1 us
  Pallas kernels  30.3 us (49%)
  waiting for transfers between devices  17.6 us (28%)
  starting transfers between devices  8.17 us (13%)
  loops' own time  3.29 us (5%)
  between operations  2.12 us (3%)
    ppermute x1, waiting for transfers between devices, steps(): tot_got = lax.ppermute(tot, 'seq', ahead)  9.67 us
    ppermute x1, waiting for transfers between devices, steps(): st_got = lax.ppermute(st_send, 'seq', back)  7.91 us
    pallas_call x2, Pallas kernels, cross(): call(functools.partial(cross_kernel, heads, rows, first, reach, split, la...  7.31 us
    pallas_call x1, Pallas kernels, steps(): call(functools.partial(local_kernel, heads, rows, first, reach, tallest),...  6.67 us
    pallas_call x1, Pallas kernels, steps(): call(functools.partial(stats_kernel, heads, rows, reach), [vmem] * 4, [vm...  5.37 us
    ppermute x1, starting transfers between devices, steps(): one_got = lax.ppermute(one, 'seq', back)  5.13 us
    pallas_call x1, Pallas kernels, plain(): call(functools.partial(plain_kernel, heads, rows), [vmem] * 4, [any_spec]...  5.08 us
    another operation x1, loops' own time, shards(): lax.switch(meta[heads + 3], [plain] + [branch(cap) for cap in caps], meta...  3.29 us
  transfers between devices with their start and end apart: 5, of which 2 were waited for; matrix products, arithmetic and copies ran while one was open for 0% of the time, Pallas kernels for 36%

profile of v3, /device:TPU:0, one launch (start us, length us, event | category | flops | bytes accessed | tf_op | source)
XLA Modules:
  0.0 62.1 jit_solution(1032590591290930465)
XLA Ops:
  1.3 1.3 %meta.1 = s32[12]{0:T(128)S(1)} custom-call(s32[1]{0:T(128)S(6)} %copy.91.shift_ref, s32[32]{0:T(128)} %order_ref.1), custom_call_target="tpu_custom_call" | custom-call | tf_op jit(solution)/shard_map/meta/pallas_call | solution.py:492
  2.6 0.6 slice.3
  3.8 58.1 %conditional.1 = ((bf16[640,1024]{1,0:T(8,128)(2,1)}, bf16[640,1024]{1,0:T(8,128)(2,1)}, bf16[640,1024]{1,0:T(8,128)(2,1)})) conditional(s32[]{:T(128)} %bitcast, (s32[12]{0:T(128)S(1)}, bf16[640,1024]{1,0:T(8,128)(2,1)}, bf16[640,1024]{1,0:T(8,128)(2,1)}, bf16[640,1024]{1,0:T(8,128)(2,1)}, ...), branch_computations={%region_0.0_spmd, %region_1.0_spmd, %region_2.0_spmd, %region_3.0_... | conditional | flops 6291456000 | bytes 55968088 | solution.py:625
  3.9 0.0 copy-start.1
  3.9 0.0 copy-start.5
  3.9 2.6 %pack.5 = (bf16[1216,256]{1,0:T(8,128)(2,1)S(1)}, bf16[800,256]{1,0:T(8,128)(2,1)S(1)}) custom-call(s32[12]{0:T(128)S(1)} %get-tuple-element.79.meta, bf16[640,1024]{1,0:T(8,128)(2,1)} %get-tuple-element.182.q_ref, bf16[640,1024]{1,0:T(8,128)(2,1)} %get-tuple-element.197.d_ref), custom_call_target="tpu_custom_call" | custom-call | bytes 2064384 | tf_op jit(solution)/shard_map/cond/branch_2_fun/pack/pallas_call | solution.py:543
  6.5 5.1 %collective-permute-start.5 = (bf16[1216,256]{1,0:T(8,128)(2,1)S(1)}, bf16[1216,256]{1,0:T(8,128)(2,1)S(1)}, u32[]{:S(2)}, u32[]{:S(2)}) collective-permute-start(bf16[1216,256]{1,0:T(8,128)(2,1)S(1)} %get-tuple-element.85), channel_id=1, source_target_pairs={{0,12},{4,0},{8,4},{12,8},{1,13},{5,1},{9,5},{13,9},{2,14},{6,2},{... | collective-permute-start | bytes 1867784 | tf_op jit(solution)/shard_map/cond/branch_2_fun/ppermute | solution.py:556
  11.7 0.4 collective-permute-start.6
  12.1 0.0 copy-done.1
  12.1 0.0 copy-done.5
  12.1 0.0 copy-start.9
  12.1 0.0 copy-start.13
  12.1 5.4 %branch_2_fun.5 = (f32[8,2,512]{2,1,0:T(2,128)S(1)}, f32[8,2,640]{2,1,0:T(2,128)S(1)}) custom-call(s32[12]{0:T(128)S(1)} %get-tuple-element.79.meta, bf16[640,1024]{1,0:T(8,128)(2,1)} %get-tuple-element.182.q_ref, bf16[640,1024]{1,0:T(8,128)(2,1)S(1)} %copy-done.1, bf16[640,1024]{1,0:T(8,128)(2,1)S(1)} %copy-done.5, bf16[640,1024]{1,0:T(8,128)(2,1)} %get-tuple-element.197.d_ref), custom_call_target="tpu_custom_call" | custom-call | flops 838860800 | bytes 2621440 | tf_op jit(solution)/shard_map/cond/branch_2_fun/pallas_call | solution.py:557
  17.5 0.5 collective-permute-start.7
  18.0 0.0 copy-done.9
  18.0 0.0 copy-done.13
  18.0 5.1 %branch_2_fun.6 = (bf16[640,1024]{1,0:T(8,128)(2,1)}, bf16[640,1024]{1,0:T(8,128)(2,1)}, bf16[640,1024]{1,0:T(8,128)(2,1)}) custom-call(s32[12]{0:T(128)S(1)} %get-tuple-element.79.meta, bf16[640,1024]{1,0:T(8,128)(2,1)S(1)} %copy-done.9, bf16[640,1024]{1,0:T(8,128)(2,1)S(1)} %copy-done.1, bf16[640,1024]{1,0:T(8,128)(2,1)S(1)} %copy-done.5, ...), custom_call_target="tpu_custom_call" | custom-call | flops 1677721600 | bytes 4587520 | tf_op jit(solution)/shard_map/cond/branch_2_fun/pallas_call | solution.py:526
  23.1 7.9 %collective-permute-done.7.refs_3_.refs_4_ = f32[8,2,512]{2,1,0:T(2,128)S(1)} collective-permute-done((f32[8,2,512]{2,1,0:T(2,128)S(1)}, f32[8,2,512]{2,1,0:T(2,128)S(1)}, u32[]{:S(2)}, u32[]{:S(2)}) %collective-permute-start.7) | collective-permute-done | bytes 32800 | tf_op jit(solution)/shard_map/cond/branch_2_fun/ppermute | solution.py:568
  31.0 0.0 collective-permute-done.5.refs_2_
  31.0 5.2 %branch_2_fun.7 = (bf16[1216,128]{1,0:T(8,128)(2,1)S(1)}, f32[8,2,512]{2,1,0:T(2,128)S(1)}, f32[8,480,128]{2,1,0:T(8,128)S(1)}, f32[8,480,128]{2,1,0:T(8,128)S(1)}) custom-call(s32[12]{0:T(128)S(1)} %get-tuple-element.79.meta, bf16[640,1024]{1,0:T(8,128)(2,1)S(1)} %copy-done.1, bf16[640,1024]{1,0:T(8,128)(2,1)S(1)} %copy-done.5, ...), custom_call_target="tpu_custom_call" | custom-call | flops 1048576000 | bytes 1966080 | tf_op jit(solution)/shard_map/cond/branch_2_fun/pallas_call | solution.py:574
  36.2 0.0 collective-permute-done.6.refs_3_
  36.3 2.1 %branch_2_fun.8 = (bf16[2016,128]{1,0:T(8,128)(2,1)S(1)}, f32[8,2,512]{2,1,0:T(2,128)S(1)}, f32[8,480,128]{2,1,0:T(8,128)S(1)}, f32[8,480,128]{2,1,0:T(8,128)S(1)}) custom-call(s32[12]{0:T(128)S(1)} %get-tuple-element.79.meta, bf16[640,1024]{1,0:T(8,128)(2,1)S(1)} %copy-done.1, bf16[640,1024]{1,0:T(8,128)(2,1)S(1)} %copy-done.5, ...), custom_call_target="tpu_custom_call" | custom-call | flops 1048576000 | bytes 1966080 | tf_op jit(solution)/shard_map/cond/branch_2_fun/pallas_call | solution.py:574
  38.3 0.5 collective-permute-start.9
  38.8 1.6 %collective-permute-start.8 = (f32[8,2,512]{2,1,0:T(2,128)S(1)}, f32[8,2,512]{2,1,0:T(2,128)S(1)}, u32[]{:S(2)}, u32[]{:S(2)}) collective-permute-start(f32[8,2,512]{2,1,0:T(2,128)S(1)} %get-tuple-element.93), channel_id=1, source_target_pairs={{0,4},{4,8},{8,12},{12,0},{1,5},{5,9},{9,13},{13,1},{2,6},{6,10},{... | collective-permute-start | bytes 98312 | tf_op jit(solution)/shard_map/cond/branch_2_fun/ppermute | solution.py:594
  40.4 9.7 %collective-permute-done.8.tot_ref = f32[8,2,512]{2,1,0:T(2,128)S(1)} collective-permute-done((f32[8,2,512]{2,1,0:T(2,128)S(1)}, f32[8,2,512]{2,1,0:T(2,128)S(1)}, u32[]{:S(2)}, u32[]{:S(2)}) %collective-permute-start.8) | collective-permute-done | bytes 32800 | tf_op jit(solution)/shard_map/cond/branch_2_fun/ppermute | solution.py:594
  50.1 6.7 %branch_2_fun.9 = (bf16[640,1024]{1,0:T(8,128)(2,1)}, bf16[640,1024]{1,0:T(8,128)(2,1)}, bf16[640,1024]{1,0:T(8,128)(2,1)}, f32[8,512,128]{2,1,0:T(8,128)S(1)}) custom-call(s32[12]{0:T(128)S(1)} %get-tuple-element.79.meta, bf16[640,1024]{1,0:T(8,128)(2,1)S(1)} %copy-done.9, ...), custom_call_target="tpu_custom_call", output_to_operand_aliasing={{0}: (9, {}), {1}: (10, {}), {2}: (11, {})} | custom-call | flops 1677721600 | bytes 5898240 | tf_op jit(solution)/shard_map/cond/branch_2_fun/pallas_call | solution.py:596
  56.8 0.0 collective-permute-done.9.got_ref
  56.8 1.9 %add.5 = bf16[640,1024]{1,0:T(8,128)(2,1)} custom-call(s32[12]{0:T(128)S(1)} %get-tuple-element.79.meta, f32[8,512,128]{2,1,0:T(8,128)S(1)} %get-tuple-element.98.part_ref, bf16[2016,128]{1,0:T(8,128)(2,1)S(1)} %collective-permute-done.9.got_ref, bf16[640,1024]{1,0:T(8,128)(2,1)} %get-tuple-element.100._dq), custom_call_target="tpu_custom_call", output_to_operand_aliasing={{}: (3, {})} | custom-call | bytes 1966080 | tf_op jit(solution)/shard_map/cond/branch_2_fun/add/pallas_call | solution.py:606
Async XLA Ops:
  3.9 8.2 %copy-start.1 = (bf16[640,1024]{1,0:T(8,128)(2,1)S(1)}, bf16[640,1024]{1,0:T(8,128)(2,1)}, u32[]{:S(2)}) copy-start(bf16[640,1024]{1,0:T(8,128)(2,1)} %get-tuple-element.187.k_ref.refs_0_) | copy-start | bytes 3932164 | tf_op jit(solution)/shard_map/cond
  3.9 8.2 %copy-start.5 = (bf16[640,1024]{1,0:T(8,128)(2,1)S(1)}, bf16[640,1024]{1,0:T(8,128)(2,1)}, u32[]{:S(2)}) copy-start(bf16[640,1024]{1,0:T(8,128)(2,1)} %get-tuple-element.192.v_ref.refs_1_) | copy-start | bytes 3932164 | tf_op jit(solution)/shard_map/cond
  6.5 24.5 %collective-permute-start.5 = (bf16[1216,256]{1,0:T(8,128)(2,1)S(1)}, bf16[1216,256]{1,0:T(8,128)(2,1)S(1)}, u32[]{:S(2)}, u32[]{:S(2)}) collective-permute-start(bf16[1216,256]{1,0:T(8,128)(2,1)S(1)} %get-tuple-element.85), channel_id=1, source_target_pairs={{0,12},{4,0},{8,4},{12,8},{1,13},{5,1},{9,5},{13,9},{2,14},{6,2},{... | collective-permute-start | bytes 1867784 | tf_op jit(solution)/shard_map/cond/branch_2_fun/ppermute | solution.py:556
  11.7 24.6 %collective-permute-start.6 = (bf16[800,256]{1,0:T(8,128)(2,1)S(1)}, bf16[800,256]{1,0:T(8,128)(2,1)S(1)}, u32[]{:S(2)}, u32[]{:S(2)}) collective-permute-start(bf16[800,256]{1,0:T(8,128)(2,1)S(1)} %get-tuple-element.86), channel_id=1, source_target_pairs={{0,12},{4,0},{8,4},{12,8},{1,13},{5,1},{9,5},{13,9},{2,14},{6,2},{... | collective-permute-start | bytes 1228808 | tf_op jit(solution)/shard_map/cond/branch_2_fun/ppermute | solution.py:569
  12.1 5.9 %copy-start.9 = (bf16[640,1024]{1,0:T(8,128)(2,1)S(1)}, bf16[640,1024]{1,0:T(8,128)(2,1)}, u32[]{:S(2)}) copy-start(bf16[640,1024]{1,0:T(8,128)(2,1)} %get-tuple-element.182.q_ref) | copy-start | bytes 3932164 | tf_op jit(solution)/shard_map/cond
  12.1 5.9 %copy-start.13 = (bf16[640,1024]{1,0:T(8,128)(2,1)S(1)}, bf16[640,1024]{1,0:T(8,128)(2,1)}, u32[]{:S(2)}) copy-start(bf16[640,1024]{1,0:T(8,128)(2,1)} %get-tuple-element.197.d_ref) | copy-start | bytes 3932164 | tf_op jit(solution)/shard_map/cond
  17.5 13.5 %collective-permute-start.7 = (f32[8,2,512]{2,1,0:T(2,128)S(1)}, f32[8,2,512]{2,1,0:T(2,128)S(1)}, u32[]{:S(2)}, u32[]{:S(2)}) collective-permute-start(f32[8,2,512]{2,1,0:T(2,128)S(1)} %get-tuple-element.87), channel_id=1, source_target_pairs={{0,12},{4,0},{8,4},{12,8},{1,13},{5,1},{9,5},{13,9},{2,14},{6,2},{... | collective-permute-start | bytes 98312 | tf_op jit(solution)/shard_map/cond/branch_2_fun/ppermute | solution.py:568
  38.3 18.4 %collective-permute-start.9 = (bf16[2016,128]{1,0:T(8,128)(2,1)S(1)}, bf16[2016,128]{1,0:T(8,128)(2,1)S(1)}, u32[]{:S(2)}, u32[]{:S(2)}) collective-permute-start(bf16[2016,128]{1,0:T(8,128)(2,1)S(1)} %get-tuple-element.99), channel_id=1, source_target_pairs={{0,4},{4,8},{8,12},{12,0},{1,5},{5,9},{9,13},{13,1},{2,6},{6,10},{... | collective-permute-start | bytes 1548296 | tf_op jit(solution)/shard_map/cond/branch_2_fun/ppermute | solution.py:595
  38.8 11.2 %collective-permute-start.8 = (f32[8,2,512]{2,1,0:T(2,128)S(1)}, f32[8,2,512]{2,1,0:T(2,128)S(1)}, u32[]{:S(2)}, u32[]{:S(2)}) collective-permute-start(f32[8,2,512]{2,1,0:T(2,128)S(1)} %get-tuple-element.93), channel_id=1, source_target_pairs={{0,4},{4,8},{8,12},{12,0},{1,5},{5,9},{9,13},{13,1},{2,6},{6,10},{... | collective-permute-start | bytes 98312 | tf_op jit(solution)/shard_map/cond/branch_2_fun/ppermute | solution.py:594

commit v4 on v3

v4 whole, which is shorter than its diff:
```python
import functools
import math

import jax
import jax.numpy as jnp
from jax import lax
from jax.experimental import pallas as pl
from jax.experimental.pallas import tpu as pltpu
from jax.sharding import PartitionSpec as P


HEADS = 32
HDIM = 128
SCALE = HDIM ** (-0.5)
LOG2_SCALE = SCALE * math.log2(math.e)
NEG = -1e30
GRAIN = 32
BLOCK = 256
PART = 0.6
FRACTIONS = ((0.525, 0.675, 1.0), (0.45, 0.6375, 1.0))
F32 = jnp.float32
BF16 = jnp.bfloat16


def up(x, m):
    return (x + m - 1) // m * m


def dot_nt(a, b):
    return lax.dot_general(a, b, (((1,), (1,)), ((), ())), preferred_element_type=F32)


def dot_nn(a, b):
    return lax.dot_general(a, b, (((1,), (0,)), ((), ())), preferred_element_type=F32)


def dot_tn(a, b):
    return lax.dot_general(a, b, (((0,), (0,)), ((), ())), preferred_element_type=F32)


def query_blocks(rows):
    return [(q0, min(BLOCK, rows - q0)) for q0 in range(0, rows, BLOCK)]


def mask_of(q0, w, diagonal, low=None):
    k0, kn = (q0, w) if diagonal else (0, q0)
    key = k0 + lax.broadcasted_iota(jnp.int32, (kn, w), 0)
    query = q0 + lax.broadcasted_iota(jnp.int32, (1, w), 1)
    if low is None:
        return key <= query
    return (key >= low) & (key <= query) if diagonal else key >= low


def masked(x, q0, w, other, low=None):
    below = jnp.where(mask_of(q0, w, True, low), x[q0:], other)
    if not q0:
        return below
    above = x[:q0] if low is None else jnp.where(mask_of(q0, w, False, low), x[:q0], other)
    return jnp.concatenate([above, below], axis=0)


def staggered(blocks, front, back):
    held = None
    for block in blocks:
        fresh = front(*block)
        if held is not None:
            back(*held)
        held = (*block, fresh)
    back(*held)


def column(meta, s):
    return pl.ds(pl.multiple_of(meta[s] * HDIM, HDIM), HDIM)


def written_out(start, stop, copies, compute):
    def finish(s):
        for copy in copies(s):
            copy.wait()

    def step(s, c):
        @pl.when(s >= start + 2)
        def _():
            finish(s - 2)

        compute(s)
        for copy in copies(s):
            copy.start()
        return c

    lax.fori_loop(start, stop, step, 0)
    for back in (2, 1):

        @pl.when(stop - back >= start)
        def _(back=back):
            finish(stop - back)


def meta_kernel(heads, rows, caps, shift_ref, order_ref, out_ref, flag_ref):
    base = lax.axis_index("head") * heads
    for h in range(heads):
        flag_ref[h] = 0
    for i in range(HEADS // 2):
        loc = order_ref[i] - base

        @pl.when((loc >= 0) & (loc < heads))
        def _():
            flag_ref[loc] = 1

    count = flag_ref[0]
    for h in range(1, heads):
        count = count + flag_ref[h]
    yes, no = jnp.int32(0), count
    for h in range(heads):
        flag = flag_ref[h]
        out_ref[jnp.where(flag > 0, yes, no)] = h
        yes, no = yes + flag, no + 1 - flag
    off = shift_ref[0]
    late = jnp.where(2 * off > rows, 1, 0)
    far = (off + GRAIN - 1) // GRAIN * GRAIN
    near = rows - off // GRAIN * GRAIN
    slot = jnp.where(late > 0, near, far)
    early, tail = jnp.int32(1), jnp.int32(1 + len(caps[0]))
    for cap in caps[0][:-1]:
        early = early + jnp.where(count * slot > cap, 1, 0)
    for cap in caps[1][:-1]:
        tail = tail + jnp.where(count * slot > cap, 1, 0)
    pick = jnp.where(count > 0, jnp.where(late > 0, tail, early), 0)
    out_ref[heads] = count
    out_ref[heads + 1] = off
    out_ref[heads + 2] = slot
    out_ref[heads + 3] = pick


def pack_kernel(heads, rows, base, sizes, late, meta, a_ref, b_ref, one_ref, two_ref, sem, mid_ref):
    count, slot = meta[heads], meta[heads + 2]
    skip = rows - slot if late else 0
    split = one_ref.shape[0]

    def each(act):
        def step(s, c):
            column = pl.multiple_of(meta[s] * HDIM, HDIM)
            low = s * slot
            for ref, shift, mine in (
                (one_ref, low, low + slot <= split),
                (two_ref, low - split, low >= split),
                (mid_ref, 0, (low < split) & (low + slot > split)),
            ):

                def copy(at, size, i, ref=ref, shift=shift):
                    src = pl.multiple_of(skip + at, GRAIN)
                    dst = pl.multiple_of(shift + at, GRAIN)
                    for j, from_ref in enumerate((a_ref, b_ref)):
                        act(
                            pltpu.make_async_copy(
                                from_ref.at[pl.ds(src, size), pl.ds(column, HDIM)],
                                ref.at[pl.ds(dst, size), pl.ds(j * HDIM, HDIM)],
                                sem.at[s, j, i],
                            )
                        )

                @pl.when(mine)
                def _(copy=copy):
                    copy(0, base, 0)
                    at = jnp.int32(base)
                    for i, size in enumerate(sizes):
                        bit = ((slot - base) // size) % 2

                        @pl.when(bit == 1)
                        def _(at=at, size=size, i=i):
                            copy(at, size, i + 1)

                        at = at + bit * size

            return c

        lax.fori_loop(0, count, step, 0)

    each(lambda copy: copy.start())
    each(lambda copy: copy.wait())
    low = split // slot * slot
    cut = split - low

    @pl.when((low < count * slot) & (cut > 0))
    def _():
        def front(i, c):
            src = pl.multiple_of(i * GRAIN, GRAIN)
            dst = pl.multiple_of(low + i * GRAIN, GRAIN)
            one_ref[pl.ds(dst, GRAIN), :] = mid_ref[pl.ds(src, GRAIN), :]
            return c

        def rest(i, c):
            src = pl.multiple_of(cut + i * GRAIN, GRAIN)
            dst = pl.multiple_of(i * GRAIN, GRAIN)
            two_ref[pl.ds(dst, GRAIN), :] = mid_ref[pl.ds(src, GRAIN), :]
            return c

        lax.fori_loop(0, cut // GRAIN, front, 0)
        lax.fori_loop(0, (slot - cut) // GRAIN, rest, 0)


def stats_kernel(heads, rows, reach, meta, q_ref, k_ref, v_ref, d_ref, send_ref, own_ref):
    off = meta[heads + 1]

    def step(s, c):
        col = column(meta, s)

        def front(q0, w):
            kn = q0 + w
            sc = dot_nt(k_ref[:kn, col], q_ref[q0:kn, col]) * LOG2_SCALE
            return sc, dot_nt(v_ref[:kn, col], d_ref[q0:kn, col])

        def back(q0, w, held):
            sc, dp = held
            kn = q0 + w
            query = q0 + lax.broadcasted_iota(jnp.int32, (1, w), 1)
            sc = masked(sc, q0, w, NEG, jnp.where(query >= off, off, 0))
            top = jnp.max(sc, axis=0, keepdims=True)
            e = jnp.exp2(sc - top)
            total = jnp.sum(e, axis=0, keepdims=True)
            rd = jnp.sum(e * dp, axis=0, keepdims=True) / total
            lse = top + jnp.log2(total)
            own_ref[s, 0:1, q0:kn] = lse
            own_ref[s, 1:2, q0:kn] = rd
            if q0 < reach:
                send_ref[s, 0:1, q0:kn] = lse
                send_ref[s, 1:2, q0:kn] = rd

        staggered(query_blocks(rows), front, back)
        return c

    lax.fori_loop(0, meta[heads], step, 0)


def plain_kernel(
    heads, rows, meta, q_ref, k_ref, v_ref, d_ref, dq_ref, dk_ref, dv_ref,
    oq_ref, ok_ref, ov_ref, ak_ref, av_ref, sem,
):
    def copies(s):
        return [
            pltpu.make_async_copy(stage.at[s % 2], out.at[:, column(meta, s)], sem.at[s % 2, i])
            for i, (stage, out) in enumerate(((oq_ref, dq_ref), (ok_ref, dk_ref), (ov_ref, dv_ref)))
        ]

    def compute(s):
        col = column(meta, s)

        def front(q0, w):
            kn = q0 + w
            sc = dot_nt(k_ref[:kn, col], q_ref[q0:kn, col]) * LOG2_SCALE
            sc = masked(sc, q0, w, NEG)
            dp = dot_nt(v_ref[:kn, col], d_ref[q0:kn, col])
            top = jnp.max(sc, axis=0, keepdims=True)
            e = jnp.exp2(sc - top)
            inv = 1.0 / jnp.sum(e, axis=0, keepdims=True)
            rd = jnp.sum(e * dp, axis=0, keepdims=True) * inv
            p = e * inv
            return p.astype(BF16), (p * (dp - rd)).astype(BF16)

        def back(q0, w, held):
            accumulate(q0, w, held, col)

        def accumulate(q0, w, held, col):
            p, ds = held
            kn = q0 + w
            gv = dot_nn(p, d_ref[q0:kn, col])
            gk = dot_nn(ds, q_ref[q0:kn, col])
            oq_ref[s % 2, q0:kn, :] = (dot_tn(ds, k_ref[:kn, col]) * SCALE).astype(BF16)
            if q0:
                av_ref[:q0, :] += gv[:q0]
                ak_ref[:q0, :] += gk[:q0]
            av_ref[q0:kn, :] = gv[q0:]
            ak_ref[q0:kn, :] = gk[q0:]

        staggered(query_blocks(rows), front, back)
        ok_ref[s % 2] = (ak_ref[...] * SCALE).astype(BF16)
        ov_ref[s % 2] = av_ref[...].astype(BF16)

    written_out(meta[heads], heads, copies, compute)


def cross_kernel(heads, rows, first, half, reach, split, late, later, meta, *refs):
    refs = list(refs)
    a_ref, b_ref, one_ref = refs[:3]
    del refs[:3]
    two_ref = refs.pop(0) if later else None
    st_ref = refs.pop(0)
    passed = refs[: 3 if late else 4] if later else ()
    del refs[: len(passed) if later else 1]
    if late:
        back_ref, tot_ref, xq_ref, buf_ref, acc_ref, sum_ref = refs
        kept = ((tot_ref, 1), (xq_ref, 2))
    else:
        back_ref, tot_ref, gk_ref, gv_ref, buf_ref, acc_ref = refs
        kept = ((tot_ref, 1), (gk_ref, 2), (gv_ref, 3))
    count, off, slot = meta[heads], meta[heads + 1], meta[heads + 2]
    done = jnp.minimum(count, split // slot)
    low, high = (done, count) if later else (0, done)

    def move(dst_ref, src_ref, start, stop, shift):
        def step(i, c):
            dst = pl.multiple_of(start + i * GRAIN, GRAIN)
            src = pl.multiple_of(start - shift + i * GRAIN, GRAIN)
            dst_ref[pl.ds(dst, GRAIN), :] = src_ref[pl.ds(src, GRAIN), :]
            return c

        lax.fori_loop(0, (stop - start) // GRAIN, step, 0)

    @pl.when(low < high)
    def _():
        filled = high * slot
        if later:
            edge = jnp.minimum(filled, split)
            move(buf_ref, one_ref, low * slot, edge, 0)
            move(buf_ref, two_ref, edge, filled, split)
        else:
            move(buf_ref, one_ref, 0, filled, 0)
        tail = pl.multiple_of(filled, GRAIN)
        buf_ref[pl.ds(tail, BLOCK), :] = jnp.zeros((BLOCK, 2 * HDIM), BF16)

    def scores(s, lanes, inside, valid, kb, vb, qb, db):
        sc = jnp.where(valid, dot_nt(kb, qb) * LOG2_SCALE, NEG)
        dp = dot_nt(vb, db)
        top = jnp.max(sc, axis=0, keepdims=True)
        e = jnp.exp2(sc - top)
        total = jnp.sum(e, axis=0, keepdims=True)
        rd = jnp.sum(e * dp, axis=0, keepdims=True) / total
        lse = top + jnp.log2(total)
        lse1 = jnp.where(inside, st_ref[s, 0:1, lanes], 0.0)
        rd1 = jnp.where(inside, st_ref[s, 1:2, lanes], 0.0)
        most = jnp.maximum(lse, lse1)
        both = most + jnp.log2(jnp.exp2(lse - most) + jnp.exp2(lse1 - most))
        rd = jnp.exp2(lse - both) * rd + jnp.exp2(lse1 - both) * rd1
        tot_ref[s, 0:1, lanes] = both
        tot_ref[s, 1:2, lanes] = rd
        p = e * jnp.where(inside, jnp.exp2(top - both), 0.0)
        return p.astype(BF16), (p * (dp - rd)).astype(BF16)

    def keys_came(s, c):
        col = column(meta, s)
        mine = pl.ds(pl.multiple_of(s * slot, GRAIN), half)
        kb, vb = buf_ref[mine, :HDIM], buf_ref[mine, HDIM:]
        place = lax.broadcasted_iota(jnp.int32, (half, BLOCK), 0)
        valid = (place >= off - (rows - slot)) & (place < slot)

        def front(q0):
            lanes = slice(q0, q0 + BLOCK)
            inside = q0 + lax.broadcasted_iota(jnp.int32, (1, BLOCK), 1) < off
            return scores(s, lanes, inside, valid, kb, vb, a_ref[lanes, col], b_ref[lanes, col])

        def back(q0, held):
            p, ds = held
            lanes = slice(q0, q0 + BLOCK)
            gk, gv = dot_nn(ds, a_ref[lanes, col]), dot_nn(p, b_ref[lanes, col])
            if q0:
                gk, gv = sum_ref[0] + gk, sum_ref[1] + gv
            if q0 + BLOCK < reach:
                sum_ref[0], sum_ref[1] = gk, gv
            else:
                acc_ref[mine, :HDIM] = (gk * SCALE).astype(BF16)
                acc_ref[mine, HDIM:] = gv.astype(BF16)
            xq_ref[s, lanes, :] = dot_tn(ds, kb)

        staggered([(q0,) for q0 in range(0, reach, BLOCK)], front, back)
        return c

    def queries_came(s, c):
        col = column(meta, s)
        gk_ref[s] = jnp.zeros(gk_ref.shape[1:], F32)
        gv_ref[s] = jnp.zeros(gv_ref.shape[1:], F32)

        def block(j, c):
            q0 = pl.multiple_of(j * BLOCK, BLOCK)
            mine = pl.ds(pl.multiple_of(s * slot + q0, GRAIN), BLOCK)
            qb, db = buf_ref[mine, :HDIM], buf_ref[mine, HDIM:]
            kb = a_ref[first:, col]
            valid = first + lax.broadcasted_iota(jnp.int32, (rows - first, BLOCK), 0) >= off
            inside = q0 + lax.broadcasted_iota(jnp.int32, (1, BLOCK), 1) < off
            p, ds = scores(s, pl.ds(q0, BLOCK), inside, valid, kb, b_ref[first:, col], qb, db)
            gv_ref[s] += dot_nn(p, db)
            gk_ref[s] += dot_nn(ds, qb)
            acc_ref[mine, :] = (dot_tn(ds, kb) * SCALE).astype(BF16)
            return c

        lax.fori_loop(0, (off + BLOCK - 1) // BLOCK, block, 0)
        return c

    if later:

        def forward(s, c):
            for ref, i in kept:
                ref[s] = passed[i][s]
            return c

        lax.fori_loop(0, low, forward, 0)
    lax.fori_loop(low, high, keys_came if late else queries_came, 0)
    if later:
        move(back_ref, passed[0], 0, low * slot, 0)
    move(back_ref, acc_ref, low * slot, high * slot, 0)


def local_kernel(heads, rows, first, half, reach, late, meta, q_ref, k_ref, v_ref, d_ref, own_ref, tot_ref, *refs):
    refs = list(refs)
    if late:
        xq_ref = refs.pop(0)
    else:
        gk_ref, gv_ref = refs[:2]
        del refs[:2]
    del refs[:3]
    dq_ref, dk_ref, dv_ref = refs[:3]
    parts = refs[3 : 5 if late else 4]
    oq_ref, ok_ref, ov_ref, ak_ref, av_ref, sem = refs[5 if late else 4 :]
    off = meta[heads + 1]
    keys_out, query_out = (pl.ds(0, half), pl.ds(0, rows)) if late else (pl.ds(0, rows), pl.ds(half, rows - half))
    skip = 0 if late else half

    def copies(s):
        col = column(meta, s)
        return [
            pltpu.make_async_copy(stage.at[s % 2], out.at[span, col], sem.at[s % 2, i])
            for i, (stage, out, span) in enumerate(
                ((oq_ref, dq_ref, query_out), (ok_ref, dk_ref, keys_out), (ov_ref, dv_ref, keys_out))
            )
        ]

    def compute(s):
        col = column(meta, s)

        def front(q0, w):
            kn = q0 + w
            query = q0 + lax.broadcasted_iota(jnp.int32, (1, w), 1)
            lse, rd = own_ref[s, 0:1, q0:kn], own_ref[s, 1:2, q0:kn]
            if q0 < reach:
                lse = jnp.where(query < off, tot_ref[s, 0:1, q0:kn], lse)
                rd = jnp.where(query < off, tot_ref[s, 1:2, q0:kn], rd)
            sc = dot_nt(k_ref[:kn, col], q_ref[q0:kn, col]) * LOG2_SCALE
            p = masked(jnp.exp2(sc - lse), q0, w, 0.0, jnp.where(query >= off, off, 0))
            dp = dot_nt(v_ref[:kn, col], d_ref[q0:kn, col])
            return p.astype(BF16), (p * (dp - rd)).astype(BF16)

        def back(q0, w, held):
            p, ds = held
            kn = q0 + w
            gv = dot_nn(p, d_ref[q0:kn, col])
            gk = dot_nn(ds, q_ref[q0:kn, col])
            dq = dot_tn(ds, k_ref[:kn, col])
            if late and q0 < reach:
                dq = dq + xq_ref[s, q0:kn, :]
            dq = dq * SCALE
            if not late and q0 < half:
                parts[0][s, q0 : min(kn, half), :] = dq[: half - q0]
            at = max(q0, skip)
            if at < kn:
                oq_ref[s % 2, at - skip : kn - skip, :] = dq[at - q0 :].astype(BF16)
            if q0:
                av_ref[:q0, :] += gv[:q0]
                ak_ref[:q0, :] += gk[:q0]
            av_ref[q0:kn, :] = gv[q0:]
            ak_ref[q0:kn, :] = gk[q0:]

        staggered(query_blocks(rows), front, back)
        if late:
            ok_ref[s % 2] = (ak_ref[:half, :] * SCALE).astype(BF16)
            ov_ref[s % 2] = av_ref[:half, :].astype(BF16)
            parts[0][s] = ak_ref[half:, :] * SCALE
            parts[1][s] = av_ref[half:, :]
        else:
            ok_ref[s % 2, :first, :] = (ak_ref[:first, :] * SCALE).astype(BF16)
            ov_ref[s % 2, :first, :] = av_ref[:first, :].astype(BF16)
            ok_ref[s % 2, first:, :] = ((ak_ref[first:, :] + gk_ref[s]) * SCALE).astype(BF16)
            ov_ref[s % 2, first:, :] = (av_ref[first:, :] + gv_ref[s]).astype(BF16)

    written_out(0, meta[heads], copies, compute)


def add_kernel(heads, rows, half, late, meta, *refs):
    n = 2 if late else 1
    parts, got_ref, outs, stages, sem = refs[:n], refs[n], refs[2 * n + 1 : 3 * n + 1], refs[3 * n + 1 : 4 * n + 1], refs[-1]
    slot = meta[heads + 2]
    size = rows - half if late else half
    skip = size - slot if late else 0
    span = pl.ds(half if late else 0, size)

    def copies(s):
        col = column(meta, s)
        return [
            pltpu.make_async_copy(stage.at[s], out.at[span, col], sem.at[s, i])
            for i, (stage, out) in enumerate(zip(stages, outs))
        ]

    def send(s, c):
        def both(i, c):
            at = pl.ds(pl.multiple_of(skip + i * GRAIN, GRAIN), GRAIN)
            src = pl.ds(pl.multiple_of(s * slot + i * GRAIN, GRAIN), GRAIN)
            for j in range(n):
                there = got_ref[src, j * HDIM : (j + 1) * HDIM].astype(F32)
                stages[j][s, at, :] = (parts[j][s, at, :] + there).astype(BF16)
            return c

        def here(i, c):
            at = pl.ds(pl.multiple_of((0 if late else slot) + i * GRAIN, GRAIN), GRAIN)
            for j in range(n):
                stages[j][s, at, :] = parts[j][s, at, :].astype(BF16)
            return c

        lax.fori_loop(0, slot // GRAIN, both, 0)
        lax.fori_loop(0, (size - slot) // GRAIN, here, 0)
        for copy in copies(s):
            copy.start()
        return c

    def wait(s, c):
        for copy in copies(s):
            copy.wait()
        return c

    lax.fori_loop(0, meta[heads], send, 0)
    lax.fori_loop(0, meta[heads], wait, 0)


def cost(flops, moved):
    return pl.CostEstimate(flops=int(flops), bytes_accessed=int(moved), transcendentals=0)


def params(mebibytes):
    return pltpu.CompilerParams(vmem_limit_bytes=mebibytes * 2**20)


def shards(queries, keys, values, d_out, shift, head_order):
    rows, width = queries.shape
    heads = width // HDIM
    first, half = rows // 4, up(rows // 2, GRAIN)
    base = first // GRAIN * GRAIN
    reach = up(rows - first, BLOCK)
    most = heads * half
    caps = [[up(int(most * f), GRAIN) for f in group] for group in FRACTIONS]
    seq = lax.axis_size("seq")
    back = [(i, (i - 1) % seq) for i in range(seq)]
    ahead = [(i, (i + 1) % seq) for i in range(seq)]

    meta = pl.pallas_call(
        functools.partial(meta_kernel, heads, rows, caps),
        out_shape=jax.ShapeDtypeStruct((heads + 4,), jnp.int32),
        in_specs=[pl.BlockSpec(memory_space=pltpu.SMEM)] * 2,
        out_specs=pl.BlockSpec(memory_space=pltpu.SMEM),
        scratch_shapes=[pltpu.SMEM((heads,), jnp.int32)],
        name="meta",
    )(shift, head_order)

    whole = jax.ShapeDtypeStruct((rows, width), BF16)
    any_spec = pl.BlockSpec(memory_space=pl.ANY)
    vmem = pl.BlockSpec(memory_space=pltpu.VMEM)
    smem = pl.BlockSpec(memory_space=pltpu.SMEM)
    tile = rows * HDIM * 2
    work = 2 * rows * rows * HDIM

    def stages(*sizes):
        stage = [pltpu.VMEM((2, n, HDIM), BF16) for n in sizes]
        sums = [pltpu.VMEM((rows, HDIM), F32)] * 2
        return stage + sums + [pltpu.SemaphoreType.DMA((2, 3))]

    def call(kernel, in_specs, out_specs, out_shape, estimate, limit, scratch=(), aliases={}):
        return pl.pallas_call(
            kernel,
            out_shape=out_shape,
            in_specs=[smem] + in_specs,
            out_specs=out_specs,
            scratch_shapes=list(scratch),
            input_output_aliases=aliases,
            cost_estimate=estimate,
            compiler_params=params(limit),
        )

    def plain(meta, queries, keys, values, d_out):
        return call(
            functools.partial(plain_kernel, heads, rows),
            [vmem] * 4,
            [any_spec] * 3,
            [whole] * 3,
            cost(heads / 2 * 4 * work, heads / 2 * 7 * tile),
            16,
            stages(rows, rows, rows),
        )(meta, queries, keys, values, d_out)

    def rows_f32(n):
        return jax.ShapeDtypeStruct((heads, n, HDIM), F32)

    def pair(n):
        return jax.ShapeDtypeStruct((heads, 2, n), F32)

    def branch(cap, late):
        there, home = (ahead, back) if late else (back, ahead)
        wide = 2 * HDIM if late else HDIM
        split = up(int(cap * PART), GRAIN)

        def cross(later, meta, ours, *args):
            size = cap if later else split
            scratch = [pltpu.VMEM((size + half, 2 * HDIM), BF16), pltpu.VMEM((size + half, wide), BF16)]
            if late:
                scratch.append(pltpu.VMEM((2, half, HDIM), F32))
            return call(
                functools.partial(cross_kernel, heads, rows, first, half, reach, split, late, later),
                [vmem] * (2 + len(args)) if later else [vmem] * 4 + [any_spec],
                [vmem] * (3 if late else 4),
                [jax.ShapeDtypeStruct((size, wide), BF16), pair(reach)]
                + ([rows_f32(reach)] if late else [rows_f32(rows - first)] * 2),
                cost(heads / 4 * 5 * work, heads / 4 * 6 * tile),
                20,
                scratch,
            )(meta, *ours, *args)

        def steps(meta, queries, keys, values, d_out):
            inputs = (queries, keys, values, d_out)
            sizes, left = [], half - base
            while sum(sizes) < left:
                sizes.append(GRAIN * 2 ** len(sizes))
            one, two = call(
                functools.partial(pack_kernel, heads, rows, base, sizes, late),
                [any_spec] * 2,
                [vmem] * 2,
                [jax.ShapeDtypeStruct((n, 2 * HDIM), BF16) for n in (split, cap - split)],
                cost(0, 2 * cap * HDIM * 4),
                8,
                [
                    pltpu.SemaphoreType.DMA((heads, 2, 1 + len(sizes))),
                    pltpu.VMEM((half, 2 * HDIM), BF16),
                ],
            )(meta, *((keys, values) if late else (queries, d_out)))
            one_got = lax.ppermute(one, "seq", there)
            st_send, st_own = call(
                functools.partial(stats_kernel, heads, rows, reach),
                [vmem] * 4,
                [vmem, vmem],
                [pair(reach), pair(rows)],
                cost(heads / 2 * 2 * work, heads / 2 * 4 * tile),
                16,
            )(meta, *inputs)
            st = st_own
            if not late:
                st = lax.ppermute(st_send, "seq", there)
            two_got = lax.ppermute(two, "seq", there)
            grads = plain(meta, *inputs)
            ours = (queries, d_out) if late else (keys, values)
            begun = cross(False, meta, ours, one_got, st, grads[0])
            returned, tot, *side = cross(True, meta, ours, one_got, two_got, st, *begun)
            if not late:
                tot = lax.ppermute(tot, "seq", home)
            came = lax.ppermute(returned, "seq", home)
            mine = (1, 2) if late else (0,)
            n, at = len(mine), 7 + len(side)
            size = rows - half if late else half
            *grads, = call(
                functools.partial(local_kernel, heads, rows, first, half, reach, late),
                [vmem] * (6 + len(side)) + [any_spec] * 3,
                [any_spec] * 3 + [vmem] * n,
                [whole] * 3 + [rows_f32(size)] * n,
                cost(heads / 2 * 4 * work, heads / 2 * 9 * tile),
                24,
                stages(rows, half, half) if late else stages(rows - half, rows, rows),
                {at + i: i for i in range(3)},
            )(meta, *inputs, st_own, tot, *side, *grads)
            parts = grads[3:]
            added = call(
                functools.partial(add_kernel, heads, rows, half, late),
                [vmem] * (n + 1) + [any_spec] * n,
                [any_spec] * n,
                [whole] * n,
                cost(0, heads / 2 * 3 * tile),
                16,
                [pltpu.VMEM((heads, size, HDIM), BF16)] * n + [pltpu.SemaphoreType.DMA((heads, n))],
                {n + 2 + i: i for i in range(n)},
            )(meta, *parts, came, *[grads[i] for i in mine])
            for i, x in zip(mine, added):
                grads[i] = x
            return tuple(grads[:3])

        return steps

    branches = [lambda *args: tuple(plain(*args))]
    for late in (False, True):
        branches += [branch(cap, late) for cap in caps[late]]
    return lax.switch(meta[heads + 3], branches, meta, queries, keys, values, d_out)


def solution(mesh):
    spec = P(("rep", "seq"), "head")
    return jax.shard_map(
        shards,
        mesh=mesh,
        in_specs=(spec, spec, spec, spec, P("rep"), P()),
        out_specs=(spec, spec, spec),
        check_vma=False,
    )
```

time: 62.2 us -> 59.6 us (0.958)
  Pallas kernels: 30.3 us -> 33.1 us
  loops' own time: 3.29 us -> 0.57 us
  waiting for transfers between devices: 17.6 us -> 14.9 us
    pallas_call x6, Pallas kernels: 19.9 us -> 22.6 us  [the longest x2 10.3 us: cross(): call(functools.partial(cross_kernel, heads, rows, first, half, reach, spl...]
    another operation x1, loops' own time: 3.29 us -> 0.57 us  [shards(): lax.switch(meta[heads + 3], branches, meta, queries, keys, values, d_out)]
    ppermute x5, waiting for transfers between devices: 17.6 us -> 14.9 us  [the longest x1 8.88 us: steps(): tot = lax.ppermute(tot, 'seq', home)]
  transfers between devices with their start and end apart: 5 -> 5, of which waited for: 2 -> 2; matrix products, arithmetic and copies ran while one was open for 0% -> 0% of each run, Pallas kernels for 36% -> 39%
where the time goes in v4:
time: 59.6 us; the launch traced here: 59.4 us
  Pallas kernels  33.1 us (56%)
  waiting for transfers between devices  14.9 us (25%)
  starting transfers between devices  8.16 us (14%)
  between operations  2.14 us (4%)
  local copies, waits for them, and re-layouts  0.6 us (1%)
    pallas_call x2, Pallas kernels, cross(): call(functools.partial(cross_kernel, heads, rows, first, half, reach, spl...  10.3 us
    ppermute x1, waiting for transfers between devices, steps(): tot = lax.ppermute(tot, 'seq', home)  8.88 us
    pallas_call x1, Pallas kernels, steps(): call(functools.partial(local_kernel, heads, rows, first, half, reach, lat...  6.69 us
    ppermute x1, waiting for transfers between devices, steps(): st = lax.ppermute(st_send, 'seq', there)  6 us
    pallas_call x1, Pallas kernels, steps(): call(functools.partial(stats_kernel, heads, rows, reach), [vmem] * 4, [vm...  5.37 us
    ppermute x1, starting transfers between devices, steps(): one_got = lax.ppermute(one, 'seq', there)  5.13 us
    pallas_call x1, Pallas kernels, plain(): call(functools.partial(plain_kernel, heads, rows), [vmem] * 4, [any_spec]...  5.08 us
    pallas_call x1, Pallas kernels, steps(): call(functools.partial(pack_kernel, heads, rows, base, sizes, late), [any...  2.49 us
  transfers between devices with their start and end apart: 5, of which 2 were waited for; matrix products, arithmetic and copies ran while one was open for 0% of the time, Pallas kernels for 39%

profile of v4, /device:TPU:0, one launch (start us, length us, event | category | flops | bytes accessed | tf_op | source)
XLA Modules:
  0.0 59.4 jit_solution(10304352979678627113)
XLA Ops:
  1.3 1.3 %meta.1 = s32[12]{0:T(128)S(1)} custom-call(s32[1]{0:T(128)S(6)} %copy.133.shift_ref, s32[32]{0:T(128)} %order_ref.1), custom_call_target="tpu_custom_call" | custom-call | tf_op jit(solution)/shard_map/meta/pallas_call | solution.py:541
  2.6 0.6 slice.3
  3.9 55.4 %conditional.1 = ((bf16[640,1024]{1,0:T(8,128)(2,1)}, bf16[640,1024]{1,0:T(8,128)(2,1)}, bf16[640,1024]{1,0:T(8,128)(2,1)})) conditional(s32[]{:T(128)} %bitcast, (s32[12]{0:T(128)S(1)}, bf16[640,1024]{1,0:T(8,128)(2,1)}, bf16[640,1024]{1,0:T(8,128)(2,1)}, bf16[640,1024]{1,0:T(8,128)(2,1)}, ...), branch_computations={%region_0.0_spmd, %region_1.0_spmd, %region_2.0_spmd, %region_3.0_... | conditional | flops 6291456000 | bytes 53084424 | solution.py:682
  3.9 0.0 copy-start.1
  3.9 0.0 copy-start.7
  3.9 2.5 %branch_2_fun.8 = (bf16[1056,256]{1,0:T(8,128)(2,1)S(1)}, bf16[672,256]{1,0:T(8,128)(2,1)S(1)}) custom-call(s32[12]{0:T(128)S(1)} %get-tuple-element.99.meta, bf16[640,1024]{1,0:T(8,128)(2,1)} %get-tuple-element.258.q_ref.a_ref, bf16[640,1024]{1,0:T(8,128)(2,1)} %get-tuple-element.279.d_ref.b_ref), custom_call_target="tpu_custom_call" | custom-call | bytes 1769472 | tf_op jit(solution)/shard_map/cond/branch_2_fun/pallas_call | solution.py:617
  6.4 5.1 %collective-permute-start.5 = (bf16[1056,256]{1,0:T(8,128)(2,1)S(1)}, bf16[1056,256]{1,0:T(8,128)(2,1)S(1)}, u32[]{:S(2)}, u32[]{:S(2)}) collective-permute-start(bf16[1056,256]{1,0:T(8,128)(2,1)S(1)} %get-tuple-element.105), channel_id=1, source_target_pairs={{0,12},{4,0},{8,4},{12,8},{1,13},{5,1},{9,5},{13,9},{2,14},{6,2},{... | collective-permute-start | bytes 1622024 | tf_op jit(solution)/shard_map/cond/branch_2_fun/ppermute | solution.py:629
  11.5 0.4 collective-permute-start.6
  12.0 0.0 copy-done.1
  12.0 0.0 copy-done.7
  12.0 0.0 copy-start.13
  12.0 0.0 copy-start.19
  12.0 5.4 %branch_2_fun.7 = (f32[8,2,512]{2,1,0:T(2,128)S(1)}, f32[8,2,640]{2,1,0:T(2,128)S(1)}) custom-call(s32[12]{0:T(128)S(1)} %get-tuple-element.99.meta, bf16[640,1024]{1,0:T(8,128)(2,1)} %get-tuple-element.258.q_ref.a_ref, bf16[640,1024]{1,0:T(8,128)(2,1)S(1)} %copy-done.1, bf16[640,1024]{1,0:T(8,128)(2,1)S(1)} %copy-done.7, ...), custom_call_target="tpu_custom_call" | custom-call | flops 838860800 | bytes 2621440 | tf_op jit(solution)/shard_map/cond/branch_2_fun/pallas_call | solution.py:630
  17.4 0.5 collective-permute-start.7
  17.9 0.0 copy-done.13
  17.9 0.0 copy-done.19
  17.9 5.1 %branch_2_fun.9 = (bf16[640,1024]{1,0:T(8,128)(2,1)}, bf16[640,1024]{1,0:T(8,128)(2,1)}, bf16[640,1024]{1,0:T(8,128)(2,1)}) custom-call(s32[12]{0:T(128)S(1)} %get-tuple-element.99.meta, bf16[640,1024]{1,0:T(8,128)(2,1)S(1)} %copy-done.13, bf16[640,1024]{1,0:T(8,128)(2,1)S(1)} %copy-done.1, bf16[640,1024]{1,0:T(8,128)(2,1)S(1)} %copy-done.7, ...), custom_call_target="tpu_custom_call" | custom-call | flops 1677721600 | bytes 4587520 | tf_op jit(solution)/shard_map/cond/branch_2_fun/pallas_call | solution.py:575
  23.0 6.0 %collective-permute-done.7.refs_3_.refs_4_ = f32[8,2,512]{2,1,0:T(2,128)S(1)} collective-permute-done((f32[8,2,512]{2,1,0:T(2,128)S(1)}, f32[8,2,512]{2,1,0:T(2,128)S(1)}, u32[]{:S(2)}, u32[]{:S(2)}) %collective-permute-start.7) | collective-permute-done | bytes 32800 | tf_op jit(solution)/shard_map/cond/branch_2_fun/ppermute | solution.py:640
  29.0 0.0 collective-permute-done.5.refs_2_
  29.0 5.9 %branch_2_fun.10 = (bf16[1056,128]{1,0:T(8,128)(2,1)S(1)}, f32[8,2,512]{2,1,0:T(2,128)S(1)}, f32[8,480,128]{2,1,0:T(8,128)S(1)}, f32[8,480,128]{2,1,0:T(8,128)S(1)}) custom-call(s32[12]{0:T(128)S(1)} %get-tuple-element.99.meta, bf16[640,1024]{1,0:T(8,128)(2,1)S(1)} %copy-done.1, bf16[640,1024]{1,0:T(8,128)(2,1)S(1)} %copy-done.7, ...), custom_call_target="tpu_custom_call" | custom-call | flops 1048576000 | bytes 1966080 | tf_op jit(solution)/shard_map/cond/branch_2_fun/pallas_call | solution.py:601
  34.9 0.0 collective-permute-done.6.refs_3_
  34.9 4.4 %branch_2_fun.11 = (bf16[1728,128]{1,0:T(8,128)(2,1)S(1)}, f32[8,2,512]{2,1,0:T(2,128)S(1)}, f32[8,480,128]{2,1,0:T(8,128)S(1)}, f32[8,480,128]{2,1,0:T(8,128)S(1)}) custom-call(s32[12]{0:T(128)S(1)} %get-tuple-element.99.meta, bf16[640,1024]{1,0:T(8,128)(2,1)S(1)} %copy-done.1, bf16[640,1024]{1,0:T(8,128)(2,1)S(1)} %copy-done.7, ...), custom_call_target="tpu_custom_call" | custom-call | flops 1048576000 | bytes 1966080 | tf_op jit(solution)/shard_map/cond/branch_2_fun/pallas_call | solution.py:601
  39.3 0.5 collective-permute-start.9
  39.8 1.6 %collective-permute-start.8 = (f32[8,2,512]{2,1,0:T(2,128)S(1)}, f32[8,2,512]{2,1,0:T(2,128)S(1)}, u32[]{:S(2)}, u32[]{:S(2)}) collective-permute-start(f32[8,2,512]{2,1,0:T(2,128)S(1)} %get-tuple-element.113), channel_id=1, source_target_pairs={{0,4},{4,8},{8,12},{12,0},{1,5},{5,9},{9,13},{13,1},{2,6},{6,10},{... | collective-permute-start | bytes 98312 | tf_op jit(solution)/shard_map/cond/branch_2_fun/ppermute | solution.py:647
  41.4 8.9 %collective-permute-done.8.tot_ref = f32[8,2,512]{2,1,0:T(2,128)S(1)} collective-permute-done((f32[8,2,512]{2,1,0:T(2,128)S(1)}, f32[8,2,512]{2,1,0:T(2,128)S(1)}, u32[]{:S(2)}, u32[]{:S(2)}) %collective-permute-start.8) | collective-permute-done | bytes 32800 | tf_op jit(solution)/shard_map/cond/branch_2_fun/ppermute | solution.py:647
  50.3 6.7 %branch_2_fun.12 = (bf16[640,1024]{1,0:T(8,128)(2,1)}, bf16[640,1024]{1,0:T(8,128)(2,1)}, bf16[640,1024]{1,0:T(8,128)(2,1)}, f32[8,320,128]{2,1,0:T(8,128)S(1)}) custom-call(s32[12]{0:T(128)S(1)} %get-tuple-element.99.meta, bf16[640,1024]{1,0:T(8,128)(2,1)S(1)} %copy-done.13, ...), custom_call_target="tpu_custom_call", output_to_operand_aliasing={{0}: (9, {}), {1}: (10, {}), {2}: (11, {})} | custom-call | flops 1677721600 | bytes 5898240 | tf_op jit(solution)/shard_map/cond/branch_2_fun/pallas_call | solution.py:652
  57.0 0.0 collective-permute-done.9.refs_1_
  57.0 1.8 %branch_2_fun.13 = bf16[640,1024]{1,0:T(8,128)(2,1)} custom-call(s32[12]{0:T(128)S(1)} %get-tuple-element.99.meta, f32[8,320,128]{2,1,0:T(8,128)S(1)} %get-tuple-element.118.refs_0_, bf16[1728,128]{1,0:T(8,128)(2,1)S(1)} %collective-permute-done.9.refs_1_, bf16[640,1024]{1,0:T(8,128)(2,1)} %get-tuple-element.120.refs_2_), custom_call_target="tpu_custom_call", output_to_operand_aliasing={{}: (3, {})} | custom-call | bytes 1966080 | tf_op jit(solution)/shard_map/cond/branch_2_fun/pallas_call | solution.py:663
Async XLA Ops:
  3.9 8.1 %copy-start.1 = (bf16[640,1024]{1,0:T(8,128)(2,1)S(1)}, bf16[640,1024]{1,0:T(8,128)(2,1)}, u32[]{:S(2)}) copy-start(bf16[640,1024]{1,0:T(8,128)(2,1)} %get-tuple-element.265.k_ref.refs_0_) | copy-start | bytes 3932164 | tf_op jit(solution)/shard_map/cond
  3.9 8.1 %copy-start.7 = (bf16[640,1024]{1,0:T(8,128)(2,1)S(1)}, bf16[640,1024]{1,0:T(8,128)(2,1)}, u32[]{:S(2)}) copy-start(bf16[640,1024]{1,0:T(8,128)(2,1)} %get-tuple-element.272.v_ref.refs_1_) | copy-start | bytes 3932164 | tf_op jit(solution)/shard_map/cond
  6.4 22.6 %collective-permute-start.5 = (bf16[1056,256]{1,0:T(8,128)(2,1)S(1)}, bf16[1056,256]{1,0:T(8,128)(2,1)S(1)}, u32[]{:S(2)}, u32[]{:S(2)}) collective-permute-start(bf16[1056,256]{1,0:T(8,128)(2,1)S(1)} %get-tuple-element.105), channel_id=1, source_target_pairs={{0,12},{4,0},{8,4},{12,8},{1,13},{5,1},{9,5},{13,9},{2,14},{6,2},{... | collective-permute-start | bytes 1622024 | tf_op jit(solution)/shard_map/cond/branch_2_fun/ppermute | solution.py:629
  11.5 23.3 %collective-permute-start.6 = (bf16[672,256]{1,0:T(8,128)(2,1)S(1)}, bf16[672,256]{1,0:T(8,128)(2,1)S(1)}, u32[]{:S(2)}, u32[]{:S(2)}) collective-permute-start(bf16[672,256]{1,0:T(8,128)(2,1)S(1)} %get-tuple-element.106), channel_id=1, source_target_pairs={{0,12},{4,0},{8,4},{12,8},{1,13},{5,1},{9,5},{13,9},{2,14},{6,2},{... | collective-permute-start | bytes 1032200 | tf_op jit(solution)/shard_map/cond/branch_2_fun/ppermute | solution.py:641
  12.0 5.9 %copy-start.13 = (bf16[640,1024]{1,0:T(8,128)(2,1)S(1)}, bf16[640,1024]{1,0:T(8,128)(2,1)}, u32[]{:S(2)}) copy-start(bf16[640,1024]{1,0:T(8,128)(2,1)} %get-tuple-element.258.q_ref.a_ref) | copy-start | bytes 3932164 | tf_op jit(solution)/shard_map/cond
  12.0 5.9 %copy-start.19 = (bf16[640,1024]{1,0:T(8,128)(2,1)S(1)}, bf16[640,1024]{1,0:T(8,128)(2,1)}, u32[]{:S(2)}) copy-start(bf16[640,1024]{1,0:T(8,128)(2,1)} %get-tuple-element.279.d_ref.b_ref) | copy-start | bytes 3932164 | tf_op jit(solution)/shard_map/cond
  17.4 11.6 %collective-permute-start.7 = (f32[8,2,512]{2,1,0:T(2,128)S(1)}, f32[8,2,512]{2,1,0:T(2,128)S(1)}, u32[]{:S(2)}, u32[]{:S(2)}) collective-permute-start(f32[8,2,512]{2,1,0:T(2,128)S(1)} %get-tuple-element.107), channel_id=1, source_target_pairs={{0,12},{4,0},{8,4},{12,8},{1,13},{5,1},{9,5},{13,9},{2,14},{6,2},{... | collective-permute-start | bytes 98312 | tf_op jit(solution)/shard_map/cond/branch_2_fun/ppermute | solution.py:640
  39.3 17.7 %collective-permute-start.9 = (bf16[1728,128]{1,0:T(8,128)(2,1)S(1)}, bf16[1728,128]{1,0:T(8,128)(2,1)S(1)}, u32[]{:S(2)}, u32[]{:S(2)}) collective-permute-start(bf16[1728,128]{1,0:T(8,128)(2,1)S(1)} %get-tuple-element.119), channel_id=1, source_target_pairs={{0,4},{4,8},{8,12},{12,0},{1,5},{5,9},{9,13},{13,1},{2,6},{6,10},{... | collective-permute-start | bytes 1327112 | tf_op jit(solution)/shard_map/cond/branch_2_fun/ppermute | solution.py:648
  39.8 10.5 %collective-permute-start.8 = (f32[8,2,512]{2,1,0:T(2,128)S(1)}, f32[8,2,512]{2,1,0:T(2,128)S(1)}, u32[]{:S(2)}, u32[]{:S(2)}) collective-permute-start(f32[8,2,512]{2,1,0:T(2,128)S(1)} %get-tuple-element.113), channel_id=1, source_target_pairs={{0,4},{4,8},{8,12},{12,0},{1,5},{5,9},{9,13},{13,1},{2,6},{6,10},{... | collective-permute-start | bytes 98312 | tf_op jit(solution)/shard_map/cond/branch_2_fun/ppermute | solution.py:647

commit v5 on v4

--- a/solution.py
+++ b/solution.py
@@ -96,7 +96,7 @@
             finish(stop - back)
 
 
-def meta_kernel(heads, rows, caps, shift_ref, order_ref, out_ref, flag_ref):
+def meta_kernel(heads, rows, caps, shift_ref, order_ref, out_ref, pick_ref, flag_ref):
     base = lax.axis_index("head") * heads
     for h in range(heads):
         flag_ref[h] = 0
@@ -129,7 +129,7 @@
     out_ref[heads] = count
     out_ref[heads + 1] = off
     out_ref[heads + 2] = slot
-    out_ref[heads + 3] = pick
+    pick_ref[0] = pick
 
 
 def pack_kernel(heads, rows, base, sizes, late, meta, a_ref, b_ref, one_ref, two_ref, sem, mid_ref):
@@ -199,10 +199,9 @@
         lax.fori_loop(0, (slot - cut) // GRAIN, rest, 0)
 
 
-def stats_kernel(heads, rows, reach, meta, q_ref, k_ref, v_ref, d_ref, send_ref, own_ref):
-    off = meta[heads + 1]
-
+def stats_kernel(heads, rows, reach, late, meta, q_ref, k_ref, v_ref, d_ref, send_ref, own_ref):
     def step(s, c):
+        off = jnp.where(s < meta[heads], meta[heads + 1], 0)
         col = column(meta, s)
 
         def front(q0, w):
@@ -229,7 +228,7 @@
         staggered(query_blocks(rows), front, back)
         return c
 
-    lax.fori_loop(0, meta[heads], step, 0)
+    lax.fori_loop(0, heads if late else meta[heads], step, 0)
 
 
 def plain_kernel(
@@ -286,7 +285,7 @@
     two_ref = refs.pop(0) if later else None
     st_ref = refs.pop(0)
     passed = refs[: 3 if late else 4] if later else ()
-    del refs[: len(passed) if later else 1]
+    del refs[: len(passed) if later else 0 if late else 1]
     if late:
         back_ref, tot_ref, xq_ref, buf_ref, acc_ref, sum_ref = refs
         kept = ((tot_ref, 1), (xq_ref, 2))
@@ -294,6 +293,7 @@
         back_ref, tot_ref, gk_ref, gv_ref, buf_ref, acc_ref = refs
         kept = ((tot_ref, 1), (gk_ref, 2), (gv_ref, 3))
     count, off, slot = meta[heads], meta[heads + 1], meta[heads + 2]
+    wide = up(half, 128)
     done = jnp.minimum(count, split // slot)
     low, high = (done, count) if later else (0, done)
 
@@ -366,23 +366,23 @@
 
     def queries_came(s, c):
         col = column(meta, s)
-        gk_ref[s] = jnp.zeros(gk_ref.shape[1:], F32)
-        gv_ref[s] = jnp.zeros(gv_ref.shape[1:], F32)
-
-        def block(j, c):
-            q0 = pl.multiple_of(j * BLOCK, BLOCK)
-            mine = pl.ds(pl.multiple_of(s * slot + q0, GRAIN), BLOCK)
-            qb, db = buf_ref[mine, :HDIM], buf_ref[mine, HDIM:]
-            kb = a_ref[first:, col]
-            valid = first + lax.broadcasted_iota(jnp.int32, (rows - first, BLOCK), 0) >= off
-            inside = q0 + lax.broadcasted_iota(jnp.int32, (1, BLOCK), 1) < off
-            p, ds = scores(s, pl.ds(q0, BLOCK), inside, valid, kb, b_ref[first:, col], qb, db)
-            gv_ref[s] += dot_nn(p, db)
-            gk_ref[s] += dot_nn(ds, qb)
-            acc_ref[mine, :] = (dot_tn(ds, kb) * SCALE).astype(BF16)
-            return c
-
-        lax.fori_loop(0, (off + BLOCK - 1) // BLOCK, block, 0)
+        for lanes, k0, fits in ((BLOCK, first, off <= BLOCK), (wide, BLOCK, off > BLOCK)):
+
+            @pl.when(fits)
+            def _(lanes=lanes, k0=k0):
+                mine = pl.ds(pl.multiple_of(s * slot, GRAIN), lanes)
+                qb, db = buf_ref[mine, :HDIM], buf_ref[mine, HDIM:]
+                kb = a_ref[k0:, col]
+                valid = k0 + lax.broadcasted_iota(jnp.int32, (rows - k0, lanes), 0) >= off
+                inside = lax.broadcasted_iota(jnp.int32, (1, lanes), 1) < off
+                p, ds = scores(s, slice(0, lanes), inside, valid, kb, b_ref[k0:, col], qb, db)
+                gv_ref[s, k0 - first :, :] = dot_nn(p, db)
+                gk_ref[s, k0 - first :, :] = dot_nn(ds, qb)
+                if k0 > first:
+                    gv_ref[s, : k0 - first, :] = jnp.zeros((k0 - first, HDIM), F32)
+                    gk_ref[s, : k0 - first, :] = jnp.zeros((k0 - first, HDIM), F32)
+                acc_ref[mine, :] = (dot_tn(ds, kb) * SCALE).astype(BF16)
+
         return c
 
     if later:
@@ -405,14 +405,13 @@
         xq_ref = refs.pop(0)
     else:
         gk_ref, gv_ref = refs[:2]
-        del refs[:2]
-    del refs[:3]
+        del refs[:5]
     dq_ref, dk_ref, dv_ref = refs[:3]
     parts = refs[3 : 5 if late else 4]
     oq_ref, ok_ref, ov_ref, ak_ref, av_ref, sem = refs[5 if late else 4 :]
-    off = meta[heads + 1]
-    keys_out, query_out = (pl.ds(0, half), pl.ds(0, rows)) if late else (pl.ds(0, rows), pl.ds(half, rows - half))
+    count = meta[heads]
     skip = 0 if late else half
+    keys_out, query_out = pl.ds(0, rows), pl.ds(skip, rows - skip)
 
     def copies(s):
         col = column(meta, s)
@@ -424,6 +423,7 @@
         ]
 
     def compute(s):
+        off = jnp.where(s < count, meta[heads + 1], 0)
         col = column(meta, s)
 
         def front(q0, w):
@@ -445,7 +445,7 @@
             gk = dot_nn(ds, q_ref[q0:kn, col])
             dq = dot_tn(ds, k_ref[:kn, col])
             if late and q0 < reach:
-                dq = dq + xq_ref[s, q0:kn, :]
+                dq = dq + jnp.where(s < count, xq_ref[s, q0:kn, :], 0.0)
             dq = dq * SCALE
             if not late and q0 < half:
                 parts[0][s, q0 : min(kn, half), :] = dq[: half - q0]
@@ -460,8 +460,8 @@
 
         staggered(query_blocks(rows), front, back)
         if late:
-            ok_ref[s % 2] = (ak_ref[:half, :] * SCALE).astype(BF16)
-            ov_ref[s % 2] = av_ref[:half, :].astype(BF16)
+            ok_ref[s % 2] = (ak_ref[...] * SCALE).astype(BF16)
+            ov_ref[s % 2] = av_ref[...].astype(BF16)
             parts[0][s] = ak_ref[half:, :] * SCALE
             parts[1][s] = av_ref[half:, :]
         else:
@@ -470,7 +470,7 @@
             ok_ref[s % 2, first:, :] = ((ak_ref[first:, :] + gk_ref[s]) * SCALE).astype(BF16)
             ov_ref[s % 2, first:, :] = (av_ref[first:, :] + gv_ref[s]).astype(BF16)
 
-    written_out(0, meta[heads], copies, compute)
+    written_out(0, heads if late else count, copies, compute)
 
 
 def add_kernel(heads, rows, half, late, meta, *refs):
@@ -538,11 +538,11 @@
     back = [(i, (i - 1) % seq) for i in range(seq)]
     ahead = [(i, (i + 1) % seq) for i in range(seq)]
 
-    meta = pl.pallas_call(
+    meta, pick = pl.pallas_call(
         functools.partial(meta_kernel, heads, rows, caps),
-        out_shape=jax.ShapeDtypeStruct((heads + 4,), jnp.int32),
+        out_shape=[jax.ShapeDtypeStruct((heads + 3,), jnp.int32), jax.ShapeDtypeStruct((1,), jnp.int32)],
         in_specs=[pl.BlockSpec(memory_space=pltpu.SMEM)] * 2,
-        out_specs=pl.BlockSpec(memory_space=pltpu.SMEM),
+        out_specs=[pl.BlockSpec(memory_space=pltpu.SMEM)] * 2,
         scratch_shapes=[pltpu.SMEM((heads,), jnp.int32)],
         name="meta",
     )(shift, head_order)
@@ -600,7 +600,7 @@
                 scratch.append(pltpu.VMEM((2, half, HDIM), F32))
             return call(
                 functools.partial(cross_kernel, heads, rows, first, half, reach, split, late, later),
-                [vmem] * (2 + len(args)) if later else [vmem] * 4 + [any_spec],
+                [vmem] * 4 + [any_spec] * (not late) if not later else [vmem] * (2 + len(args)),
                 [vmem] * (3 if late else 4),
                 [jax.ShapeDtypeStruct((size, wide), BF16), pair(reach)]
                 + ([rows_f32(reach)] if late else [rows_f32(rows - first)] * 2),
@@ -628,7 +628,7 @@
             )(meta, *((keys, values) if late else (queries, d_out)))
             one_got = lax.ppermute(one, "seq", there)
             st_send, st_own = call(
-                functools.partial(stats_kernel, heads, rows, reach),
+                functools.partial(stats_kernel, heads, rows, reach, late),
                 [vmem] * 4,
                 [vmem, vmem],
                 [pair(reach), pair(rows)],
@@ -639,9 +639,9 @@
             if not late:
                 st = lax.ppermute(st_send, "seq", there)
             two_got = lax.ppermute(two, "seq", there)
-            grads = plain(meta, *inputs)
+            grads = () if late else plain(meta, *inputs)
             ours = (queries, d_out) if late else (keys, values)
-            begun = cross(False, meta, ours, one_got, st, grads[0])
+            begun = cross(False, meta, ours, one_got, st, *grads[:1])
             returned, tot, *side = cross(True, meta, ours, one_got, two_got, st, *begun)
             if not late:
                 tot = lax.ppermute(tot, "seq", home)
@@ -651,13 +651,13 @@
             size = rows - half if late else half
             *grads, = call(
                 functools.partial(local_kernel, heads, rows, first, half, reach, late),
-                [vmem] * (6 + len(side)) + [any_spec] * 3,
+                [vmem] * (6 + len(side)) + [any_spec] * len(grads),
                 [any_spec] * 3 + [vmem] * n,
                 [whole] * 3 + [rows_f32(size)] * n,
                 cost(heads / 2 * 4 * work, heads / 2 * 9 * tile),
                 24,
-                stages(rows, half, half) if late else stages(rows - half, rows, rows),
-                {at + i: i for i in range(3)},
+                stages(rows if late else rows - half, rows, rows),
+                {at + i: i for i in range(len(grads))},
             )(meta, *inputs, st_own, tot, *side, *grads)
             parts = grads[3:]
             added = call(
@@ -679,7 +679,7 @@
     branches = [lambda *args: tuple(plain(*args))]
     for late in (False, True):
         branches += [branch(cap, late) for cap in caps[late]]
-    return lax.switch(meta[heads + 3], branches, meta, queries, keys, values, d_out)
+    return lax.switch(pick.reshape(()), branches, meta, queries, keys, values, d_out)
 
 
 def solution(mesh):

time: 59.6 us -> 55 us (0.923)
  Pallas kernels: 33.1 us -> 28.9 us
    pallas_call x2, Pallas kernels: 10.3 us -> 6.25 us  [cross(): call(functools.partial(cross_kernel, heads, rows, first, half, reach, spl...]
  transfers between devices with their start and end apart: 5 -> 5, of which waited for: 2 -> 2; matrix products, arithmetic and copies ran while one was open for 0% -> 0% of each run, Pallas kernels for 39% -> 38%
where the time goes in v5:
time: 55 us; the launch traced here: 54.8 us
  Pallas kernels  28.9 us (53%)
  waiting for transfers between devices  14.9 us (27%)
  starting transfers between devices  8.16 us (15%)
  between operations  2.15 us (4%)
  loops' own time  0.65 us (1%)
    ppermute x1, waiting for transfers between devices, steps(): tot = lax.ppermute(tot, 'seq', home)  8.88 us
    pallas_call x1, Pallas kernels, steps(): call(functools.partial(local_kernel, heads, rows, first, half, reach, lat...  6.62 us
    pallas_call x2, Pallas kernels, cross(): call(functools.partial(cross_kernel, heads, rows, first, half, reach, spl...  6.25 us
    ppermute x1, waiting for transfers between devices, steps(): st = lax.ppermute(st_send, 'seq', there)  5.99 us
    pallas_call x1, Pallas kernels, steps(): call(functools.partial(stats_kernel, heads, rows, reach, late), [vmem] *...  5.37 us
    ppermute x1, starting transfers between devices, steps(): one_got = lax.ppermute(one, 'seq', there)  5.13 us
    pallas_call x1, Pallas kernels, plain(): call(functools.partial(plain_kernel, heads, rows), [vmem] * 4, [any_spec]...  5.08 us
    pallas_call x1, Pallas kernels, steps(): call(functools.partial(pack_kernel, heads, rows, base, sizes, late), [any...  2.49 us
  transfers between devices with their start and end apart: 5, of which 2 were waited for; matrix products, arithmetic and copies ran while one was open for 0% of the time, Pallas kernels for 38%

profile of v5, /device:TPU:0, one launch (start us, length us, event | category | flops | bytes accessed | tf_op | source)
XLA Modules:
  0.0 54.8 jit_solution(16151206682323260987)
XLA Ops:
  1.3 1.3 %meta.1 = (s32[11]{0:T(128)S(1)}, s32[1]{0:T(128)}) custom-call(s32[1]{0:T(128)S(6)} %copy.87.shift_ref, s32[32]{0:T(128)} %order_ref.1), custom_call_target="tpu_custom_call" | custom-call | tf_op jit(solution)/shard_map/meta/pallas_call | solution.py:541
  3.3 51.3 %conditional.1 = ((bf16[640,1024]{1,0:T(8,128)(2,1)}, bf16[640,1024]{1,0:T(8,128)(2,1)}, bf16[640,1024]{1,0:T(8,128)(2,1)})) conditional(s32[]{:T(128)} %bitcast, (s32[11]{0:T(128)S(1)}, bf16[640,1024]{1,0:T(8,128)(2,1)}, bf16[640,1024]{1,0:T(8,128)(2,1)}, bf16[640,1024]{1,0:T(8,128)(2,1)}, ...), branch_computations={%region_0.0_spmd, %region_1.0_spmd, %region_2.0_spmd, %region_3.0_... | conditional | flops 6291456000 | bytes 50725208 | solution.py:682
  3.3 0.0 copy-start.1
  3.3 0.0 copy-start.7
  3.3 2.5 %branch_2_fun.8 = (bf16[1056,256]{1,0:T(8,128)(2,1)S(1)}, bf16[672,256]{1,0:T(8,128)(2,1)S(1)}) custom-call(s32[11]{0:T(128)S(1)} %get-tuple-element.99.meta, bf16[640,1024]{1,0:T(8,128)(2,1)} %get-tuple-element.100.q_ref.a_ref, bf16[640,1024]{1,0:T(8,128)(2,1)} %get-tuple-element.103.d_ref.b_ref), custom_call_target="tpu_custom_call" | custom-call | bytes 1769472 | tf_op jit(solution)/shard_map/cond/branch_2_fun/pallas_call | solution.py:617
  5.8 5.1 %collective-permute-start.5 = (bf16[1056,256]{1,0:T(8,128)(2,1)S(1)}, bf16[1056,256]{1,0:T(8,128)(2,1)S(1)}, u32[]{:S(2)}, u32[]{:S(2)}) collective-permute-start(bf16[1056,256]{1,0:T(8,128)(2,1)S(1)} %get-tuple-element.105), channel_id=1, source_target_pairs={{0,12},{4,0},{8,4},{12,8},{1,13},{5,1},{9,5},{13,9},{2,14},{6,2},{... | collective-permute-start | bytes 1622024 | tf_op jit(solution)/shard_map/cond/branch_2_fun/ppermute | solution.py:629
  10.9 0.4 collective-permute-start.6
  11.4 0.0 copy-done.1
  11.4 0.0 copy-done.7
  11.4 0.0 copy-start.13
  11.4 0.0 copy-start.19
  11.4 5.4 %branch_2_fun.7 = (f32[8,2,512]{2,1,0:T(2,128)S(1)}, f32[8,2,640]{2,1,0:T(2,128)S(1)}) custom-call(s32[11]{0:T(128)S(1)} %get-tuple-element.99.meta, bf16[640,1024]{1,0:T(8,128)(2,1)} %get-tuple-element.100.q_ref.a_ref, bf16[640,1024]{1,0:T(8,128)(2,1)S(1)} %copy-done.1, bf16[640,1024]{1,0:T(8,128)(2,1)S(1)} %copy-done.7, ...), custom_call_target="tpu_custom_call" | custom-call | flops 838860800 | bytes 2621440 | tf_op jit(solution)/shard_map/cond/branch_2_fun/pallas_call | solution.py:630
  16.8 0.5 collective-permute-start.7
  17.3 0.0 copy-done.13
  17.3 0.0 copy-done.19
  17.3 5.1 %branch_2_fun.9 = (bf16[640,1024]{1,0:T(8,128)(2,1)}, bf16[640,1024]{1,0:T(8,128)(2,1)}, bf16[640,1024]{1,0:T(8,128)(2,1)}) custom-call(s32[11]{0:T(128)S(1)} %get-tuple-element.99.meta, bf16[640,1024]{1,0:T(8,128)(2,1)S(1)} %copy-done.13, bf16[640,1024]{1,0:T(8,128)(2,1)S(1)} %copy-done.1, bf16[640,1024]{1,0:T(8,128)(2,1)S(1)} %copy-done.7, ...), custom_call_target="tpu_custom_call" | custom-call | flops 1677721600 | bytes 4587520 | tf_op jit(solution)/shard_map/cond/branch_2_fun/pallas_call | solution.py:575
  22.4 6.0 %collective-permute-done.7.refs_3_.refs_4_ = f32[8,2,512]{2,1,0:T(2,128)S(1)} collective-permute-done((f32[8,2,512]{2,1,0:T(2,128)S(1)}, f32[8,2,512]{2,1,0:T(2,128)S(1)}, u32[]{:S(2)}, u32[]{:S(2)}) %collective-permute-start.7) | collective-permute-done | bytes 32800 | tf_op jit(solution)/shard_map/cond/branch_2_fun/ppermute | solution.py:640
  28.4 0.0 collective-permute-done.5.refs_2_
  28.4 3.5 %branch_2_fun.10 = (bf16[1056,128]{1,0:T(8,128)(2,1)S(1)}, f32[8,2,512]{2,1,0:T(2,128)S(1)}, f32[8,480,128]{2,1,0:T(8,128)S(1)}, f32[8,480,128]{2,1,0:T(8,128)S(1)}) custom-call(s32[11]{0:T(128)S(1)} %get-tuple-element.99.meta, bf16[640,1024]{1,0:T(8,128)(2,1)S(1)} %copy-done.1, bf16[640,1024]{1,0:T(8,128)(2,1)S(1)} %copy-done.7, ...), custom_call_target="tpu_custom_call" | custom-call | flops 1048576000 | bytes 1966080 | tf_op jit(solution)/shard_map/cond/branch_2_fun/pallas_call | solution.py:601
  31.9 0.0 collective-permute-done.6.refs_3_
  31.9 2.7 %branch_2_fun.11 = (bf16[1728,128]{1,0:T(8,128)(2,1)S(1)}, f32[8,2,512]{2,1,0:T(2,128)S(1)}, f32[8,480,128]{2,1,0:T(8,128)S(1)}, f32[8,480,128]{2,1,0:T(8,128)S(1)}) custom-call(s32[11]{0:T(128)S(1)} %get-tuple-element.99.meta, bf16[640,1024]{1,0:T(8,128)(2,1)S(1)} %copy-done.1, bf16[640,1024]{1,0:T(8,128)(2,1)S(1)} %copy-done.7, ...), custom_call_target="tpu_custom_call" | custom-call | flops 1048576000 | bytes 1966080 | tf_op jit(solution)/shard_map/cond/branch_2_fun/pallas_call | solution.py:601
  34.7 0.5 collective-permute-start.9
  35.2 1.6 %collective-permute-start.8 = (f32[8,2,512]{2,1,0:T(2,128)S(1)}, f32[8,2,512]{2,1,0:T(2,128)S(1)}, u32[]{:S(2)}, u32[]{:S(2)}) collective-permute-start(f32[8,2,512]{2,1,0:T(2,128)S(1)} %get-tuple-element.113), channel_id=1, source_target_pairs={{0,4},{4,8},{8,12},{12,0},{1,5},{5,9},{9,13},{13,1},{2,6},{6,10},{... | collective-permute-start | bytes 98312 | tf_op jit(solution)/shard_map/cond/branch_2_fun/ppermute | solution.py:647
  36.7 8.9 %collective-permute-done.8.tot_ref = f32[8,2,512]{2,1,0:T(2,128)S(1)} collective-permute-done((f32[8,2,512]{2,1,0:T(2,128)S(1)}, f32[8,2,512]{2,1,0:T(2,128)S(1)}, u32[]{:S(2)}, u32[]{:S(2)}) %collective-permute-start.8) | collective-permute-done | bytes 32800 | tf_op jit(solution)/shard_map/cond/branch_2_fun/ppermute | solution.py:647
  45.6 6.6 %branch_2_fun.12 = (bf16[640,1024]{1,0:T(8,128)(2,1)}, bf16[640,1024]{1,0:T(8,128)(2,1)}, bf16[640,1024]{1,0:T(8,128)(2,1)}, f32[8,320,128]{2,1,0:T(8,128)S(1)}) custom-call(s32[11]{0:T(128)S(1)} %get-tuple-element.99.meta, bf16[640,1024]{1,0:T(8,128)(2,1)S(1)} %copy-done.13, ...), custom_call_target="tpu_custom_call", output_to_operand_aliasing={{0}: (9, {}), {1}: (10, {}), {2}: (11, {})} | custom-call | flops 1677721600 | bytes 5898240 | tf_op jit(solution)/shard_map/cond/branch_2_fun/pallas_call | solution.py:652
  52.2 0.0 collective-permute-done.9.refs_1_
  52.3 1.8 %branch_2_fun.13 = bf16[640,1024]{1,0:T(8,128)(2,1)} custom-call(s32[11]{0:T(128)S(1)} %get-tuple-element.99.meta, f32[8,320,128]{2,1,0:T(8,128)S(1)} %get-tuple-element.118.refs_0_, bf16[1728,128]{1,0:T(8,128)(2,1)S(1)} %collective-permute-done.9.refs_1_, bf16[640,1024]{1,0:T(8,128)(2,1)} %get-tuple-element.120.refs_2_), custom_call_target="tpu_custom_call", output_to_operand_aliasing={{}: (3, {})} | custom-call | bytes 1966080 | tf_op jit(solution)/shard_map/cond/branch_2_fun/pallas_call | solution.py:663
Async XLA Ops:
  3.3 8.1 %copy-start.1 = (bf16[640,1024]{1,0:T(8,128)(2,1)S(1)}, bf16[640,1024]{1,0:T(8,128)(2,1)}, u32[]{:S(2)}) copy-start(bf16[640,1024]{1,0:T(8,128)(2,1)} %get-tuple-element.101.k_ref.refs_0_) | copy-start | bytes 3932164 | tf_op jit(solution)/shard_map/cond
  3.3 8.1 %copy-start.7 = (bf16[640,1024]{1,0:T(8,128)(2,1)S(1)}, bf16[640,1024]{1,0:T(8,128)(2,1)}, u32[]{:S(2)}) copy-start(bf16[640,1024]{1,0:T(8,128)(2,1)} %get-tuple-element.102.v_ref.refs_1_) | copy-start | bytes 3932164 | tf_op jit(solution)/shard_map/cond
  5.8 22.6 %collective-permute-start.5 = (bf16[1056,256]{1,0:T(8,128)(2,1)S(1)}, bf16[1056,256]{1,0:T(8,128)(2,1)S(1)}, u32[]{:S(2)}, u32[]{:S(2)}) collective-permute-start(bf16[1056,256]{1,0:T(8,128)(2,1)S(1)} %get-tuple-element.105), channel_id=1, source_target_pairs={{0,12},{4,0},{8,4},{12,8},{1,13},{5,1},{9,5},{13,9},{2,14},{6,2},{... | collective-permute-start | bytes 1622024 | tf_op jit(solution)/shard_map/cond/branch_2_fun/ppermute | solution.py:629
  10.9 21.0 %collective-permute-start.6 = (bf16[672,256]{1,0:T(8,128)(2,1)S(1)}, bf16[672,256]{1,0:T(8,128)(2,1)S(1)}, u32[]{:S(2)}, u32[]{:S(2)}) collective-permute-start(bf16[672,256]{1,0:T(8,128)(2,1)S(1)} %get-tuple-element.106), channel_id=1, source_target_pairs={{0,12},{4,0},{8,4},{12,8},{1,13},{5,1},{9,5},{13,9},{2,14},{6,2},{... | collective-permute-start | bytes 1032200 | tf_op jit(solution)/shard_map/cond/branch_2_fun/ppermute | solution.py:641
  11.4 5.9 %copy-start.13 = (bf16[640,1024]{1,0:T(8,128)(2,1)S(1)}, bf16[640,1024]{1,0:T(8,128)(2,1)}, u32[]{:S(2)}) copy-start(bf16[640,1024]{1,0:T(8,128)(2,1)} %get-tuple-element.100.q_ref.a_ref) | copy-start | bytes 3932164 | tf_op jit(solution)/shard_map/cond
  11.4 5.9 %copy-start.19 = (bf16[640,1024]{1,0:T(8,128)(2,1)S(1)}, bf16[640,1024]{1,0:T(8,128)(2,1)}, u32[]{:S(2)}) copy-start(bf16[640,1024]{1,0:T(8,128)(2,1)} %get-tuple-element.103.d_ref.b_ref) | copy-start | bytes 3932164 | tf_op jit(solution)/shard_map/cond
  16.8 11.6 %collective-permute-start.7 = (f32[8,2,512]{2,1,0:T(2,128)S(1)}, f32[8,2,512]{2,1,0:T(2,128)S(1)}, u32[]{:S(2)}, u32[]{:S(2)}) collective-permute-start(f32[8,2,512]{2,1,0:T(2,128)S(1)} %get-tuple-element.107), channel_id=1, source_target_pairs={{0,12},{4,0},{8,4},{12,8},{1,13},{5,1},{9,5},{13,9},{2,14},{6,2},{... | collective-permute-start | bytes 98312 | tf_op jit(solution)/shard_map/cond/branch_2_fun/ppermute | solution.py:640
  34.7 17.6 %collective-permute-start.9 = (bf16[1728,128]{1,0:T(8,128)(2,1)S(1)}, bf16[1728,128]{1,0:T(8,128)(2,1)S(1)}, u32[]{:S(2)}, u32[]{:S(2)}) collective-permute-start(bf16[1728,128]{1,0:T(8,128)(2,1)S(1)} %get-tuple-element.119), channel_id=1, source_target_pairs={{0,4},{4,8},{8,12},{12,0},{1,5},{5,9},{9,13},{13,1},{2,6},{6,10},{... | collective-permute-start | bytes 1327112 | tf_op jit(solution)/shard_map/cond/branch_2_fun/ppermute | solution.py:648
  35.2 10.5 %collective-permute-start.8 = (f32[8,2,512]{2,1,0:T(2,128)S(1)}, f32[8,2,512]{2,1,0:T(2,128)S(1)}, u32[]{:S(2)}, u32[]{:S(2)}) collective-permute-start(f32[8,2,512]{2,1,0:T(2,128)S(1)} %get-tuple-element.113), channel_id=1, source_target_pairs={{0,4},{4,8},{8,12},{12,0},{1,5},{5,9},{9,13},{13,1},{2,6},{6,10},{... | collective-permute-start | bytes 98312 | tf_op jit(solution)/shard_map/cond/branch_2_fun/ppermute | solution.py:647
